TPU v7x, 768 devices: a whole 4x8x12 slice. The times are simulated.
768 devices in a mesh: row: 96 (over y_lo, z, core), col: 8 (over x, y_hi).
Axes of the slice: x: 4, y: 8 (y_hi: 2, y_lo: 4; y = y_hi * 4 + y_lo), z: 12, core: 2. Of those that a mesh axis runs over, the one named last changes fastest.
Arguments:
- static_design: bfloat16 [1536, 24576], P('col', 'row'), may hold values from -6 to 6
- tv_design: bfloat16 [1536, 24576], P('row', 'col'), may hold values from -0.15625 to 0.15625
- taps: float32 [32], replicated, may hold values from -1 to 1
- arc_id: int32 [1536], replicated, may hold values from 0 to 3, never falling along the last dimension, each value on 1 to 768 neighbouring positions
Outputs:
- normal_block: float32 [24576, 24576], P('row', 'col')
Inputs may be any that keep to these rules, and one draw needn't show every extreme that they name: `arc_id`: arc numbers never fall along the rows; each arc has 1 to 768 rows and one has exactly 768.
All inputs are finite; a program needn't handle non-finite values.
Results may differ from a plain program's by a relative error of at most 0.0029.
Values may be sent and summed in bfloat16 or wider, within the bound.
No kernel may reach another device: no remote copies, remote signals or barrier semaphores. Data moves between devices by JAX's collectives and lax.ppermute only.
A program may use at most 64 MiB of HBM per device.

v0:
```python
import jax
import jax.numpy as jnp
from jax import lax
from jax.sharding import Mesh
from jax.sharding import PartitionSpec as P

COL = ("col_0", "col_1")


def padded(cells, sides, width):
    for axis, dim in sides:
        count = lax.axis_size(axis)
        ends = count - 1
        head = lax.slice_in_dim(cells, 0, width, axis=dim)
        tail = lax.slice_in_dim(cells, cells.shape[dim] - width, cells.shape[dim], axis=dim)
        cells = jnp.concatenate(
            [
                lax.ppermute(tail, axis, [(i, (i + 1) % count) for i in range(ends)]),
                cells,
                lax.ppermute(head, axis, [((i + 1) % count, i) for i in range(ends)]),
            ],
            axis=dim,
        )
    return cells


def gathered_by_axis(shard, axes, dim):
    for axis in reversed(axes):
        shard = lax.all_gather(shard, axis, axis=dim, tiled=True)
    return shard


def shift_down(values, steps, fill):
    pads = [(steps, 0)] + [(0, 0)] * (values.ndim - 1)
    return jnp.pad(values, pads, constant_values=fill)[: values.shape[0]]


def shift_up(values, steps, fill):
    pads = [(0, steps)] + [(0, 0)] * (values.ndim - 1)
    return jnp.pad(values, pads, constant_values=fill)[steps:]


def decorrelate(block, arcs, taps):
    count = taps.shape[0]
    forward = jnp.zeros(block.shape, jnp.float32)
    for step in range(count):
        same = (shift_down(arcs, step, -2) == arcs)[:, None]
        forward = forward + taps[step] * jnp.where(same, shift_down(block, step, 0.0), 0.0)
    backward = jnp.zeros(block.shape, jnp.float32)
    for step in range(count):
        same = (shift_up(arcs, step, -2) == arcs)[:, None]
        backward = backward + taps[step] * jnp.where(same, shift_up(forward, step, 0.0), 0.0)
    return backward


def body(static_design, tv_design, taps, arc_id):
    edge = taps.shape[0] - 1
    own_rows = static_design.shape[0]
    padded_arcs = jnp.pad(arc_id, (edge, edge), constant_values=-1)
    extended = padded(static_design, ((COL, 0),), edge)
    start = lax.axis_index(COL) * own_rows
    local_arcs = lax.dynamic_slice_in_dim(padded_arcs, start, own_rows + 2 * edge)
    filtered = decorrelate(extended.astype(jnp.float32), local_arcs, taps)
    weighted = filtered[edge : edge + own_rows].astype(jnp.bfloat16)
    whole_static = gathered_by_axis(weighted, COL, 0)
    contract = (((0,), (0,)), ((), ()))
    return lax.dot_general(
        whole_static,
        lax.all_gather(tv_design, "row", axis=0, tiled=True),
        contract,
        preferred_element_type=jnp.float32,
    )


def solution(mesh):
    finer = Mesh(mesh.devices.reshape(mesh.shape["row"], 4, 2), ("row", "col_0", "col_1"))
    placed = (P(COL, "row"), P("row", COL), P(), P())
    return jax.shard_map(
        body, mesh=finer, in_specs=placed, out_specs=P("row", COL), check_vma=False
    )
```

profile of v0, /device:TPU:1, one launch (start us, length us, event | category | flops | bytes accessed | tf_op | source)
XLA Modules:
  0.0 211.7 jit_solution(16732732377414815799)
XLA Ops:
  6.5 0.0 all-gather.2.cloned.1.call-start
  6.5 0.7 all-gather.2.cloned.1.call-update
  7.3 0.7 fusion.228
  8.0 8.3 %collective-permute-start = (bf16[31,256]{1,0:T(8,128)(2,1)S(1)}, bf16[31,256]{1,0:T(8,128)(2,1)S(1)}, u32[]{:S(2)}, u32[]{:S(2)}) collective-permute-start(bf16[31,256]{1,0:T(8,128)(2,1)S(1)} %get-tuple-element.10), channel_id=1, source_target_pairs={{0,1},{1,2},{2,3},{3,4},{4,5},{5,6},{6,7},{8,9},{9,10},{10,11},{11... | collective-permute-start | bytes 47624 | tf_op jit(solution)/shard_map/ppermute | solution.py:18
  16.3 1.3 collective-permute-start.1
  17.6 0.8 pad_dynamic-slice_fusion
  18.4 2.1 fusion.229
  20.4 0.1 slice_compare_fusion.1
  20.5 0.1 fusion.226
  20.6 0.1 fusion.225
  20.7 0.1 fusion.227
  20.8 1.8 fusion.230
  22.7 0.1 slice.674
  22.7 0.1 slice.672
  22.8 0.1 slice.676
  22.9 0.0 collective-permute-done
  22.9 1.8 collective-permute-done.1
  24.7 0.9 maximum_convert_fusion
  25.6 22.2 %fusion.128 = f32[254,256]{1,0:T(8,128)S(1)} fusion(f32[254,256]{1,0:T(8,128)S(1)} %maximum_convert_fusion, f32[]{:T(128)} %bitcast.31, f32[]{:T(128)} %bitcast.30, f32[]{:T(128)} %bitcast.29, f32[]{:T(128)} %bitcast.28, f32[]{:T(128)} %bitcast.27, f32[]{:T(128)} %bitcast.26, f32[]{:T(128)} %bitcast.25, f32[]{:T(128)} %bitcast.24, f32[]{:T(128)} %bitcast.23, ...), kind=kLoop, calls=%fused_computation.186 | loop fusion | flops 6112256 | bytes 528194 | tf_op jit(solution)/shard_map/add | solution.py:48
  47.9 0.7 fusion.160
  48.6 18.6 %fusion.146 = f32[254,256]{1,0:T(8,128)S(1)} fusion(f32[254,256]{1,0:T(8,128)S(1)} %fusion.128, f32[]{:T(128)} %bitcast.26, f32[]{:T(128)} %bitcast.25, f32[]{:T(128)} %bitcast.24, f32[]{:T(128)} %bitcast.23, f32[]{:T(128)} %bitcast.22, f32[]{:T(128)} %bitcast.21, f32[]{:T(128)} %bitcast.20, f32[]{:T(128)} %bitcast.19, f32[]{:T(128)} %bitcast.18, ...), kind=kLoop, calls=%fused_computation.204 | loop fusion | flops 5136896 | bytes 526904 | tf_op jit(solution)/shard_map/add | solution.py:52
  67.1 2.7 %fusion.164 = bf16[192,256]{1,0:T(8,128)(2,1)S(1)} fusion(f32[254,256]{1,0:T(8,128)S(1)} %get-tuple-element.7, f32[254,256]{1,0:T(8,128)S(1)} %get-tuple-element.6, f32[254,256]{1,0:T(8,128)S(1)} %get-tuple-element.8, f32[254,256]{1,0:T(8,128)S(1)} %get-tuple-element.9, f32[254,256]{1,0:T(8,128)S(1)} %get-tuple-element.5, f32[254,256]{1,0:T(8,128)S(1)} %fusion.146, ...), kind=kLoop, calls=%fused_computation.223 | loop fusion | flops 638976 | bytes 1278544 | tf_op jit(solution)/shard_map/convert
  69.9 8.3 %all_gather.9 = bf16[384,256]{1,0:T(8,128)(2,1)S(1)} all-gather(bf16[192,256]{1,0:T(8,128)(2,1)S(1)} %fusion.164), channel_id=1, replica_groups=mesh['row'=96,'col_0'=4,'col_1'=2] {'col_1'}, dimensions={0}, use_global_device_ids=true | all-gather | bytes 294912 | tf_op jit(solution)/shard_map/all_gather | solution.py:29
  78.2 11.3 %all_gather.10 = bf16[1536,256]{1,0:T(8,128)(2,1)S(1)} all-gather(bf16[384,256]{1,0:T(8,128)(2,1)S(1)} %all_gather.9), channel_id=1, replica_groups=mesh['row'=96,'col_0'=4,'col_1'=2] {'col_0'}, dimensions={0}, use_global_device_ids=true | all-gather | bytes 983040 | tf_op jit(solution)/shard_map/all_gather | solution.py:29
  89.5 107.4 %all-gather.2.cloned.1.call-done = bf16[1536,3072]{1,0:T(8,128)(2,1)} async-done(((bf16[16,3072]{1,0:T(8,128)(2,1)}), bf16[1536,3072]{1,0:T(8,128)(2,1)}) %all-gather.2.cloned.1.call-update) | async-done | bytes 9437200 | tf_op jit(solution)/shard_map/all_gather | solution.py:69
  196.8 8.0 %fusion.231 = f32[256,3072]{1,0:T(8,128)} fusion(bf16[1536,256]{1,0:T(8,128)(2,1)S(1)} %all_gather.10, bf16[1536,3072]{1,0:T(8,128)(2,1)} %all-gather.2.cloned.1.call-done), kind=kOutput, calls=%fused_computation.358 | convolution fusion | flops 2415919104 | bytes 13369344 | tf_op jit(solution)/shard_map/dot_general | solution.py:67
Async XLA Ops:
  6.5 190.3 %all-gather.2.cloned.1.call-start = ((), (), s32[]{:S(2)}) async-start(), calls=%async_computation | async-start | bytes 9535488 | tf_op jit(solution)/shard_map/all_gather | solution.py:69
  8.0 14.9 %collective-permute-start = (bf16[31,256]{1,0:T(8,128)(2,1)S(1)}, bf16[31,256]{1,0:T(8,128)(2,1)S(1)}, u32[]{:S(2)}, u32[]{:S(2)}) collective-permute-start(bf16[31,256]{1,0:T(8,128)(2,1)S(1)} %get-tuple-element.10), channel_id=1, source_target_pairs={{0,1},{1,2},{2,3},{3,4},{4,5},{5,6},{6,7},{8,9},{9,10},{10,11},{11... | collective-permute-start | bytes 47624 | tf_op jit(solution)/shard_map/ppermute | solution.py:18
  16.3 8.4 %collective-permute-start.1 = (bf16[31,256]{1,0:T(8,128)(2,1)S(1)}, bf16[31,256]{1,0:T(8,128)(2,1)S(1)}, u32[]{:S(2)}, u32[]{:S(2)}) collective-permute-start(bf16[31,256]{1,0:T(8,128)(2,1)S(1)} %get-tuple-element.11), channel_id=1, source_target_pairs={{1,0},{2,1},{3,2},{4,3},{5,4},{6,5},{7,6},{9,8},{10,9},{11,10},{12... | collective-permute-start | bytes 47624 | tf_op jit(solution)/shard_map/ppermute | solution.py:20
Sparse Core Ops, SparseCore 0:
  9.8 186.9 all-gather.1
where the time goes:
time: 213 us; the launch traced here: 212 us
  waiting for transfers between devices  110 us (52%)
  other arithmetic  45.5 us (21%)
  blocking collectives  19.6 us (9%)
  between operations  13.5 us (6%)
  starting transfers between devices  9.55 us (4%)
  matrix products  8 us (4%)
  local copies, waits for them, and re-layouts  5.66 us (3%)
    all_gather x1, waiting for transfers between devices, body(): lax.all_gather(tv_design, 'row', axis=0, tiled=True)  107 us
    add x1, other arithmetic, decorrelate(): forward + taps[step] * jnp.where(same, shift_down(block, step, 0.0), 0.0)  22.2 us
    all_gather x2, blocking collectives, gathered_by_axis(): shard = lax.all_gather(shard, axis, axis=dim, tiled=True)  19.6 us
    add x1, other arithmetic, decorrelate(): backward + taps[step] * jnp.where(same, shift_up(forward, step, 0.0), 0.0)  18.6 us
    ppermute x1, starting transfers between devices, padded(): lax.ppermute(tail, axis, [(i, (i + 1) % count) for i in range(ends)])  8.26 us
    dot_general x1, matrix products, body(): lax.dot_general(whole_static, lax.all_gather(tv_design, 'row', axis=0, ti...  8 us
  transfers between devices with their start and end apart: 3, of which 2 were waited for; matrix products, arithmetic and copies ran while one was open for 24% of the time, Pallas kernels for 0%

commit v1 on v0

v1 whole, which is shorter than its diff:
```python
import functools

import jax
import jax.numpy as jnp
from jax import lax
from jax.experimental import pallas as pl
from jax.experimental.pallas import tpu as pltpu
from jax.sharding import Mesh
from jax.sharding import PartitionSpec as P

BLOCK = 256
EDGE = 32
COL = ("col_0", "col_1")


def split(values, parts):
    pieces = []
    for _ in range(parts):
        piece = values.astype(jnp.bfloat16)
        pieces.append(piece)
        values = values - piece.astype(jnp.float32)
    return pieces


def banded(taps, lag):
    band = jnp.zeros(lag.shape, jnp.float32)
    for step in range(taps.shape[0]):
        band = jnp.where(lag == step, taps[step], band)
    return band


def weigh(groups, taps, arc_rows, arc_ahead, arc_behind, static, out, padded, *filtered):
    rows, width = static.shape
    wide = BLOCK + EDGE
    down = lax.broadcasted_iota(jnp.int32, (BLOCK, wide), 0)
    across = lax.broadcasted_iota(jnp.int32, (BLOCK, wide), 1)
    forward = banded(taps, down + EDGE - across)
    backward = banded(taps, across - down)

    padded[:EDGE] = jnp.zeros((EDGE, width), padded.dtype)
    padded[EDGE:] = static[...]
    for piece in filtered:
        piece[rows:] = jnp.zeros((EDGE, width), piece.dtype)
    dot = functools.partial(jnp.dot, preferred_element_type=jnp.float32)
    for start in range(0, rows, BLOCK):
        same = arc_rows[start : start + BLOCK] == arc_behind[:, start : start + wide]
        window = padded[start : start + wide]
        total = jnp.zeros((BLOCK, width), jnp.float32)
        for piece in split(jnp.where(same, forward, 0.0), 3)[::-1]:
            total = total + dot(piece, window)
        for ref, piece in zip(filtered, split(total, 3), strict=True):
            ref[start : start + BLOCK] = piece
    per = rows // groups // 16
    for start in range(0, rows, BLOCK):
        same = arc_rows[start : start + BLOCK] == arc_ahead[:, start : start + wide]
        pieces = split(jnp.where(same, backward, 0.0), 3)
        total = jnp.zeros((BLOCK, width), jnp.float32)
        for i, j in ((2, 0), (1, 1), (0, 2), (1, 0), (0, 1), (0, 0)):
            total = total + dot(pieces[i], filtered[j][start : start + wide])
        total = total.astype(out.dtype)
        for tile in range(BLOCK // 16):
            group, place = divmod(start // 16 + tile, per)
            at = (place * groups + group) * 16
            out[at : at + 16] = total[tile * 16 : tile * 16 + 16]


def weighted(static, taps, arc_id, groups):
    rows, width = static.shape
    spare = (0, 128 - EDGE)
    arc_behind = jnp.pad(arc_id, (EDGE, 0), constant_values=-1)
    arc_behind = jnp.pad(arc_behind, spare, constant_values=-1)[None]
    arc_ahead = jnp.pad(arc_id, (0, 128), constant_values=-1)[None]
    vmem = pl.BlockSpec(memory_space=pltpu.VMEM)
    return pl.pallas_call(
        functools.partial(weigh, groups),
        out_shape=jax.ShapeDtypeStruct((rows, width), jnp.bfloat16),
        in_specs=[pl.BlockSpec(memory_space=pltpu.SMEM)] + [vmem] * 4,
        out_specs=vmem,
        scratch_shapes=[pltpu.VMEM((rows + EDGE, width), jnp.bfloat16)] * 4,
        cost_estimate=pl.CostEstimate(
            flops=18 * rows * (BLOCK + EDGE) * width,
            bytes_accessed=4 * rows * width,
            transcendentals=0,
        ),
    )(taps, arc_id[:, None], arc_ahead, arc_behind, static)


def body(static_design, tv_design, taps, arc_id):
    short = lax.all_gather(tv_design, "short", axis=0, tiled=True)
    whole_tv = lax.all_gather(short, ("ring", "core"), axis=0, tiled=True)
    whole_static = static_design
    for axis in reversed(COL):
        whole_static = lax.all_gather(whole_static, axis, axis=0, tiled=True)
    left = weighted(whole_static, taps, arc_id, lax.axis_size("short"))
    contract = (((0,), (0,)), ((), ()))
    return lax.dot_general(left, whole_tv, contract, preferred_element_type=jnp.float32)


def solution(mesh):
    finer = Mesh(
        mesh.devices.reshape(4, 12, 2, 4, 2),
        ("short", "ring", "core", "col_0", "col_1"),
    )
    row = ("short", "ring", "core")
    placed = (P(COL, row), P(row, COL), P(), P())
    return jax.shard_map(
        body, mesh=finer, in_specs=placed, out_specs=P(row, COL), check_vma=False
    )
```

time: 213 us -> 115 us (0.54)
  waiting for transfers between devices: 110 us -> 48.1 us
  other arithmetic: 45.5 us -> 0 us
  blocking collectives: 19.6 us -> 34.8 us
  starting transfers between devices: 9.55 us -> 0.01 us
  Pallas kernels: 0 us -> 6.76 us
    all_gather x1, waiting for transfers between devices: 107 us -> 48.1 us  [body(): whole_tv = lax.all_gather(short, ('ring', 'core'), axis=0, tiled=True)]
    add x2 -> x0, other arithmetic: 40.8 us -> none  [the longest x1 22.2 us: decorrelate(): forward + taps[step] * jnp.where(same, shift_down(block, step, 0.0), 0.0)]
    all_gather x2 -> x3, blocking collectives: 19.6 us -> 34.8 us  [the longest x2 20 us: body(): whole_static = lax.all_gather(whole_static, axis, axis=0, tiled=True)]
    ppermute x2 -> x0, starting transfers between devices: 9.55 us -> none  [the longest x1 8.26 us: padded(): lax.ppermute(tail, axis, [(i, (i + 1) % count) for i in range(ends)])]
    pallas_call x0 -> x1, Pallas kernels: none -> 6.76 us  [weighted(): pl.pallas_call(functools.partial(weigh, groups), out_shape=jax.ShapeDtype...]
    slice x6 -> x0, local copies, waits for them, and re-layouts: 4.88 us -> none  [the longest x1 2.07 us: decorrelate(): taps[step] * jnp.where(same, shift_up(forward, step, 0.0), 0.0)]
    broadcast_in_dim x0 -> x3, local copies, waits for them, and re-layouts: none -> 3.04 us  [the longest x1 1.85 us: weighted(): arc_id[:, None]]
    another operation x1 -> x0, other arithmetic: 2.75 us -> none
  transfers between devices with their start and end apart: 3 -> 1, of which waited for: 2 -> 1; matrix products, arithmetic and copies ran while one was open for 24% -> 3% of each run, Pallas kernels for 0% -> 6%
where the time goes in v1:
time: 115 us
  waiting for transfers between devices  48.1 us (42%)
  blocking collectives  34.8 us (30%)
  between operations  13.4 us (12%)
  matrix products  8.26 us (7%)
  Pallas kernels  6.76 us (6%)
  local copies, waits for them, and re-layouts  3.89 us (3%)
    all_gather x1, waiting for transfers between devices, body(): whole_tv = lax.all_gather(short, ('ring', 'core'), axis=0, tiled=True)  48.1 us
    all_gather x2, blocking collectives, body(): whole_static = lax.all_gather(whole_static, axis, axis=0, tiled=True)  20 us
    all_gather x1, blocking collectives, body(): short = lax.all_gather(tv_design, 'short', axis=0, tiled=True)  14.8 us
    dot_general x1, matrix products, body(): lax.dot_general(left, whole_tv, contract, preferred_element_type=jnp.floa...  8.26 us
    pallas_call x1, Pallas kernels, weighted(): pl.pallas_call(functools.partial(weigh, groups), out_shape=jax.ShapeDtype...  6.76 us
  transfers between devices with their start and end apart: 1, of which 1 were waited for; matrix products, arithmetic and copies ran while one was open for 3% of the time, Pallas kernels for 6%

profile of v1, /device:TPU:1, one launch (start us, length us, event | category | flops | bytes accessed | tf_op | source)
XLA Modules:
  0.0 115.2 jit_solution(11619264997579160094)
XLA Ops:
  6.5 0.0 all-gather.2.cloned.1.call-start
  6.5 14.8 %all_gather.14 = bf16[64,3072]{1,0:T(8,128)(2,1)} all-gather(bf16[16,3072]{1,0:T(8,128)(2,1)} %param.5), channel_id=1, replica_groups=mesh['short'=4,'ring'=12,'core'=2,'col_0'=4,'col_1'=2] {'short'}, dimensions={0}, use_global_device_ids=true | all-gather | bytes 491520 | tf_op jit(solution)/shard_map/all_gather | solution.py:89
  21.3 0.0 all-gather.2.cloned.1.call-update
  21.3 1.8 %broadcast_in_dim.12.arc_rows = s32[1536,1]{1,0:T(8,128)} reshape(s32[1536]{0:T(1024)} %param.7) | data formatting | bytes 12288 | tf_op jit(solution)/shard_map/broadcast_in_dim | solution.py:85
  23.2 0.8 fusion
  24.0 0.6 broadcast_in_dim.11.arc_behind
  24.6 0.6 broadcast_in_dim.10.arc_ahead
  25.2 8.2 %all_gather.12 = bf16[384,256]{1,0:T(8,128)(2,1)S(1)} all-gather(bf16[192,256]{1,0:T(8,128)(2,1)} %param.4), channel_id=1, replica_groups=mesh['short'=4,'ring'=12,'core'=2,'col_0'=4,'col_1'=2] {'col_1'}, dimensions={0}, use_global_device_ids=true | all-gather | bytes 294912 | tf_op jit(solution)/shard_map/all_gather | solution.py:93
  33.5 11.8 %all_gather.13.static = bf16[1536,256]{1,0:T(8,128)(2,1)} all-gather(bf16[384,256]{1,0:T(8,128)(2,1)S(1)} %all_gather.12), channel_id=1, replica_groups=mesh['short'=4,'ring'=12,'core'=2,'col_0'=4,'col_1'=2] {'col_0'}, dimensions={0}, use_global_device_ids=true | all-gather | bytes 983040 | tf_op jit(solution)/shard_map/all_gather | solution.py:93
  45.2 6.8 %shard_map.46 = bf16[1536,256]{1,0:T(8,128)(2,1)} custom-call(f32[32]{0:T(128)} %taps.1, s32[1536,1]{1,0:T(8,128)} %broadcast_in_dim.12.arc_rows, s32[1,1664]{1,0:T(1,128)} %broadcast_in_dim.10.arc_ahead, s32[1,1664]{1,0:T(1,128)} %broadcast_in_dim.11.arc_behind, bf16[1536,256]{1,0:T(8,128)(2,1)} %all_gather.13.static), custom_call_target="tpu_custom_call" | custom-call | flops 2038431744 | bytes 1572864 | tf_op jit(solution)/shard_map/pallas_call | solution.py:74
  52.0 48.1 %all-gather.2.cloned.1.call-done = bf16[1536,3072]{1,0:T(8,128)(2,1)} async-done(((bf16[64,3072]{1,0:T(8,128)(2,1)}), bf16[1536,3072]{1,0:T(8,128)(2,1)}) %all-gather.2.cloned.1.call-update) | async-done | bytes 9437200 | tf_op jit(solution)/shard_map/all_gather | solution.py:90
  100.1 8.3 %fusion.1 = f32[256,3072]{1,0:T(8,128)} fusion(bf16[1536,256]{1,0:T(8,128)(2,1)} %shard_map.46, bf16[1536,3072]{1,0:T(8,128)(2,1)} %all-gather.2.cloned.1.call-done), kind=kOutput, calls=%fused_computation.1 | convolution fusion | flops 2415919104 | bytes 13369344 | tf_op jit(solution)/shard_map/dot_general | solution.py:96
Async XLA Ops:
  6.5 93.5 %all-gather.2.cloned.1.call-start = ((), (), s32[]{:S(2)}) async-start(), calls=%async_computation | async-start | bytes 9830400 | tf_op jit(solution)/shard_map/all_gather | solution.py:90
Sparse Core Ops, SparseCore 0:
  21.5 78.5 all-gather.1

commit v2 on v1

v2 whole, which is shorter than its diff:
```python
import functools

import jax
import jax.numpy as jnp
from jax import lax
from jax.experimental import pallas as pl
from jax.experimental.pallas import tpu as pltpu
from jax.sharding import Mesh
from jax.sharding import PartitionSpec as P

BLOCK = 256
EDGE = 32
COL = ("col_0", "col_1")


def split(values, parts):
    pieces = []
    for _ in range(parts):
        piece = values.astype(jnp.bfloat16)
        pieces.append(piece)
        values = values - piece.astype(jnp.float32)
    return pieces


def banded(taps, lag):
    band = jnp.zeros(lag.shape, jnp.float32)
    for step in range(taps.shape[0]):
        band = jnp.where(lag == step, taps[step], band)
    return band


def weigh(groups, turns, place, taps, arc_rows, arc_ahead, arc_behind, *refs):
    pairs, (out, padded, *filtered) = refs[: len(turns)], refs[len(turns) :]
    rows, width = out.shape
    wide = BLOCK + EDGE
    down = lax.broadcasted_iota(jnp.int32, (BLOCK, wide), 0)
    across = lax.broadcasted_iota(jnp.int32, (BLOCK, wide), 1)
    forward = banded(taps, down + EDGE - across)
    backward = banded(taps, across - down)

    padded[:EDGE] = jnp.zeros((EDGE, width), padded.dtype)
    for turn, pair in zip(turns, pairs, strict=True):
        own = pair.shape[1]
        for j in range(2):
            block = lax.rem(place[0] + turn, 4) * 2 + (place[1] + j) % 2
            at = pl.multiple_of(EDGE + block * own, 32)
            padded[pl.ds(at, own)] = pair[j]
    for piece in filtered:
        piece[rows:] = jnp.zeros((EDGE, width), piece.dtype)
    dot = functools.partial(jnp.dot, preferred_element_type=jnp.float32)
    for start in range(0, rows, BLOCK):
        same = arc_rows[start : start + BLOCK] == arc_behind[:, start : start + wide]
        window = padded[start : start + wide]
        total = jnp.zeros((BLOCK, width), jnp.float32)
        for piece in split(jnp.where(same, forward, 0.0), 3)[::-1]:
            total = total + dot(piece, window)
        for ref, piece in zip(filtered, split(total, 3), strict=True):
            ref[start : start + BLOCK] = piece
    per = rows // groups // 16
    for start in range(0, rows, BLOCK):
        same = arc_rows[start : start + BLOCK] == arc_ahead[:, start : start + wide]
        pieces = split(jnp.where(same, backward, 0.0), 3)
        total = jnp.zeros((BLOCK, width), jnp.float32)
        for i, j in ((2, 0), (1, 1), (0, 2), (1, 0), (0, 1), (0, 0)):
            total = total + dot(pieces[i], filtered[j][start : start + wide])
        total = total.astype(out.dtype)
        for tile in range(BLOCK // 16):
            group, spot = divmod(start // 16 + tile, per)
            at = (spot * groups + group) * 16
            out[at : at + 16] = total[tile * 16 : tile * 16 + 16]


SMEM = pl.BlockSpec(memory_space=pltpu.SMEM)
VMEM = pl.BlockSpec(memory_space=pltpu.VMEM)


def weighted(place, pairs, turns, taps, arc_id, groups):
    width = pairs[0].shape[-1]
    rows = arc_id.shape[0]
    arc_behind = jnp.pad(arc_id, (EDGE, 128 - EDGE), constant_values=-1)[None]
    arc_ahead = jnp.pad(arc_id, (0, 128), constant_values=-1)[None]
    return pl.pallas_call(
        functools.partial(weigh, groups, turns),
        out_shape=jax.ShapeDtypeStruct((rows, width), jnp.bfloat16),
        in_specs=[SMEM, SMEM] + [VMEM] * (3 + len(pairs)),
        out_specs=VMEM,
        scratch_shapes=[pltpu.VMEM((rows + EDGE, width), jnp.bfloat16)] * 4,
        compiler_params=pltpu.CompilerParams(vmem_limit_bytes=16 << 20),
        cost_estimate=pl.CostEstimate(
            flops=18 * rows * (BLOCK + EDGE) * width,
            bytes_accessed=4 * rows * width,
            transcendentals=0,
        ),
    )(place, taps, arc_id[:, None], arc_ahead, arc_behind, *pairs)


def accumulate(hops, sides, carried, spot, *refs):
    weights, refs = refs[:sides], refs[sides:]
    blocks, refs = refs[: len(hops)], refs[len(hops) :]
    priors, outs, left = refs[:carried], refs[carried : carried + sides], refs[-1]
    z, core = spot[0], spot[1]
    half = weights[0].shape[0] // 24

    @pl.when(pl.program_id(0) == 0)
    def _():
        for side in range(sides):
            picked = []
            for (hop, part), block in zip(hops, blocks, strict=True):
                origin = lax.rem(z + jnp.where(core == 0, 12 - hop, hop), 12)
                at = origin * 2 if part == 2 else origin * 2 + (core + part) % 2
                rows = pl.ds(pl.multiple_of(at * half, half), block.shape[0])
                picked.append(weights[side][rows])
            left[side] = jnp.concatenate(picked, axis=0).T

    right = jnp.concatenate([block[...] for block in blocks], axis=0)
    for side in range(sides):
        total = jnp.dot(left[side], right, preferred_element_type=jnp.float32)
        for prior in priors[side::sides]:
            total = total + prior[...]
        outs[side][...] = total


def product(spot, weights, blocks, hops, priors, tile):
    sides = len(weights)
    depth = sum(block.shape[0] for block in blocks)
    columns = blocks[0].shape[1]
    width = weights[0].shape[1]
    spec = pl.BlockSpec((width, tile), lambda i: (0, i))
    return pl.pallas_call(
        functools.partial(accumulate, hops, sides, len(priors)),
        out_shape=[jax.ShapeDtypeStruct((width, columns), jnp.float32)] * sides,
        grid=(columns // tile,),
        in_specs=[SMEM]
        + [VMEM] * sides
        + [pl.BlockSpec((b.shape[0], tile), lambda i: (0, i)) for b in blocks]
        + [spec] * len(priors),
        out_specs=[spec] * sides,
        scratch_shapes=[pltpu.VMEM((sides, width, depth), jnp.bfloat16)],
        compiler_params=pltpu.CompilerParams(vmem_limit_bytes=16 << 20),
        cost_estimate=pl.CostEstimate(
            flops=2 * sides * width * depth * columns,
            bytes_accessed=2 * depth * columns + 4 * (sides + len(priors)) * width * columns,
            transcendentals=0,
        ),
    )(spot, *weights, *blocks, *priors)


def block_of(static_design, tv_design, taps, arc_id):
    turns = lax.axis_size("ring")
    half = turns // 2
    spot = jnp.stack([lax.axis_index("ring"), lax.axis_index("core")])
    place = jnp.stack([lax.axis_index("col_0"), lax.axis_index("col_1")])
    swap = [(0, 1), (1, 0)]
    onward = [(2 * i, (i + 1) % turns * 2) for i in range(turns)]
    onward += [((i + 1) % turns * 2 + 1, i * 2 + 1) for i in range(turns)]

    def hop(block):
        return lax.ppermute(block, ("ring", "core"), onward)

    other = lax.ppermute(static_design, "col_1", swap)
    mine = [lax.all_gather(tv_design, "short", axis=0, tiled=True)]
    theirs = [lax.ppermute(mine[0], "core", swap)]

    pair = jnp.stack([static_design, other])
    steps = (1, 3, 2)
    pairs = [pair]
    for step in steps:
        pairs.append(lax.ppermute(pair, "col_0", [((i + step) % 4, i) for i in range(4)]))
    for _ in range(1, half):
        mine.append(hop(mine[-1]))
        theirs.append(hop(theirs[-1]))
    mine.append(hop(mine[-1]))

    left = weighted(place, pairs, (0,) + steps, taps, arc_id, lax.axis_size("short"))
    lefts = (left, lax.ppermute(left, "core", swap))

    def both(first, last):
        blocks = [mine[d] for d in range(first, last)]
        hops = [(d, 0) for d in range(first, last)]
        for d in range(max(first, 1), last):
            blocks.append(theirs[d])
            hops.append((d, 1))
        return blocks, tuple(hops)

    sums = product(spot, lefts, *both(0, 4), (), 512)
    sums = product(spot, lefts, *both(4, half), sums, 512)
    handed = lax.ppermute(sums[1], "core", swap)
    far = lax.all_gather(mine[half], "core", axis=0, tiled=True)
    return product(spot, lefts[:1], [far], ((half, 2),), (sums[0], handed), 512)[0]


def solution(mesh):
    finer = Mesh(
        mesh.devices.reshape(4, 12, 2, 4, 2),
        ("short", "ring", "core", "col_0", "col_1"),
    )
    row = ("short", "ring", "core")
    placed = (P(COL, row), P(row, COL), P(), P())
    return jax.shard_map(
        block_of, mesh=finer, in_specs=placed, out_specs=P(row, COL), check_vma=False
    )
```

time: 115 us -> 136 us (1.18); the launches traced: 115 us -> 134 us
  starting transfers between devices: 0.01 us -> 74.4 us
  waiting for transfers between devices: 48.1 us -> 15.3 us
  blocking collectives: 34.8 us -> 16 us
  between operations: 13.4 us -> 0.34 us
  Pallas kernels: 6.76 us -> 17 us
  matrix products: 8.26 us -> 0 us
  local copies, waits for them, and re-layouts: 3.89 us -> 9.94 us
    ppermute x0 -> x18, starting transfers between devices: none -> 74.4 us  [the longest x11 38 us: hop(): return lax.ppermute(block, ('ring', 'core'), onward)]
    all_gather x1 -> x0, waiting for transfers between devices: 48.1 us -> none  [body(): whole_tv = lax.all_gather(short, ('ring', 'core'), axis=0, tiled=True)]
    all_gather x3 -> x2, blocking collectives: 34.8 us -> 16 us  [the longest x1 12.7 us: block_of(): mine = [lax.all_gather(tv_design, 'short', axis=0, tiled=True)]]
    ppermute x0 -> x18, waiting for transfers between devices: none -> 15.3 us  [the longest x11 10.3 us: hop(): return lax.ppermute(block, ('ring', 'core'), onward)]
    pallas_call x1 -> x4, Pallas kernels: 6.76 us -> 17 us  [the longest x3 12 us: product(): pl.pallas_call(functools.partial(accumulate, hops, sides, len(priors)), o...]
    dot_general x1 -> x0, matrix products: 8.26 us -> none  [body(): lax.dot_general(left, whole_tv, contract, preferred_element_type=jnp.floa...]
    unnamed x0 -> x26, local copies, waits for them, and re-layouts: none -> 8.12 us
  transfers between devices with their start and end apart: 1 -> 18, of which waited for: 1 -> 6; matrix products, arithmetic and copies ran while one was open for 3% -> 2% of each run, Pallas kernels for 6% -> 7%
where the time goes in v2:
time: 136 us; the launch traced here: 134 us
  starting transfers between devices  74.4 us (55%)
  Pallas kernels  17 us (12%)
  blocking collectives  16 us (12%)
  waiting for transfers between devices  15.3 us (11%)
  local copies, waits for them, and re-layouts  9.94 us (7%)
    ppermute x11, starting transfers between devices, hop(): return lax.ppermute(block, ('ring', 'core'), onward)  38 us
    ppermute x1, starting transfers between devices, block_of(): theirs = [lax.ppermute(mine[0], 'core', swap)]  14.2 us
    all_gather x1, blocking collectives, block_of(): mine = [lax.all_gather(tv_design, 'short', axis=0, tiled=True)]  12.7 us
    pallas_call x3, Pallas kernels, product(): pl.pallas_call(functools.partial(accumulate, hops, sides, len(priors)), o...  12 us
    ppermute x11, waiting for transfers between devices, hop(): return lax.ppermute(block, ('ring', 'core'), onward)  10.3 us
    ppermute x3, starting transfers between devices, block_of(): lax.ppermute(pair, 'col_0', [((i + step) % 4, i) for i in range(4)])  9.93 us
    unnamed x26, local copies, waits for them, and re-layouts  8.12 us
    ppermute x1, starting transfers between devices, block_of(): other = lax.ppermute(static_design, 'col_1', swap)  7.61 us
  transfers between devices with their start and end apart: 18, of which 6 were waited for; matrix products, arithmetic and copies ran while one was open for 2% of the time, Pallas kernels for 7%

profile of v2, /device:TPU:1, one launch (start us, length us, event | category | flops | bytes accessed | tf_op | source)
XLA Modules:
  0.0 134.0 jit_solution(11542642700914069968)
XLA Ops:
  0.0 12.7 %all_gather.6.refs_2_ = bf16[64,3072]{1,0:T(8,128)(2,1)S(1)} all-gather(bf16[16,3072]{1,0:T(8,128)(2,1)} %param.5), channel_id=1, replica_groups=mesh['short'=4,'ring'=12,'core'=2,'col_0'=4,'col_1'=2] {'short'}, dimensions={0}, use_global_device_ids=true | all-gather | bytes 491520 | tf_op jit(solution)/shard_map/all_gather | solution.py:161
  12.7 14.2 %collective-permute-start.11 = (bf16[64,3072]{1,0:T(8,128)(2,1)S(1)}, bf16[64,3072]{1,0:T(8,128)(2,1)S(1)}, u32[]{:S(2)}, u32[]{:S(2)}) collective-permute-start(bf16[64,3072]{1,0:T(8,128)(2,1)S(1)} %all_gather.6.refs_2_), channel_id=1, source_target_pairs={{0,8},{8,0},{1,9},{9,1},{2,10},{10,2},{3,11},{11,3},{4,12},{12,4},... | collective-permute-start | bytes 1179656 | tf_op jit(solution)/shard_map/ppermute | solution.py:162
  26.9 5.8 %collective-permute-start.4 = (bf16[64,3072]{1,0:T(8,128)(2,1)S(1)}, bf16[64,3072]{1,0:T(8,128)(2,1)S(1)}, u32[]{:S(2)}, u32[]{:S(2)}) collective-permute-start(bf16[64,3072]{1,0:T(8,128)(2,1)S(1)} %all_gather.6.refs_2_), channel_id=1, source_target_pairs={{0,16},{16,32},{32,48},{48,64},{64,80},{80,96},{96,112},{112,128},... | collective-permute-start | bytes 1179656 | tf_op jit(solution)/shard_map/ppermute | solution.py:158
  32.7 2.2 %collective-permute-start.12 = (bf16[64,3072]{1,0:T(8,128)(2,1)S(1)}, bf16[64,3072]{1,0:T(8,128)(2,1)S(1)}, u32[]{:S(2)}, u32[]{:S(2)}) collective-permute-start(bf16[64,3072]{1,0:T(8,128)(2,1)S(1)} %collective-permute-done.11), channel_id=1, source_target_pairs={{0,16},{16,32},{32,48},{48,64},{64,80},{80,96},{96,112},{112,128},... | collective-permute-start | bytes 1179656 | tf_op jit(solution)/shard_map/ppermute | solution.py:158
  34.9 2.5 %collective-permute-done.4.refs_3_ = bf16[64,3072]{1,0:T(8,128)(2,1)S(1)} collective-permute-done((bf16[64,3072]{1,0:T(8,128)(2,1)S(1)}, bf16[64,3072]{1,0:T(8,128)(2,1)S(1)}, u32[]{:S(2)}, u32[]{:S(2)}) %collective-permute-start.4) | collective-permute-done | bytes 393248 | tf_op jit(solution)/shard_map/ppermute | solution.py:158
  37.4 5.0 %collective-permute-start.5 = (bf16[64,3072]{1,0:T(8,128)(2,1)S(1)}, bf16[64,3072]{1,0:T(8,128)(2,1)S(1)}, u32[]{:S(2)}, u32[]{:S(2)}) collective-permute-start(bf16[64,3072]{1,0:T(8,128)(2,1)S(1)} %collective-permute-done.4.refs_3_), channel_id=1, source_target_pairs={{0,16},{16,32},{32,48},{48,64},{64,80},{80,96},{96,112},{112,128},... | collective-permute-start | bytes 1179656 | tf_op jit(solution)/shard_map/ppermute | solution.py:158
  42.4 4.2 %collective-permute-start.13 = (bf16[64,3072]{1,0:T(8,128)(2,1)S(1)}, bf16[64,3072]{1,0:T(8,128)(2,1)S(1)}, u32[]{:S(2)}, u32[]{:S(2)}) collective-permute-start(bf16[64,3072]{1,0:T(8,128)(2,1)S(1)} %collective-permute-done.12.refs_6_), channel_id=1, source_target_pairs={{0,16},{16,32},{32,48},{48,64},{64,80},{80,96},{96,112},{112,128},... | collective-permute-start | bytes 1179656 | tf_op jit(solution)/shard_map/ppermute | solution.py:158
  46.6 7.6 %collective-permute-start = (bf16[192,256]{1,0:T(8,128)(2,1)}, bf16[192,256]{1,0:T(8,128)(2,1)S(1)}, u32[]{:S(2)}, u32[]{:S(2)}) collective-permute-start(bf16[192,256]{1,0:T(8,128)(2,1)} %param.4), channel_id=1, source_target_pairs={{0,1},{1,0},{2,3},{3,2},{4,5},{5,4},{6,7},{7,6},{8,9},{9,8},{10,11... | collective-permute-start | bytes 294920 | tf_op jit(solution)/shard_map/ppermute | solution.py:160
  55.2 1.5 %collective-permute-done = bf16[192,256]{1,0:T(8,128)(2,1)S(1)} collective-permute-done((bf16[192,256]{1,0:T(8,128)(2,1)}, bf16[192,256]{1,0:T(8,128)(2,1)S(1)}, u32[]{:S(2)}, u32[]{:S(2)}) %collective-permute-start) | collective-permute-done | bytes 98336 | tf_op jit(solution)/shard_map/ppermute | solution.py:160
  57.7 4.4 %collective-permute-start.1 = (bf16[2,192,256]{2,1,0:T(8,128)(2,1)S(1)}, bf16[2,192,256]{2,1,0:T(8,128)(2,1)S(1)}, u32[]{:S(2)}, u32[]{:S(2)}) collective-permute-start(bf16[2,192,256]{2,1,0:T(8,128)(2,1)S(1)} %pad_maximum_fusion.refs_0_), channel_id=1, source_target_pairs={{2,0},{4,2},{6,4},{0,6},{3,1},{5,3},{7,5},{1,7},{10,8},{12,10},{14... | collective-permute-start | bytes 589832 | tf_op jit(solution)/shard_map/ppermute | solution.py:168
  62.1 1.9 %collective-permute-start.2 = (bf16[2,192,256]{2,1,0:T(8,128)(2,1)S(1)}, bf16[2,192,256]{2,1,0:T(8,128)(2,1)S(1)}, u32[]{:S(2)}, u32[]{:S(2)}) collective-permute-start(bf16[2,192,256]{2,1,0:T(8,128)(2,1)S(1)} %pad_maximum_fusion.refs_0_), channel_id=1, source_target_pairs={{6,0},{0,2},{2,4},{4,6},{7,1},{1,3},{3,5},{5,7},{14,8},{8,10},{10,... | collective-permute-start | bytes 589832 | tf_op jit(solution)/shard_map/ppermute | solution.py:168
  64.0 3.6 %collective-permute-start.3 = (bf16[2,192,256]{2,1,0:T(8,128)(2,1)S(1)}, bf16[2,192,256]{2,1,0:T(8,128)(2,1)S(1)}, u32[]{:S(2)}, u32[]{:S(2)}) collective-permute-start(bf16[2,192,256]{2,1,0:T(8,128)(2,1)S(1)} %pad_maximum_fusion.refs_0_), channel_id=1, source_target_pairs={{4,0},{6,2},{0,4},{2,6},{5,1},{7,3},{1,5},{3,7},{12,8},{14,10},{8,... | collective-permute-start | bytes 589832 | tf_op jit(solution)/shard_map/ppermute | solution.py:168
  68.5 1.9 %collective-permute-start.6 = (bf16[64,3072]{1,0:T(8,128)(2,1)S(1)}, bf16[64,3072]{1,0:T(8,128)(2,1)S(1)}, u32[]{:S(2)}, u32[]{:S(2)}) collective-permute-start(bf16[64,3072]{1,0:T(8,128)(2,1)S(1)} %collective-permute-done.5.refs_4_), channel_id=1, source_target_pairs={{0,16},{16,32},{32,48},{48,64},{64,80},{80,96},{96,112},{112,128},... | collective-permute-start | bytes 1179656 | tf_op jit(solution)/shard_map/ppermute | solution.py:158
  70.5 1.9 %collective-permute-start.14 = (bf16[64,3072]{1,0:T(8,128)(2,1)S(1)}, bf16[64,3072]{1,0:T(8,128)(2,1)S(1)}, u32[]{:S(2)}, u32[]{:S(2)}) collective-permute-start(bf16[64,3072]{1,0:T(8,128)(2,1)S(1)} %collective-permute-done.13.refs_7_), channel_id=1, source_target_pairs={{0,16},{16,32},{32,48},{48,64},{64,80},{80,96},{96,112},{112,128},... | collective-permute-start | bytes 1179656 | tf_op jit(solution)/shard_map/ppermute | solution.py:158
  72.5 3.5 %collective-permute-done.2.refs_2_ = bf16[2,192,256]{2,1,0:T(8,128)(2,1)S(1)} collective-permute-done((bf16[2,192,256]{2,1,0:T(8,128)(2,1)S(1)}, bf16[2,192,256]{2,1,0:T(8,128)(2,1)S(1)}, u32[]{:S(2)}, u32[]{:S(2)}) %collective-permute-start.2) | collective-permute-done | bytes 196640 | tf_op jit(solution)/shard_map/ppermute | solution.py:168
  76.6 5.0 %shard_map.46.refs_0_ = bf16[1536,256]{1,0:T(8,128)(2,1)S(1)} custom-call(s32[2]{0:T(128)S(1)} %pad_add_fusion.1.place, f32[32]{0:T(128)S(1)} %copy-done.12, s32[1536,1]{1,0:T(8,128)S(1)} %broadcast_in_dim.12.arc_rows, s32[1,1664]{1,0:T(1,128)S(1)} %broadcast_in_dim.10.arc_ahead, s32[1,1664]{1,0:T(1,128)S(1)} %broadcast_in_dim.11.arc_behind, ...), custom_call_target="tpu_custom_call" | custom-call | flops 2038431744 | bytes 1572864 | tf_op jit(solution)/shard_map/pallas_call | solution.py:82
  81.6 1.9 %collective-permute-start.10 = (bf16[1536,256]{1,0:T(8,128)(2,1)S(1)}, bf16[1536,256]{1,0:T(8,128)(2,1)S(1)}, u32[]{:S(2)}, u32[]{:S(2)}) collective-permute-start(bf16[1536,256]{1,0:T(8,128)(2,1)S(1)} %shard_map.46.refs_0_), channel_id=1, source_target_pairs={{0,8},{8,0},{1,9},{9,1},{2,10},{10,2},{3,11},{11,3},{4,12},{12,4},... | collective-permute-start | bytes 2359304 | tf_op jit(solution)/shard_map/ppermute | solution.py:175
  83.6 2.8 %collective-permute-start.7 = (bf16[64,3072]{1,0:T(8,128)(2,1)S(1)}, bf16[64,3072]{1,0:T(8,128)(2,1)S(1)}, u32[]{:S(2)}, u32[]{:S(2)}) collective-permute-start(bf16[64,3072]{1,0:T(8,128)(2,1)S(1)} %collective-permute-done.6.refs_5_), channel_id=1, source_target_pairs={{0,16},{16,32},{32,48},{48,64},{64,80},{80,96},{96,112},{112,128},... | collective-permute-start | bytes 1179656 | tf_op jit(solution)/shard_map/ppermute | solution.py:158
  87.2 1.9 %collective-permute-start.15 = (bf16[64,3072]{1,0:T(8,128)(2,1)S(1)}, bf16[64,3072]{1,0:T(8,128)(2,1)S(1)}, u32[]{:S(2)}, u32[]{:S(2)}) collective-permute-start(bf16[64,3072]{1,0:T(8,128)(2,1)S(1)} %collective-permute-done.14.refs_8_), channel_id=1, source_target_pairs={{0,16},{16,32},{32,48},{48,64},{64,80},{80,96},{96,112},{112,128},... | collective-permute-start | bytes 1179656 | tf_op jit(solution)/shard_map/ppermute | solution.py:158
  89.8 2.6 %collective-permute-done.7.refs_2_ = bf16[64,3072]{1,0:T(8,128)(2,1)S(1)} collective-permute-done((bf16[64,3072]{1,0:T(8,128)(2,1)S(1)}, bf16[64,3072]{1,0:T(8,128)(2,1)S(1)}, u32[]{:S(2)}, u32[]{:S(2)}) %collective-permute-start.7) | collective-permute-done | bytes 393248 | tf_op jit(solution)/shard_map/ppermute | solution.py:158
  92.4 3.7 %collective-permute-start.8 = (bf16[64,3072]{1,0:T(8,128)(2,1)S(1)}, bf16[64,3072]{1,0:T(8,128)(2,1)S(1)}, u32[]{:S(2)}, u32[]{:S(2)}) collective-permute-start(bf16[64,3072]{1,0:T(8,128)(2,1)S(1)} %collective-permute-done.7.refs_2_), channel_id=1, source_target_pairs={{0,16},{16,32},{32,48},{48,64},{64,80},{80,96},{96,112},{112,128},... | collective-permute-start | bytes 1179656 | tf_op jit(solution)/shard_map/ppermute | solution.py:158
  96.6 3.7 %collective-permute-start.16 = (bf16[64,3072]{1,0:T(8,128)(2,1)S(1)}, bf16[64,3072]{1,0:T(8,128)(2,1)S(1)}, u32[]{:S(2)}, u32[]{:S(2)}) collective-permute-start(bf16[64,3072]{1,0:T(8,128)(2,1)S(1)} %collective-permute-done.15.refs_4_), channel_id=1, source_target_pairs={{0,16},{16,32},{32,48},{48,64},{64,80},{80,96},{96,112},{112,128},... | collective-permute-start | bytes 1179656 | tf_op jit(solution)/shard_map/ppermute | solution.py:158
  100.4 1.0 copy-done.1
  101.4 1.0 copy-done.3
  102.4 1.0 copy-done.5
  106.4 4.2 %shard_map.47 = (f32[256,3072]{1,0:T(8,128)S(1)}, f32[256,3072]{1,0:T(8,128)S(1)}) custom-call(s32[2]{0:T(128)S(1)} %pad_add_fusion.spot, bf16[1536,256]{1,0:T(8,128)(2,1)S(1)} %shard_map.46.refs_0_, bf16[1536,256]{1,0:T(8,128)(2,1)S(1)} %collective-permute-done.10.refs_1_, bf16[64,3072]{1,0:T(8,128)(2,1)S(1)} %all_gather.6.refs_2_, ...), custom_call_target="tpu_custom_call" | custom-call | flops 1409286144 | bytes 9043968 | tf_op jit(solution)/shard_map/pallas_call | solution.py:129
  110.6 3.7 %shard_map.48 = (f32[256,3072]{1,0:T(8,128)S(1)}, f32[256,3072]{1,0:T(8,128)S(1)}) custom-call(s32[2]{0:T(128)S(1)} %pad_add_fusion.spot, bf16[1536,256]{1,0:T(8,128)(2,1)S(1)} %shard_map.46.refs_0_, bf16[1536,256]{1,0:T(8,128)(2,1)S(1)} %collective-permute-done.10.refs_1_, bf16[64,3072]{1,0:T(8,128)(2,1)S(1)} %collective-permute-done.7.refs_2_, ...), custom_call_target="tpu_custom_call" | custom-call | flops 805306368 | bytes 14155776 | tf_op jit(solution)/shard_map/pallas_call | solution.py:129
  114.3 2.6 %collective-permute-start.17 = (f32[256,3072]{1,0:T(8,128)S(1)}, f32[256,3072]{1,0:T(8,128)S(1)}, u32[]{:S(2)}, u32[]{:S(2)}) collective-permute-start(f32[256,3072]{1,0:T(8,128)S(1)} %get-tuple-element.12), channel_id=1, source_target_pairs={{0,8},{8,0},{1,9},{9,1},{2,10},{10,2},{3,11},{11,3},{4,12},{12,4},... | collective-permute-start | bytes 9437192 | tf_op jit(solution)/shard_map/ppermute | solution.py:187
  117.0 4.8 %collective-permute-start.9 = (bf16[64,3072]{1,0:T(8,128)(2,1)S(1)}, bf16[64,3072]{1,0:T(8,128)(2,1)S(1)}, u32[]{:S(2)}, u32[]{:S(2)}) collective-permute-start(bf16[64,3072]{1,0:T(8,128)(2,1)S(1)} %collective-permute-done.8.refs_3_), channel_id=1, source_target_pairs={{0,16},{16,32},{32,48},{48,64},{64,80},{80,96},{96,112},{112,128},... | collective-permute-start | bytes 1179656 | tf_op jit(solution)/shard_map/ppermute | solution.py:158
  121.8 4.7 %collective-permute-done.9 = bf16[64,3072]{1,0:T(8,128)(2,1)S(1)} collective-permute-done((bf16[64,3072]{1,0:T(8,128)(2,1)S(1)}, bf16[64,3072]{1,0:T(8,128)(2,1)S(1)}, u32[]{:S(2)}, u32[]{:S(2)}) %collective-permute-start.9) | collective-permute-done | bytes 393248 | tf_op jit(solution)/shard_map/ppermute | solution.py:158
  126.5 3.3 %all_gather.7.refs_1_ = bf16[128,3072]{1,0:T(8,128)(2,1)S(1)} all-gather(bf16[64,3072]{1,0:T(8,128)(2,1)S(1)} %collective-permute-done.9), channel_id=1, replica_groups=mesh['short'=4,'ring'=12,'core'=2,'col_0'=4,'col_1'=2] {'core'}, dimensions={0}, use_global_device_ids=true | all-gather | bytes 1179648 | tf_op jit(solution)/shard_map/all_gather | solution.py:188
  129.9 4.2 %shard_map.49 = f32[256,3072]{1,0:T(8,128)} custom-call(s32[2]{0:T(128)S(1)} %pad_add_fusion.spot, bf16[1536,256]{1,0:T(8,128)(2,1)S(1)} %shard_map.46.refs_0_, bf16[128,3072]{1,0:T(8,128)(2,1)S(1)} %all_gather.7.refs_1_, f32[256,3072]{1,0:T(8,128)S(1)} %get-tuple-element.11.refs_2_, f32[256,3072]{1,0:T(8,128)S(1)} %collective-permute-done.17.refs_3_), custom_call_target="tpu_custom_call" | custom-call | flops 201326592 | bytes 10223616 | tf_op jit(solution)/shard_map/pallas_call | solution.py:129
  (43 shorter events, 8.5 us)
Async XLA Ops:
  12.7 20.0 %collective-permute-start.11 = (bf16[64,3072]{1,0:T(8,128)(2,1)S(1)}, bf16[64,3072]{1,0:T(8,128)(2,1)S(1)}, u32[]{:S(2)}, u32[]{:S(2)}) collective-permute-start(bf16[64,3072]{1,0:T(8,128)(2,1)S(1)} %all_gather.6.refs_2_), channel_id=1, source_target_pairs={{0,8},{8,0},{1,9},{9,1},{2,10},{10,2},{3,11},{11,3},{4,12},{12,4},... | collective-permute-start | bytes 1179656 | tf_op jit(solution)/shard_map/ppermute | solution.py:162
  26.9 10.5 %collective-permute-start.4 = (bf16[64,3072]{1,0:T(8,128)(2,1)S(1)}, bf16[64,3072]{1,0:T(8,128)(2,1)S(1)}, u32[]{:S(2)}, u32[]{:S(2)}) collective-permute-start(bf16[64,3072]{1,0:T(8,128)(2,1)S(1)} %all_gather.6.refs_2_), channel_id=1, source_target_pairs={{0,16},{16,32},{32,48},{48,64},{64,80},{80,96},{96,112},{112,128},... | collective-permute-start | bytes 1179656 | tf_op jit(solution)/shard_map/ppermute | solution.py:158
  32.7 9.7 %collective-permute-start.12 = (bf16[64,3072]{1,0:T(8,128)(2,1)S(1)}, bf16[64,3072]{1,0:T(8,128)(2,1)S(1)}, u32[]{:S(2)}, u32[]{:S(2)}) collective-permute-start(bf16[64,3072]{1,0:T(8,128)(2,1)S(1)} %collective-permute-done.11), channel_id=1, source_target_pairs={{0,16},{16,32},{32,48},{48,64},{64,80},{80,96},{96,112},{112,128},... | collective-permute-start | bytes 1179656 | tf_op jit(solution)/shard_map/ppermute | solution.py:158
  37.4 38.6 %copy-start = (bf16[64,3072]{1,0:T(8,128)(2,1)}, bf16[64,3072]{1,0:T(8,128)(2,1)S(1)}, u32[]{:S(2)}) copy-start(bf16[64,3072]{1,0:T(8,128)(2,1)S(1)} %collective-permute-done.4.refs_3_) | copy-start | bytes 1179652
  37.4 31.1 %collective-permute-start.5 = (bf16[64,3072]{1,0:T(8,128)(2,1)S(1)}, bf16[64,3072]{1,0:T(8,128)(2,1)S(1)}, u32[]{:S(2)}, u32[]{:S(2)}) collective-permute-start(bf16[64,3072]{1,0:T(8,128)(2,1)S(1)} %collective-permute-done.4.refs_3_), channel_id=1, source_target_pairs={{0,16},{16,32},{32,48},{48,64},{64,80},{80,96},{96,112},{112,128},... | collective-permute-start | bytes 1179656 | tf_op jit(solution)/shard_map/ppermute | solution.py:158
  42.4 33.5 %copy-start.2 = (bf16[64,3072]{1,0:T(8,128)(2,1)}, bf16[64,3072]{1,0:T(8,128)(2,1)S(1)}, u32[]{:S(2)}) copy-start(bf16[64,3072]{1,0:T(8,128)(2,1)S(1)} %collective-permute-done.12.refs_6_) | copy-start | bytes 1179652
  42.4 28.0 %collective-permute-start.13 = (bf16[64,3072]{1,0:T(8,128)(2,1)S(1)}, bf16[64,3072]{1,0:T(8,128)(2,1)S(1)}, u32[]{:S(2)}, u32[]{:S(2)}) collective-permute-start(bf16[64,3072]{1,0:T(8,128)(2,1)S(1)} %collective-permute-done.12.refs_6_), channel_id=1, source_target_pairs={{0,16},{16,32},{32,48},{48,64},{64,80},{80,96},{96,112},{112,128},... | collective-permute-start | bytes 1179656 | tf_op jit(solution)/shard_map/ppermute | solution.py:158
  46.6 10.1 %collective-permute-start = (bf16[192,256]{1,0:T(8,128)(2,1)}, bf16[192,256]{1,0:T(8,128)(2,1)S(1)}, u32[]{:S(2)}, u32[]{:S(2)}) collective-permute-start(bf16[192,256]{1,0:T(8,128)(2,1)} %param.4), channel_id=1, source_target_pairs={{0,1},{1,0},{2,3},{3,2},{4,5},{5,4},{6,7},{7,6},{8,9},{9,8},{10,11... | collective-permute-start | bytes 294920 | tf_op jit(solution)/shard_map/ppermute | solution.py:160
  57.7 14.8 %collective-permute-start.1 = (bf16[2,192,256]{2,1,0:T(8,128)(2,1)S(1)}, bf16[2,192,256]{2,1,0:T(8,128)(2,1)S(1)}, u32[]{:S(2)}, u32[]{:S(2)}) collective-permute-start(bf16[2,192,256]{2,1,0:T(8,128)(2,1)S(1)} %pad_maximum_fusion.refs_0_), channel_id=1, source_target_pairs={{2,0},{4,2},{6,4},{0,6},{3,1},{5,3},{7,5},{1,7},{10,8},{12,10},{14... | collective-permute-start | bytes 589832 | tf_op jit(solution)/shard_map/ppermute | solution.py:168
  62.1 13.9 %collective-permute-start.2 = (bf16[2,192,256]{2,1,0:T(8,128)(2,1)S(1)}, bf16[2,192,256]{2,1,0:T(8,128)(2,1)S(1)}, u32[]{:S(2)}, u32[]{:S(2)}) collective-permute-start(bf16[2,192,256]{2,1,0:T(8,128)(2,1)S(1)} %pad_maximum_fusion.refs_0_), channel_id=1, source_target_pairs={{6,0},{0,2},{2,4},{4,6},{7,1},{1,3},{3,5},{5,7},{14,8},{8,10},{10,... | collective-permute-start | bytes 589832 | tf_op jit(solution)/shard_map/ppermute | solution.py:168
  64.0 12.0 %collective-permute-start.3 = (bf16[2,192,256]{2,1,0:T(8,128)(2,1)S(1)}, bf16[2,192,256]{2,1,0:T(8,128)(2,1)S(1)}, u32[]{:S(2)}, u32[]{:S(2)}) collective-permute-start(bf16[2,192,256]{2,1,0:T(8,128)(2,1)S(1)} %pad_maximum_fusion.refs_0_), channel_id=1, source_target_pairs={{4,0},{6,2},{0,4},{2,6},{5,1},{7,3},{1,5},{3,7},{12,8},{14,10},{8,... | collective-permute-start | bytes 589832 | tf_op jit(solution)/shard_map/ppermute | solution.py:168
  68.5 13.1 %copy-start.4 = (bf16[64,3072]{1,0:T(8,128)(2,1)}, bf16[64,3072]{1,0:T(8,128)(2,1)S(1)}, u32[]{:S(2)}) copy-start(bf16[64,3072]{1,0:T(8,128)(2,1)S(1)} %collective-permute-done.5.refs_4_) | copy-start | bytes 1179652
  68.5 15.1 %collective-permute-start.6 = (bf16[64,3072]{1,0:T(8,128)(2,1)S(1)}, bf16[64,3072]{1,0:T(8,128)(2,1)S(1)}, u32[]{:S(2)}, u32[]{:S(2)}) collective-permute-start(bf16[64,3072]{1,0:T(8,128)(2,1)S(1)} %collective-permute-done.5.refs_4_), channel_id=1, source_target_pairs={{0,16},{16,32},{32,48},{48,64},{64,80},{80,96},{96,112},{112,128},... | collective-permute-start | bytes 1179656 | tf_op jit(solution)/shard_map/ppermute | solution.py:158
  70.5 11.2 %copy-start.6 = (bf16[64,3072]{1,0:T(8,128)(2,1)}, bf16[64,3072]{1,0:T(8,128)(2,1)S(1)}, u32[]{:S(2)}) copy-start(bf16[64,3072]{1,0:T(8,128)(2,1)S(1)} %collective-permute-done.13.refs_7_) | copy-start | bytes 1179652
  70.5 16.7 %collective-permute-start.14 = (bf16[64,3072]{1,0:T(8,128)(2,1)S(1)}, bf16[64,3072]{1,0:T(8,128)(2,1)S(1)}, u32[]{:S(2)}, u32[]{:S(2)}) collective-permute-start(bf16[64,3072]{1,0:T(8,128)(2,1)S(1)} %collective-permute-done.13.refs_7_), channel_id=1, source_target_pairs={{0,16},{16,32},{32,48},{48,64},{64,80},{80,96},{96,112},{112,128},... | collective-permute-start | bytes 1179656 | tf_op jit(solution)/shard_map/ppermute | solution.py:158
  76.0 0.7 copy-start.12
  81.6 18.8 %collective-permute-start.10 = (bf16[1536,256]{1,0:T(8,128)(2,1)S(1)}, bf16[1536,256]{1,0:T(8,128)(2,1)S(1)}, u32[]{:S(2)}, u32[]{:S(2)}) collective-permute-start(bf16[1536,256]{1,0:T(8,128)(2,1)S(1)} %shard_map.46.refs_0_), channel_id=1, source_target_pairs={{0,8},{8,0},{1,9},{9,1},{2,10},{10,2},{3,11},{11,3},{4,12},{12,4},... | collective-permute-start | bytes 2359304 | tf_op jit(solution)/shard_map/ppermute | solution.py:175
  83.6 8.8 %collective-permute-start.7 = (bf16[64,3072]{1,0:T(8,128)(2,1)S(1)}, bf16[64,3072]{1,0:T(8,128)(2,1)S(1)}, u32[]{:S(2)}, u32[]{:S(2)}) collective-permute-start(bf16[64,3072]{1,0:T(8,128)(2,1)S(1)} %collective-permute-done.6.refs_5_), channel_id=1, source_target_pairs={{0,16},{16,32},{32,48},{48,64},{64,80},{80,96},{96,112},{112,128},... | collective-permute-start | bytes 1179656 | tf_op jit(solution)/shard_map/ppermute | solution.py:158
  86.4 0.7 copy-start.8
  87.2 9.5 %collective-permute-start.15 = (bf16[64,3072]{1,0:T(8,128)(2,1)S(1)}, bf16[64,3072]{1,0:T(8,128)(2,1)S(1)}, u32[]{:S(2)}, u32[]{:S(2)}) collective-permute-start(bf16[64,3072]{1,0:T(8,128)(2,1)S(1)} %collective-permute-done.14.refs_8_), channel_id=1, source_target_pairs={{0,16},{16,32},{32,48},{48,64},{64,80},{80,96},{96,112},{112,128},... | collective-permute-start | bytes 1179656 | tf_op jit(solution)/shard_map/ppermute | solution.py:158
  89.1 0.8 copy-start.10
  92.4 18.2 %collective-permute-start.8 = (bf16[64,3072]{1,0:T(8,128)(2,1)S(1)}, bf16[64,3072]{1,0:T(8,128)(2,1)S(1)}, u32[]{:S(2)}, u32[]{:S(2)}) collective-permute-start(bf16[64,3072]{1,0:T(8,128)(2,1)S(1)} %collective-permute-done.7.refs_2_), channel_id=1, source_target_pairs={{0,16},{16,32},{32,48},{48,64},{64,80},{80,96},{96,112},{112,128},... | collective-permute-start | bytes 1179656 | tf_op jit(solution)/shard_map/ppermute | solution.py:158
  96.6 14.0 %collective-permute-start.16 = (bf16[64,3072]{1,0:T(8,128)(2,1)S(1)}, bf16[64,3072]{1,0:T(8,128)(2,1)S(1)}, u32[]{:S(2)}, u32[]{:S(2)}) collective-permute-start(bf16[64,3072]{1,0:T(8,128)(2,1)S(1)} %collective-permute-done.15.refs_4_), channel_id=1, source_target_pairs={{0,16},{16,32},{32,48},{48,64},{64,80},{80,96},{96,112},{112,128},... | collective-permute-start | bytes 1179656 | tf_op jit(solution)/shard_map/ppermute | solution.py:158
  100.4 1.0 copy-start.1
  101.4 1.0 copy-start.3
  102.4 1.0 copy-start.5
  103.4 1.0 copy-start.7
  104.4 1.0 copy-start.9
  105.4 1.0 copy-start.11
  114.3 15.5 %collective-permute-start.17 = (f32[256,3072]{1,0:T(8,128)S(1)}, f32[256,3072]{1,0:T(8,128)S(1)}, u32[]{:S(2)}, u32[]{:S(2)}) collective-permute-start(f32[256,3072]{1,0:T(8,128)S(1)} %get-tuple-element.12), channel_id=1, source_target_pairs={{0,8},{8,0},{1,9},{9,1},{2,10},{10,2},{3,11},{11,3},{4,12},{12,4},... | collective-permute-start | bytes 9437192 | tf_op jit(solution)/shard_map/ppermute | solution.py:187
  117.0 9.6 %collective-permute-start.9 = (bf16[64,3072]{1,0:T(8,128)(2,1)S(1)}, bf16[64,3072]{1,0:T(8,128)(2,1)S(1)}, u32[]{:S(2)}, u32[]{:S(2)}) collective-permute-start(bf16[64,3072]{1,0:T(8,128)(2,1)S(1)} %collective-permute-done.8.refs_3_), channel_id=1, source_target_pairs={{0,16},{16,32},{32,48},{48,64},{64,80},{80,96},{96,112},{112,128},... | collective-permute-start | bytes 1179656 | tf_op jit(solution)/shard_map/ppermute | solution.py:158

commit v3 on v2

--- a/solution.py
+++ b/solution.py
@@ -8,7 +8,7 @@
 from jax.sharding import Mesh
 from jax.sharding import PartitionSpec as P
 
-BLOCK = 256
+BLOCK = 192
 EDGE = 32
 COL = ("col_0", "col_1")
 
@@ -29,8 +29,8 @@
     return band
 
 
-def weigh(groups, turns, place, taps, arc_rows, arc_ahead, arc_behind, *refs):
-    pairs, (out, padded, *filtered) = refs[: len(turns)], refs[len(turns) :]
+def weigh(groups, places, taps, arc_rows, arc_ahead, arc_behind, *refs):
+    stacks, (out, padded, *filtered) = refs[:3], refs[3:]
     rows, width = out.shape
     wide = BLOCK + EDGE
     down = lax.broadcasted_iota(jnp.int32, (BLOCK, wide), 0)
@@ -39,12 +39,11 @@
     backward = banded(taps, across - down)
 
     padded[:EDGE] = jnp.zeros((EDGE, width), padded.dtype)
-    for turn, pair in zip(turns, pairs, strict=True):
-        own = pair.shape[1]
-        for j in range(2):
-            block = lax.rem(place[0] + turn, 4) * 2 + (place[1] + j) % 2
-            at = pl.multiple_of(EDGE + block * own, 32)
-            padded[pl.ds(at, own)] = pair[j]
+    blocks = [(stack, i) for stack in stacks for i in range(stack.shape[0])]
+    for number, (stack, i) in enumerate(blocks):
+        own = stack.shape[1]
+        at = pl.multiple_of(EDGE + places[number] * own, 32)
+        padded[pl.ds(at, own)] = stack[i]
     for piece in filtered:
         piece[rows:] = jnp.zeros((EDGE, width), piece.dtype)
     dot = functools.partial(jnp.dot, preferred_element_type=jnp.float32)
@@ -74,15 +73,15 @@
 VMEM = pl.BlockSpec(memory_space=pltpu.VMEM)
 
 
-def weighted(place, pairs, turns, taps, arc_id, groups):
-    width = pairs[0].shape[-1]
+def weighted(places, stacks, taps, arc_id, groups):
+    width = stacks[0].shape[-1]
     rows = arc_id.shape[0]
     arc_behind = jnp.pad(arc_id, (EDGE, 128 - EDGE), constant_values=-1)[None]
     arc_ahead = jnp.pad(arc_id, (0, 128), constant_values=-1)[None]
     return pl.pallas_call(
-        functools.partial(weigh, groups, turns),
+        functools.partial(weigh, groups),
         out_shape=jax.ShapeDtypeStruct((rows, width), jnp.bfloat16),
-        in_specs=[SMEM, SMEM] + [VMEM] * (3 + len(pairs)),
+        in_specs=[SMEM, SMEM] + [VMEM] * (3 + len(stacks)),
         out_specs=VMEM,
         scratch_shapes=[pltpu.VMEM((rows + EDGE, width), jnp.bfloat16)] * 4,
         compiler_params=pltpu.CompilerParams(vmem_limit_bytes=16 << 20),
@@ -91,24 +90,21 @@
             bytes_accessed=4 * rows * width,
             transcendentals=0,
         ),
-    )(place, taps, arc_id[:, None], arc_ahead, arc_behind, *pairs)
-
-
-def accumulate(hops, sides, carried, spot, *refs):
+    )(places, taps, arc_id[:, None], arc_ahead, arc_behind, *stacks)
+
+
+def accumulate(count, sides, carried, at, *refs):
     weights, refs = refs[:sides], refs[sides:]
-    blocks, refs = refs[: len(hops)], refs[len(hops) :]
+    blocks, refs = refs[:count], refs[count:]
     priors, outs, left = refs[:carried], refs[carried : carried + sides], refs[-1]
-    z, core = spot[0], spot[1]
     half = weights[0].shape[0] // 24
 
     @pl.when(pl.program_id(0) == 0)
     def _():
         for side in range(sides):
             picked = []
-            for (hop, part), block in zip(hops, blocks, strict=True):
-                origin = lax.rem(z + jnp.where(core == 0, 12 - hop, hop), 12)
-                at = origin * 2 if part == 2 else origin * 2 + (core + part) % 2
-                rows = pl.ds(pl.multiple_of(at * half, half), block.shape[0])
+            for number in range(left.shape[2] // half):
+                rows = pl.ds(pl.multiple_of(at[number] * half, half), half)
                 picked.append(weights[side][rows])
             left[side] = jnp.concatenate(picked, axis=0).T
 
@@ -120,14 +116,14 @@
         outs[side][...] = total
 
 
-def product(spot, weights, blocks, hops, priors, tile):
+def product(at, weights, blocks, priors, tile):
     sides = len(weights)
     depth = sum(block.shape[0] for block in blocks)
     columns = blocks[0].shape[1]
     width = weights[0].shape[1]
     spec = pl.BlockSpec((width, tile), lambda i: (0, i))
     return pl.pallas_call(
-        functools.partial(accumulate, hops, sides, len(priors)),
+        functools.partial(accumulate, len(blocks), sides, len(priors)),
         out_shape=[jax.ShapeDtypeStruct((width, columns), jnp.float32)] * sides,
         grid=(columns // tile,),
         in_specs=[SMEM]
@@ -142,14 +138,13 @@
             bytes_accessed=2 * depth * columns + 4 * (sides + len(priors)) * width * columns,
             transcendentals=0,
         ),
-    )(spot, *weights, *blocks, *priors)
+    )(at, *weights, *blocks, *priors)
 
 
 def block_of(static_design, tv_design, taps, arc_id):
     turns = lax.axis_size("ring")
     half = turns // 2
-    spot = jnp.stack([lax.axis_index("ring"), lax.axis_index("core")])
-    place = jnp.stack([lax.axis_index("col_0"), lax.axis_index("col_1")])
+    ring, core = lax.axis_index("ring"), lax.axis_index("core")
     swap = [(0, 1), (1, 0)]
     onward = [(2 * i, (i + 1) % turns * 2) for i in range(turns)]
     onward += [((i + 1) % turns * 2 + 1, i * 2 + 1) for i in range(turns)]
@@ -162,31 +157,37 @@
     theirs = [lax.ppermute(mine[0], "core", swap)]
 
     pair = jnp.stack([static_design, other])
-    steps = (1, 3, 2)
-    pairs = [pair]
-    for step in steps:
-        pairs.append(lax.ppermute(pair, "col_0", [((i + step) % 4, i) for i in range(4)]))
+    beside = lax.ppermute(pair, "col_0", [(i, i ^ 1) for i in range(4)])
+    opposite = lax.ppermute(jnp.concatenate([pair, beside]), "col_0", [(i, 3 - i) for i in range(4)])
+    places = (lax.axis_index("col_0") ^ jnp.array([0, 0, 1, 1, 3, 3, 2, 2], jnp.int32)) * 2
+    places = places + (lax.axis_index("col_1") ^ jnp.array([0, 1] * 4, jnp.int32))
+
     for _ in range(1, half):
         mine.append(hop(mine[-1]))
         theirs.append(hop(theirs[-1]))
     mine.append(hop(mine[-1]))
 
-    left = weighted(place, pairs, (0,) + steps, taps, arc_id, lax.axis_size("short"))
+    left = weighted(places, (pair, beside, opposite), taps, arc_id, lax.axis_size("short"))
     lefts = (left, lax.ppermute(left, "core", swap))
 
-    def both(first, last):
-        blocks = [mine[d] for d in range(first, last)]
-        hops = [(d, 0) for d in range(first, last)]
-        for d in range(max(first, 1), last):
-            blocks.append(theirs[d])
-            hops.append((d, 1))
-        return blocks, tuple(hops)
-
-    sums = product(spot, lefts, *both(0, 4), (), 512)
-    sums = product(spot, lefts, *both(4, half), sums, 512)
+    def chosen(blocks):
+        part = jnp.array([part for part, _ in blocks], jnp.int32)
+        steps = jnp.array([steps for _, steps in blocks], jnp.int32)
+        origin = (ring + turns + jnp.where(core == 0, -steps, steps)) % turns
+        return origin * 2 + (core + part) % 2
+
+    def near(blocks, priors):
+        tv = [(mine, theirs)[part][steps] for part, steps in blocks]
+        return product(chosen(blocks), lefts, tv, priors, 512)
+
+    sums = near([(0, d) for d in range(4)] + [(1, d) for d in range(1, 4)], ())
+    sums = near([(0, 4), (1, 4), (0, 5)], sums)
     handed = lax.ppermute(sums[1], "core", swap)
-    far = lax.all_gather(mine[half], "core", axis=0, tiled=True)
-    return product(spot, lefts[:1], [far], ((half, 2),), (sums[0], handed), 512)[0]
+    far = [lax.all_gather(theirs[half - 1], "core", axis=0, tiled=True)]
+    far.append(lax.all_gather(mine[half], "core", axis=0, tiled=True))
+    steps = jnp.array([1 - half, half - 1, -half, half], jnp.int32)
+    at = (ring + turns + steps) % turns * 2 + jnp.array([1, 0, 0, 1], jnp.int32)
+    return product(at, lefts[:1], far, (sums[0], handed), 512)[0]
 
 
 def solution(mesh):

time: 136 us -> 122 us (0.90)
  starting transfers between devices: 74.4 us -> 65.8 us
  local copies, waits for them, and re-layouts: 9.94 us -> 4.24 us
  waiting for transfers between devices: 15.3 us -> 9.73 us
  blocking collectives: 16 us -> 20.8 us
  other arithmetic: 1.07 us -> 3.25 us
    ppermute x11, starting transfers between devices: 38 us -> 30.1 us  [hop(): return lax.ppermute(block, ('ring', 'core'), onward)]
    unnamed x26 -> x18, local copies, waits for them, and re-layouts: 8.12 us -> 2.43 us
    all_gather x1 -> x2, blocking collectives: 3.32 us -> 8.12 us  [the longest x1 4.06 us: block_of(): far.append(lax.all_gather(mine[half], 'core', axis=0, tiled=True))]
    ppermute x11, waiting for transfers between devices: 10.3 us -> 7.48 us  [hop(): return lax.ppermute(block, ('ring', 'core'), onward)]
    ppermute x3 -> x2, starting transfers between devices: 9.93 us -> 7.51 us  [the longest x1 4.39 us: block_of(): lax.ppermute(jnp.concatenate([pair, beside]), 'col_0', [(i, 3 - i) for i...]
    ppermute x1, starting transfers between devices: 2.65 us -> 4.47 us  [block_of(): handed = lax.ppermute(sums[1], 'core', swap)]
    ppermute x1, waiting for transfers between devices: 1.53 us -> 0.01 us  [block_of(): other = lax.ppermute(static_design, 'col_1', swap)]
    add x0 -> x4, other arithmetic: none -> 1.4 us  [the longest x2 0.71 us: chosen(): return origin * 2 + (core + part) % 2]
  transfers between devices with their start and end apart: 18 -> 17, of which waited for: 6 -> 6; matrix products, arithmetic and copies ran while one was open for 2% -> 4% of each run, Pallas kernels for 7% -> 7%
where the time goes in v3:
time: 122 us; the launch traced here: 121 us
  starting transfers between devices  65.8 us (54%)
  blocking collectives  20.8 us (17%)
  Pallas kernels  16.4 us (13%)
  waiting for transfers between devices  9.73 us (8%)
  local copies, waits for them, and re-layouts  4.24 us (3%)
  other arithmetic  3.25 us (3%)
    ppermute x11, starting transfers between devices, hop(): return lax.ppermute(block, ('ring', 'core'), onward)  30.1 us
    ppermute x1, starting transfers between devices, block_of(): theirs = [lax.ppermute(mine[0], 'core', swap)]  14.2 us
    pallas_call x3, Pallas kernels, product(): pl.pallas_call(functools.partial(accumulate, len(blocks), sides, len(prio...  12.9 us
    all_gather x1, blocking collectives, block_of(): mine = [lax.all_gather(tv_design, 'short', axis=0, tiled=True)]  12.7 us
    ppermute x1, starting transfers between devices, block_of(): other = lax.ppermute(static_design, 'col_1', swap)  7.61 us
    ppermute x11, waiting for transfers between devices, hop(): return lax.ppermute(block, ('ring', 'core'), onward)  7.48 us
    ppermute x1, starting transfers between devices, block_of(): handed = lax.ppermute(sums[1], 'core', swap)  4.47 us
    ppermute x1, starting transfers between devices, block_of(): lax.ppermute(jnp.concatenate([pair, beside]), 'col_0', [(i, 3 - i) for i...  4.39 us
  transfers between devices with their start and end apart: 17, of which 6 were waited for; matrix products, arithmetic and copies ran while one was open for 4% of the time, Pallas kernels for 7%

profile of v3, /device:TPU:1, one launch (start us, length us, event | category | flops | bytes accessed | tf_op | source)
XLA Modules:
  0.0 120.6 jit_solution(7378693273487713524)
XLA Ops:
  0.0 12.7 %all_gather.9.refs_2_ = bf16[64,3072]{1,0:T(8,128)(2,1)S(1)} all-gather(bf16[16,3072]{1,0:T(8,128)(2,1)} %param.13), channel_id=1, replica_groups=mesh['short'=4,'ring'=12,'core'=2,'col_0'=4,'col_1'=2] {'short'}, dimensions={0}, use_global_device_ids=true | all-gather | bytes 491520 | tf_op jit(solution)/shard_map/all_gather | solution.py:156
  12.7 14.2 %collective-permute-start.3 = (bf16[64,3072]{1,0:T(8,128)(2,1)S(1)}, bf16[64,3072]{1,0:T(8,128)(2,1)S(1)}, u32[]{:S(2)}, u32[]{:S(2)}) collective-permute-start(bf16[64,3072]{1,0:T(8,128)(2,1)S(1)} %all_gather.9.refs_2_), channel_id=1, source_target_pairs={{0,8},{8,0},{1,9},{9,1},{2,10},{10,2},{3,11},{11,3},{4,12},{12,4},... | collective-permute-start | bytes 1179656 | tf_op jit(solution)/shard_map/ppermute | solution.py:157
  26.9 5.8 %collective-permute-start.9 = (bf16[64,3072]{1,0:T(8,128)(2,1)S(1)}, bf16[64,3072]{1,0:T(8,128)(2,1)S(1)}, u32[]{:S(2)}, u32[]{:S(2)}) collective-permute-start(bf16[64,3072]{1,0:T(8,128)(2,1)S(1)} %all_gather.9.refs_2_), channel_id=1, source_target_pairs={{0,16},{16,32},{32,48},{48,64},{64,80},{80,96},{96,112},{112,128},... | collective-permute-start | bytes 1179656 | tf_op jit(solution)/shard_map/ppermute | solution.py:153
  32.7 7.6 %collective-permute-start = (bf16[192,256]{1,0:T(8,128)(2,1)}, bf16[192,256]{1,0:T(8,128)(2,1)S(1)}, u32[]{:S(2)}, u32[]{:S(2)}) collective-permute-start(bf16[192,256]{1,0:T(8,128)(2,1)} %param.12), channel_id=1, source_target_pairs={{0,1},{1,0},{2,3},{3,2},{4,5},{5,4},{6,7},{7,6},{8,9},{9,8},{10,11... | collective-permute-start | bytes 294920 | tf_op jit(solution)/shard_map/ppermute | solution.py:155
  40.3 2.2 %collective-permute-start.4 = (bf16[64,3072]{1,0:T(8,128)(2,1)S(1)}, bf16[64,3072]{1,0:T(8,128)(2,1)S(1)}, u32[]{:S(2)}, u32[]{:S(2)}) collective-permute-start(bf16[64,3072]{1,0:T(8,128)(2,1)S(1)} %collective-permute-done.3), channel_id=1, source_target_pairs={{0,16},{16,32},{32,48},{48,64},{64,80},{80,96},{96,112},{112,128},... | collective-permute-start | bytes 1179656 | tf_op jit(solution)/shard_map/ppermute | solution.py:153
  42.5 2.2 %collective-permute-start.10 = (bf16[64,3072]{1,0:T(8,128)(2,1)S(1)}, bf16[64,3072]{1,0:T(8,128)(2,1)S(1)}, u32[]{:S(2)}, u32[]{:S(2)}) collective-permute-start(bf16[64,3072]{1,0:T(8,128)(2,1)S(1)} %collective-permute-done.9.refs_3_), channel_id=1, source_target_pairs={{0,16},{16,32},{32,48},{48,64},{64,80},{80,96},{96,112},{112,128},... | collective-permute-start | bytes 1179656 | tf_op jit(solution)/shard_map/ppermute | solution.py:153
  44.7 0.9 pad_maximum_fusion.1.refs_0_
  45.6 3.1 %collective-permute-start.1 = (bf16[2,192,256]{2,1,0:T(8,128)(2,1)S(1)}, bf16[2,192,256]{2,1,0:T(8,128)(2,1)S(1)}, u32[]{:S(2)}, u32[]{:S(2)}) collective-permute-start(bf16[2,192,256]{2,1,0:T(8,128)(2,1)S(1)} %pad_maximum_fusion.1.refs_0_), channel_id=1, source_target_pairs={{0,2},{2,0},{4,6},{6,4},{1,3},{3,1},{5,7},{7,5},{8,10},{10,8},{12,... | collective-permute-start | bytes 589832 | tf_op jit(solution)/shard_map/ppermute | solution.py:160
  49.1 3.1 %collective-permute-start.5 = (bf16[64,3072]{1,0:T(8,128)(2,1)S(1)}, bf16[64,3072]{1,0:T(8,128)(2,1)}, u32[]{:S(2)}, u32[]{:S(2)}) collective-permute-start(bf16[64,3072]{1,0:T(8,128)(2,1)S(1)} %collective-permute-done.4.refs_6_), channel_id=1, source_target_pairs={{0,16},{16,32},{32,48},{48,64},{64,80},{80,96},{96,112},{112,128},... | collective-permute-start | bytes 1179656 | tf_op jit(solution)/shard_map/ppermute | solution.py:153
  53.1 3.4 %collective-permute-start.11 = (bf16[64,3072]{1,0:T(8,128)(2,1)S(1)}, bf16[64,3072]{1,0:T(8,128)(2,1)}, u32[]{:S(2)}, u32[]{:S(2)}) collective-permute-start(bf16[64,3072]{1,0:T(8,128)(2,1)S(1)} %collective-permute-done.10.refs_4_), channel_id=1, source_target_pairs={{0,16},{16,32},{32,48},{48,64},{64,80},{80,96},{96,112},{112,128},... | collective-permute-start | bytes 1179656 | tf_op jit(solution)/shard_map/ppermute | solution.py:153
  56.5 0.9 pad_maximum_fusion
  57.4 4.4 %collective-permute-start.2 = (bf16[4,192,256]{2,1,0:T(8,128)(2,1)S(1)}, bf16[4,192,256]{2,1,0:T(8,128)(2,1)S(1)}, u32[]{:S(2)}, u32[]{:S(2)}) collective-permute-start(bf16[4,192,256]{2,1,0:T(8,128)(2,1)S(1)} %pad_maximum_fusion), channel_id=1, source_target_pairs={{0,6},{2,4},{4,2},{6,0},{1,7},{3,5},{5,3},{7,1},{8,14},{10,12},{12... | collective-permute-start | bytes 1179656 | tf_op jit(solution)/shard_map/ppermute | solution.py:161
  61.8 1.0 broadcast_in_dim.12.arc_rows
  62.8 0.8 fusion.12
  64.4 1.9 %collective-permute-start.6 = (bf16[64,3072]{1,0:T(8,128)(2,1)}, bf16[64,3072]{1,0:T(8,128)(2,1)}, u32[]{:S(2)}, u32[]{:S(2)}) collective-permute-start(bf16[64,3072]{1,0:T(8,128)(2,1)} %collective-permute-done.5.refs_7_), channel_id=1, source_target_pairs={{0,16},{16,32},{32,48},{48,64},{64,80},{80,96},{96,112},{112,128},... | collective-permute-start | bytes 1179656 | tf_op jit(solution)/shard_map/ppermute | solution.py:153
  66.3 1.9 %collective-permute-start.12 = (bf16[64,3072]{1,0:T(8,128)(2,1)}, bf16[64,3072]{1,0:T(8,128)(2,1)S(1)}, u32[]{:S(2)}, u32[]{:S(2)}) collective-permute-start(bf16[64,3072]{1,0:T(8,128)(2,1)} %collective-permute-done.11.refs_5_), channel_id=1, source_target_pairs={{0,16},{16,32},{32,48},{48,64},{64,80},{80,96},{96,112},{112,128},... | collective-permute-start | bytes 1179656 | tf_op jit(solution)/shard_map/ppermute | solution.py:153
  68.2 2.2 %collective-permute-done.2.refs_2_ = bf16[4,192,256]{2,1,0:T(8,128)(2,1)S(1)} collective-permute-done((bf16[4,192,256]{2,1,0:T(8,128)(2,1)S(1)}, bf16[4,192,256]{2,1,0:T(8,128)(2,1)S(1)}, u32[]{:S(2)}, u32[]{:S(2)}) %collective-permute-start.2) | collective-permute-done | bytes 393248 | tf_op jit(solution)/shard_map/ppermute | solution.py:161
  71.2 1.0 copy-done.1
  72.9 3.5 %shard_map.118.refs_0_ = bf16[1536,256]{1,0:T(8,128)(2,1)S(1)} custom-call(s32[8]{0:T(128)S(1)} %xor_add_fusion.places, f32[32]{0:T(128)S(1)} %copy-done.2, s32[1536,1]{1,0:T(8,128)S(1)} %broadcast_in_dim.12.arc_rows, s32[1,1664]{1,0:T(1,128)S(1)} %broadcast_in_dim.10.arc_ahead, s32[1,1664]{1,0:T(1,128)S(1)} %broadcast_in_dim.11.arc_behind, ...), custom_call_target="tpu_custom_call" | custom-call | flops 1585446912 | bytes 1572864 | tf_op jit(solution)/shard_map/pallas_call | solution.py:81
  76.3 1.9 %collective-permute-start.15 = (bf16[1536,256]{1,0:T(8,128)(2,1)S(1)}, bf16[1536,256]{1,0:T(8,128)(2,1)S(1)}, u32[]{:S(2)}, u32[]{:S(2)}) collective-permute-start(bf16[1536,256]{1,0:T(8,128)(2,1)S(1)} %shard_map.118.refs_0_), channel_id=1, source_target_pairs={{0,8},{8,0},{1,9},{9,1},{2,10},{10,2},{3,11},{11,3},{4,12},{12,4},... | collective-permute-start | bytes 2359304 | tf_op jit(solution)/shard_map/ppermute | solution.py:171
  78.3 3.5 %collective-permute-start.13 = (bf16[64,3072]{1,0:T(8,128)(2,1)S(1)}, bf16[64,3072]{1,0:T(8,128)(2,1)S(1)}, u32[]{:S(2)}, u32[]{:S(2)}) collective-permute-start(bf16[64,3072]{1,0:T(8,128)(2,1)S(1)} %collective-permute-done.12.refs_2_), channel_id=1, source_target_pairs={{0,16},{16,32},{32,48},{48,64},{64,80},{80,96},{96,112},{112,128},... | collective-permute-start | bytes 1179656 | tf_op jit(solution)/shard_map/ppermute | solution.py:153
  81.8 1.9 %collective-permute-start.7 = (bf16[64,3072]{1,0:T(8,128)(2,1)}, bf16[64,3072]{1,0:T(8,128)(2,1)S(1)}, u32[]{:S(2)}, u32[]{:S(2)}) collective-permute-start(bf16[64,3072]{1,0:T(8,128)(2,1)} %collective-permute-done.6.refs_8_), channel_id=1, source_target_pairs={{0,16},{16,32},{32,48},{48,64},{64,80},{80,96},{96,112},{112,128},... | collective-permute-start | bytes 1179656 | tf_op jit(solution)/shard_map/ppermute | solution.py:153
  84.5 5.2 %shard_map.119 = (f32[256,3072]{1,0:T(8,128)S(1)}, f32[256,3072]{1,0:T(8,128)S(1)}) custom-call(s32[7]{0:T(128)S(1)} %fusion.1.at, bf16[1536,256]{1,0:T(8,128)(2,1)S(1)} %shard_map.118.refs_0_, bf16[1536,256]{1,0:T(8,128)(2,1)S(1)} %collective-permute-done.15.refs_1_, bf16[64,3072]{1,0:T(8,128)(2,1)S(1)} %all_gather.9.refs_2_, ...), custom_call_target="tpu_custom_call" | custom-call | flops 1409286144 | bytes 9043968 | tf_op jit(solution)/shard_map/pallas_call | solution.py:125
  89.7 1.6 %collective-permute-done.7.refs_3_ = bf16[64,3072]{1,0:T(8,128)(2,1)S(1)} collective-permute-done((bf16[64,3072]{1,0:T(8,128)(2,1)}, bf16[64,3072]{1,0:T(8,128)(2,1)S(1)}, u32[]{:S(2)}, u32[]{:S(2)}) %collective-permute-start.7) | collective-permute-done | bytes 393248 | tf_op jit(solution)/shard_map/ppermute | solution.py:153
  91.3 3.4 %shard_map.120 = (f32[256,3072]{1,0:T(8,128)S(1)}, f32[256,3072]{1,0:T(8,128)S(1)}) custom-call(s32[3]{0:T(128)S(1)} %fusion.at, bf16[1536,256]{1,0:T(8,128)(2,1)S(1)} %shard_map.118.refs_0_, bf16[1536,256]{1,0:T(8,128)(2,1)S(1)} %collective-permute-done.15.refs_1_, bf16[64,3072]{1,0:T(8,128)(2,1)S(1)} %collective-permute-done.12.refs_2_, ...), custom_call_target="tpu_custom_call" | custom-call | flops 603979776 | bytes 13762560 | tf_op jit(solution)/shard_map/pallas_call | solution.py:125
  94.7 4.5 %collective-permute-start.16 = (f32[256,3072]{1,0:T(8,128)S(1)}, f32[256,3072]{1,0:T(8,128)S(1)}, u32[]{:S(2)}, u32[]{:S(2)}) collective-permute-start(f32[256,3072]{1,0:T(8,128)S(1)} %get-tuple-element.12), channel_id=1, source_target_pairs={{0,8},{8,0},{1,9},{9,1},{2,10},{10,2},{3,11},{11,3},{4,12},{12,4},... | collective-permute-start | bytes 9437192 | tf_op jit(solution)/shard_map/ppermute | solution.py:185
  99.2 1.9 %collective-permute-start.14 = (bf16[64,3072]{1,0:T(8,128)(2,1)S(1)}, bf16[64,3072]{1,0:T(8,128)(2,1)S(1)}, u32[]{:S(2)}, u32[]{:S(2)}) collective-permute-start(bf16[64,3072]{1,0:T(8,128)(2,1)S(1)} %collective-permute-done.13.refs_4_), channel_id=1, source_target_pairs={{0,16},{16,32},{32,48},{48,64},{64,80},{80,96},{96,112},{112,128},... | collective-permute-start | bytes 1179656 | tf_op jit(solution)/shard_map/ppermute | solution.py:153
  101.1 2.3 %collective-permute-start.8 = (bf16[64,3072]{1,0:T(8,128)(2,1)S(1)}, bf16[64,3072]{1,0:T(8,128)(2,1)S(1)}, u32[]{:S(2)}, u32[]{:S(2)}) collective-permute-start(bf16[64,3072]{1,0:T(8,128)(2,1)S(1)} %collective-permute-done.7.refs_3_), channel_id=1, source_target_pairs={{0,16},{16,32},{32,48},{48,64},{64,80},{80,96},{96,112},{112,128},... | collective-permute-start | bytes 1179656 | tf_op jit(solution)/shard_map/ppermute | solution.py:153
  103.5 4.5 %collective-permute-done.14 = bf16[64,3072]{1,0:T(8,128)(2,1)S(1)} collective-permute-done((bf16[64,3072]{1,0:T(8,128)(2,1)S(1)}, bf16[64,3072]{1,0:T(8,128)(2,1)S(1)}, u32[]{:S(2)}, u32[]{:S(2)}) %collective-permute-start.14) | collective-permute-done | bytes 393248 | tf_op jit(solution)/shard_map/ppermute | solution.py:153
  108.0 4.1 %all_gather.11.refs_2_ = bf16[128,3072]{1,0:T(8,128)(2,1)S(1)} all-gather(bf16[64,3072]{1,0:T(8,128)(2,1)S(1)} %collective-permute-done.14), channel_id=1, replica_groups=mesh['short'=4,'ring'=12,'core'=2,'col_0'=4,'col_1'=2] {'core'}, dimensions={0}, use_global_device_ids=true | all-gather | bytes 1179648 | tf_op jit(solution)/shard_map/all_gather | solution.py:187
  112.2 4.1 %all_gather.10.refs_1_ = bf16[128,3072]{1,0:T(8,128)(2,1)S(1)} all-gather(bf16[64,3072]{1,0:T(8,128)(2,1)S(1)} %collective-permute-done.8), channel_id=1, replica_groups=mesh['short'=4,'ring'=12,'core'=2,'col_0'=4,'col_1'=2] {'core'}, dimensions={0}, use_global_device_ids=true | all-gather | bytes 1179648 | tf_op jit(solution)/shard_map/all_gather | solution.py:186
  116.3 4.3 %shard_map.121 = f32[256,3072]{1,0:T(8,128)} custom-call(s32[4]{0:T(128)S(1)} %fusion.9.at, bf16[1536,256]{1,0:T(8,128)(2,1)S(1)} %shard_map.118.refs_0_, bf16[128,3072]{1,0:T(8,128)(2,1)S(1)} %all_gather.10.refs_1_, bf16[128,3072]{1,0:T(8,128)(2,1)S(1)} %all_gather.11.refs_2_, f32[256,3072]{1,0:T(8,128)S(1)} %get-tuple-element.11.refs_3_, ...), custom_call_target="tpu_custom_call" | custom-call | flops 402653184 | bytes 11010048 | tf_op jit(solution)/shard_map/pallas_call | solution.py:125
  (37 shorter events, 4.2 us)
Async XLA Ops:
  12.7 27.6 %collective-permute-start.3 = (bf16[64,3072]{1,0:T(8,128)(2,1)S(1)}, bf16[64,3072]{1,0:T(8,128)(2,1)S(1)}, u32[]{:S(2)}, u32[]{:S(2)}) collective-permute-start(bf16[64,3072]{1,0:T(8,128)(2,1)S(1)} %all_gather.9.refs_2_), channel_id=1, source_target_pairs={{0,8},{8,0},{1,9},{9,1},{2,10},{10,2},{3,11},{11,3},{4,12},{12,4},... | collective-permute-start | bytes 1179656 | tf_op jit(solution)/shard_map/ppermute | solution.py:157
  26.9 15.6 %collective-permute-start.9 = (bf16[64,3072]{1,0:T(8,128)(2,1)S(1)}, bf16[64,3072]{1,0:T(8,128)(2,1)S(1)}, u32[]{:S(2)}, u32[]{:S(2)}) collective-permute-start(bf16[64,3072]{1,0:T(8,128)(2,1)S(1)} %all_gather.9.refs_2_), channel_id=1, source_target_pairs={{0,16},{16,32},{32,48},{48,64},{64,80},{80,96},{96,112},{112,128},... | collective-permute-start | bytes 1179656 | tf_op jit(solution)/shard_map/ppermute | solution.py:153
  32.7 12.0 %collective-permute-start = (bf16[192,256]{1,0:T(8,128)(2,1)}, bf16[192,256]{1,0:T(8,128)(2,1)S(1)}, u32[]{:S(2)}, u32[]{:S(2)}) collective-permute-start(bf16[192,256]{1,0:T(8,128)(2,1)} %param.12), channel_id=1, source_target_pairs={{0,1},{1,0},{2,3},{3,2},{4,5},{5,4},{6,7},{7,6},{8,9},{9,8},{10,11... | collective-permute-start | bytes 294920 | tf_op jit(solution)/shard_map/ppermute | solution.py:155
  40.3 8.8 %collective-permute-start.4 = (bf16[64,3072]{1,0:T(8,128)(2,1)S(1)}, bf16[64,3072]{1,0:T(8,128)(2,1)S(1)}, u32[]{:S(2)}, u32[]{:S(2)}) collective-permute-start(bf16[64,3072]{1,0:T(8,128)(2,1)S(1)} %collective-permute-done.3), channel_id=1, source_target_pairs={{0,16},{16,32},{32,48},{48,64},{64,80},{80,96},{96,112},{112,128},... | collective-permute-start | bytes 1179656 | tf_op jit(solution)/shard_map/ppermute | solution.py:153
  42.5 10.5 %collective-permute-start.10 = (bf16[64,3072]{1,0:T(8,128)(2,1)S(1)}, bf16[64,3072]{1,0:T(8,128)(2,1)S(1)}, u32[]{:S(2)}, u32[]{:S(2)}) collective-permute-start(bf16[64,3072]{1,0:T(8,128)(2,1)S(1)} %collective-permute-done.9.refs_3_), channel_id=1, source_target_pairs={{0,16},{16,32},{32,48},{48,64},{64,80},{80,96},{96,112},{112,128},... | collective-permute-start | bytes 1179656 | tf_op jit(solution)/shard_map/ppermute | solution.py:153
  45.6 10.8 %collective-permute-start.1 = (bf16[2,192,256]{2,1,0:T(8,128)(2,1)S(1)}, bf16[2,192,256]{2,1,0:T(8,128)(2,1)S(1)}, u32[]{:S(2)}, u32[]{:S(2)}) collective-permute-start(bf16[2,192,256]{2,1,0:T(8,128)(2,1)S(1)} %pad_maximum_fusion.1.refs_0_), channel_id=1, source_target_pairs={{0,2},{2,0},{4,6},{6,4},{1,3},{3,1},{5,7},{7,5},{8,10},{10,8},{12,... | collective-permute-start | bytes 589832 | tf_op jit(solution)/shard_map/ppermute | solution.py:160
  49.1 15.2 %collective-permute-start.5 = (bf16[64,3072]{1,0:T(8,128)(2,1)S(1)}, bf16[64,3072]{1,0:T(8,128)(2,1)}, u32[]{:S(2)}, u32[]{:S(2)}) collective-permute-start(bf16[64,3072]{1,0:T(8,128)(2,1)S(1)} %collective-permute-done.4.refs_6_), channel_id=1, source_target_pairs={{0,16},{16,32},{32,48},{48,64},{64,80},{80,96},{96,112},{112,128},... | collective-permute-start | bytes 1179656 | tf_op jit(solution)/shard_map/ppermute | solution.py:153
  53.1 13.2 %collective-permute-start.11 = (bf16[64,3072]{1,0:T(8,128)(2,1)S(1)}, bf16[64,3072]{1,0:T(8,128)(2,1)}, u32[]{:S(2)}, u32[]{:S(2)}) collective-permute-start(bf16[64,3072]{1,0:T(8,128)(2,1)S(1)} %collective-permute-done.10.refs_4_), channel_id=1, source_target_pairs={{0,16},{16,32},{32,48},{48,64},{64,80},{80,96},{96,112},{112,128},... | collective-permute-start | bytes 1179656 | tf_op jit(solution)/shard_map/ppermute | solution.py:153
  57.4 13.1 %collective-permute-start.2 = (bf16[4,192,256]{2,1,0:T(8,128)(2,1)S(1)}, bf16[4,192,256]{2,1,0:T(8,128)(2,1)S(1)}, u32[]{:S(2)}, u32[]{:S(2)}) collective-permute-start(bf16[4,192,256]{2,1,0:T(8,128)(2,1)S(1)} %pad_maximum_fusion), channel_id=1, source_target_pairs={{0,6},{2,4},{4,2},{6,0},{1,7},{3,5},{5,3},{7,1},{8,14},{10,12},{12... | collective-permute-start | bytes 1179656 | tf_op jit(solution)/shard_map/ppermute | solution.py:161
  62.8 20.9 %copy-start.6 = (s32[7]{0:T(128)S(1)}, s32[7]{0:T(128)}, u32[]{:S(2)}) copy-start(s32[7]{0:T(128)} %constant.81.clone) | copy-start | bytes 88
  62.8 21.6 %copy-start.3 = (s32[3]{0:T(128)S(1)}, s32[3]{0:T(128)}, u32[]{:S(2)}) copy-start(s32[3]{0:T(128)} %constant.83.clone) | copy-start | bytes 40
  62.8 21.6 %copy-start.4 = (s32[3]{0:T(128)S(1)}, s32[3]{0:T(128)}, u32[]{:S(2)}) copy-start(s32[3]{0:T(128)} %constant.84.clone) | copy-start | bytes 40
  62.8 21.6 %copy-start.5 = (s32[3]{0:T(128)S(1)}, s32[3]{0:T(128)}, u32[]{:S(2)}) copy-start(s32[3]{0:T(128)} %constant.93) | copy-start | bytes 40
  64.4 17.4 %collective-permute-start.6 = (bf16[64,3072]{1,0:T(8,128)(2,1)}, bf16[64,3072]{1,0:T(8,128)(2,1)}, u32[]{:S(2)}, u32[]{:S(2)}) collective-permute-start(bf16[64,3072]{1,0:T(8,128)(2,1)} %collective-permute-done.5.refs_7_), channel_id=1, source_target_pairs={{0,16},{16,32},{32,48},{48,64},{64,80},{80,96},{96,112},{112,128},... | collective-permute-start | bytes 1179656 | tf_op jit(solution)/shard_map/ppermute | solution.py:153
  66.3 12.0 %collective-permute-start.12 = (bf16[64,3072]{1,0:T(8,128)(2,1)}, bf16[64,3072]{1,0:T(8,128)(2,1)S(1)}, u32[]{:S(2)}, u32[]{:S(2)}) collective-permute-start(bf16[64,3072]{1,0:T(8,128)(2,1)} %collective-permute-done.11.refs_5_), channel_id=1, source_target_pairs={{0,16},{16,32},{32,48},{48,64},{64,80},{80,96},{96,112},{112,128},... | collective-permute-start | bytes 1179656 | tf_op jit(solution)/shard_map/ppermute | solution.py:153
  70.5 0.7 copy-start
  71.2 1.0 copy-start.1
  72.2 0.7 copy-start.2
  76.3 8.1 %collective-permute-start.15 = (bf16[1536,256]{1,0:T(8,128)(2,1)S(1)}, bf16[1536,256]{1,0:T(8,128)(2,1)S(1)}, u32[]{:S(2)}, u32[]{:S(2)}) collective-permute-start(bf16[1536,256]{1,0:T(8,128)(2,1)S(1)} %shard_map.118.refs_0_), channel_id=1, source_target_pairs={{0,8},{8,0},{1,9},{9,1},{2,10},{10,2},{3,11},{11,3},{4,12},{12,4},... | collective-permute-start | bytes 2359304 | tf_op jit(solution)/shard_map/ppermute | solution.py:171
  78.3 11.4 %collective-permute-start.13 = (bf16[64,3072]{1,0:T(8,128)(2,1)S(1)}, bf16[64,3072]{1,0:T(8,128)(2,1)S(1)}, u32[]{:S(2)}, u32[]{:S(2)}) collective-permute-start(bf16[64,3072]{1,0:T(8,128)(2,1)S(1)} %collective-permute-done.12.refs_2_), channel_id=1, source_target_pairs={{0,16},{16,32},{32,48},{48,64},{64,80},{80,96},{96,112},{112,128},... | collective-permute-start | bytes 1179656 | tf_op jit(solution)/shard_map/ppermute | solution.py:153
  81.8 9.5 %collective-permute-start.7 = (bf16[64,3072]{1,0:T(8,128)(2,1)}, bf16[64,3072]{1,0:T(8,128)(2,1)S(1)}, u32[]{:S(2)}, u32[]{:S(2)}) collective-permute-start(bf16[64,3072]{1,0:T(8,128)(2,1)} %collective-permute-done.6.refs_8_), channel_id=1, source_target_pairs={{0,16},{16,32},{32,48},{48,64},{64,80},{80,96},{96,112},{112,128},... | collective-permute-start | bytes 1179656 | tf_op jit(solution)/shard_map/ppermute | solution.py:153
  91.3 12.2 %copy-start.7 = (s32[4]{0:T(128)S(1)}, s32[4]{0:T(128)}, u32[]{:S(2)}) copy-start(s32[4]{0:T(128)} %constant.85.clone) | copy-start | bytes 52
  91.3 12.2 %copy-start.8 = (s32[4]{0:T(128)S(1)}, s32[4]{0:T(128)}, u32[]{:S(2)}) copy-start(s32[4]{0:T(128)} %constant.86.clone) | copy-start | bytes 52
  94.7 21.6 %collective-permute-start.16 = (f32[256,3072]{1,0:T(8,128)S(1)}, f32[256,3072]{1,0:T(8,128)S(1)}, u32[]{:S(2)}, u32[]{:S(2)}) collective-permute-start(f32[256,3072]{1,0:T(8,128)S(1)} %get-tuple-element.12), channel_id=1, source_target_pairs={{0,8},{8,0},{1,9},{9,1},{2,10},{10,2},{3,11},{11,3},{4,12},{12,4},... | collective-permute-start | bytes 9437192 | tf_op jit(solution)/shard_map/ppermute | solution.py:185
  99.2 8.8 %collective-permute-start.14 = (bf16[64,3072]{1,0:T(8,128)(2,1)S(1)}, bf16[64,3072]{1,0:T(8,128)(2,1)S(1)}, u32[]{:S(2)}, u32[]{:S(2)}) collective-permute-start(bf16[64,3072]{1,0:T(8,128)(2,1)S(1)} %collective-permute-done.13.refs_4_), channel_id=1, source_target_pairs={{0,16},{16,32},{32,48},{48,64},{64,80},{80,96},{96,112},{112,128},... | collective-permute-start | bytes 1179656 | tf_op jit(solution)/shard_map/ppermute | solution.py:153
  101.1 11.1 %collective-permute-start.8 = (bf16[64,3072]{1,0:T(8,128)(2,1)S(1)}, bf16[64,3072]{1,0:T(8,128)(2,1)S(1)}, u32[]{:S(2)}, u32[]{:S(2)}) collective-permute-start(bf16[64,3072]{1,0:T(8,128)(2,1)S(1)} %collective-permute-done.7.refs_3_), channel_id=1, source_target_pairs={{0,16},{16,32},{32,48},{48,64},{64,80},{80,96},{96,112},{112,128},... | collective-permute-start | bytes 1179656 | tf_op jit(solution)/shard_map/ppermute | solution.py:153

commit v4 on v3

--- a/solution.py
+++ b/solution.py
@@ -84,7 +84,7 @@
         in_specs=[SMEM, SMEM] + [VMEM] * (3 + len(stacks)),
         out_specs=VMEM,
         scratch_shapes=[pltpu.VMEM((rows + EDGE, width), jnp.bfloat16)] * 4,
-        compiler_params=pltpu.CompilerParams(vmem_limit_bytes=16 << 20),
+        compiler_params=pltpu.CompilerParams(vmem_limit_bytes=12 << 20),
         cost_estimate=pl.CostEstimate(
             flops=18 * rows * (BLOCK + EDGE) * width,
             bytes_accessed=4 * rows * width,
@@ -132,7 +132,7 @@
         + [spec] * len(priors),
         out_specs=[spec] * sides,
         scratch_shapes=[pltpu.VMEM((sides, width, depth), jnp.bfloat16)],
-        compiler_params=pltpu.CompilerParams(vmem_limit_bytes=16 << 20),
+        compiler_params=pltpu.CompilerParams(vmem_limit_bytes=14 << 20),
         cost_estimate=pl.CostEstimate(
             flops=2 * sides * width * depth * columns,
             bytes_accessed=2 * depth * columns + 4 * (sides + len(priors)) * width * columns,
@@ -178,7 +178,7 @@
 
     def near(blocks, priors):
         tv = [(mine, theirs)[part][steps] for part, steps in blocks]
-        return product(chosen(blocks), lefts, tv, priors, 512)
+        return product(chosen(blocks), lefts, tv, priors, 1024)
 
     sums = near([(0, d) for d in range(4)] + [(1, d) for d in range(1, 4)], ())
     sums = near([(0, 4), (1, 4), (0, 5)], sums)
@@ -187,7 +187,7 @@
     far.append(lax.all_gather(mine[half], "core", axis=0, tiled=True))
     steps = jnp.array([1 - half, half - 1, -half, half], jnp.int32)
     at = (ring + turns + steps) % turns * 2 + jnp.array([1, 0, 0, 1], jnp.int32)
-    return product(at, lefts[:1], far, (sums[0], handed), 512)[0]
+    return product(at, lefts[:1], far, (sums[0], handed), 1024)[0]
 
 
 def solution(mesh):

time: 122 us -> 119 us (0.975)
  Pallas kernels: 16.4 us -> 13.7 us
  waiting for transfers between devices: 9.73 us -> 11.9 us
  local copies, waits for them, and re-layouts: 4.24 us -> 2.5 us
    pallas_call x3, Pallas kernels: 12.9 us -> 10.3 us  [product(): pl.pallas_call(functools.partial(accumulate, len(blocks), sides, len(prio...]
    ppermute x11, waiting for transfers between devices: 7.48 us -> 9.7 us  [hop(): return lax.ppermute(block, ('ring', 'core'), onward)]
    unnamed x18 -> x14, local copies, waits for them, and re-layouts: 2.43 us -> 0.69 us
  transfers between devices with their start and end apart: 17 -> 17, of which waited for: 6 -> 7; matrix products, arithmetic and copies ran while one was open for 4% -> 4% of each run, Pallas kernels for 7% -> 6%
where the time goes in v4:
time: 119 us; the launch traced here: 118 us
  starting transfers between devices  65.9 us (55%)
  blocking collectives  20.8 us (17%)
  Pallas kernels  13.7 us (12%)
  waiting for transfers between devices  11.9 us (10%)
  other arithmetic  3.25 us (3%)
  local copies, waits for them, and re-layouts  2.5 us (2%)
    ppermute x11, starting transfers between devices, hop(): return lax.ppermute(block, ('ring', 'core'), onward)  30.1 us
    ppermute x1, starting transfers between devices, block_of(): theirs = [lax.ppermute(mine[0], 'core', swap)]  14.2 us
    all_gather x1, blocking collectives, block_of(): mine = [lax.all_gather(tv_design, 'short', axis=0, tiled=True)]  12.7 us
    pallas_call x3, Pallas kernels, product(): pl.pallas_call(functools.partial(accumulate, len(blocks), sides, len(prio...  10.3 us
    ppermute x11, waiting for transfers between devices, hop(): return lax.ppermute(block, ('ring', 'core'), onward)  9.7 us
    ppermute x1, starting transfers between devices, block_of(): other = lax.ppermute(static_design, 'col_1', swap)  7.61 us
    ppermute x1, starting transfers between devices, block_of(): handed = lax.ppermute(sums[1], 'core', swap)  4.57 us
    ppermute x1, starting transfers between devices, block_of(): lax.ppermute(jnp.concatenate([pair, beside]), 'col_0', [(i, 3 - i) for i...  4.39 us
  transfers between devices with their start and end apart: 17, of which 7 were waited for; matrix products, arithmetic and copies ran while one was open for 4% of the time, Pallas kernels for 6%

profile of v4, /device:TPU:1, one launch (start us, length us, event | category | flops | bytes accessed | tf_op | source)
XLA Modules:
  0.0 118.5 jit_solution(10859906625609382395)
XLA Ops:
  0.0 12.7 %all_gather.9.refs_2_ = bf16[64,3072]{1,0:T(8,128)(2,1)S(1)} all-gather(bf16[16,3072]{1,0:T(8,128)(2,1)} %param.13), channel_id=1, replica_groups=mesh['short'=4,'ring'=12,'core'=2,'col_0'=4,'col_1'=2] {'short'}, dimensions={0}, use_global_device_ids=true | all-gather | bytes 491520 | tf_op jit(solution)/shard_map/all_gather | solution.py:156
  12.7 14.2 %collective-permute-start.3 = (bf16[64,3072]{1,0:T(8,128)(2,1)S(1)}, bf16[64,3072]{1,0:T(8,128)(2,1)S(1)}, u32[]{:S(2)}, u32[]{:S(2)}) collective-permute-start(bf16[64,3072]{1,0:T(8,128)(2,1)S(1)} %all_gather.9.refs_2_), channel_id=1, source_target_pairs={{0,8},{8,0},{1,9},{9,1},{2,10},{10,2},{3,11},{11,3},{4,12},{12,4},... | collective-permute-start | bytes 1179656 | tf_op jit(solution)/shard_map/ppermute | solution.py:157
  26.9 5.8 %collective-permute-start.9 = (bf16[64,3072]{1,0:T(8,128)(2,1)S(1)}, bf16[64,3072]{1,0:T(8,128)(2,1)S(1)}, u32[]{:S(2)}, u32[]{:S(2)}) collective-permute-start(bf16[64,3072]{1,0:T(8,128)(2,1)S(1)} %all_gather.9.refs_2_), channel_id=1, source_target_pairs={{0,16},{16,32},{32,48},{48,64},{64,80},{80,96},{96,112},{112,128},... | collective-permute-start | bytes 1179656 | tf_op jit(solution)/shard_map/ppermute | solution.py:153
  32.7 7.6 %collective-permute-start = (bf16[192,256]{1,0:T(8,128)(2,1)}, bf16[192,256]{1,0:T(8,128)(2,1)S(1)}, u32[]{:S(2)}, u32[]{:S(2)}) collective-permute-start(bf16[192,256]{1,0:T(8,128)(2,1)} %param.12), channel_id=1, source_target_pairs={{0,1},{1,0},{2,3},{3,2},{4,5},{5,4},{6,7},{7,6},{8,9},{9,8},{10,11... | collective-permute-start | bytes 294920 | tf_op jit(solution)/shard_map/ppermute | solution.py:155
  40.3 2.2 %collective-permute-start.4 = (bf16[64,3072]{1,0:T(8,128)(2,1)S(1)}, bf16[64,3072]{1,0:T(8,128)(2,1)S(1)}, u32[]{:S(2)}, u32[]{:S(2)}) collective-permute-start(bf16[64,3072]{1,0:T(8,128)(2,1)S(1)} %collective-permute-done.3), channel_id=1, source_target_pairs={{0,16},{16,32},{32,48},{48,64},{64,80},{80,96},{96,112},{112,128},... | collective-permute-start | bytes 1179656 | tf_op jit(solution)/shard_map/ppermute | solution.py:153
  42.5 2.2 %collective-permute-start.10 = (bf16[64,3072]{1,0:T(8,128)(2,1)S(1)}, bf16[64,3072]{1,0:T(8,128)(2,1)S(1)}, u32[]{:S(2)}, u32[]{:S(2)}) collective-permute-start(bf16[64,3072]{1,0:T(8,128)(2,1)S(1)} %collective-permute-done.9.refs_3_), channel_id=1, source_target_pairs={{0,16},{16,32},{32,48},{48,64},{64,80},{80,96},{96,112},{112,128},... | collective-permute-start | bytes 1179656 | tf_op jit(solution)/shard_map/ppermute | solution.py:153
  44.7 0.9 pad_maximum_fusion.1.refs_0_
  45.6 3.1 %collective-permute-start.1 = (bf16[2,192,256]{2,1,0:T(8,128)(2,1)S(1)}, bf16[2,192,256]{2,1,0:T(8,128)(2,1)S(1)}, u32[]{:S(2)}, u32[]{:S(2)}) collective-permute-start(bf16[2,192,256]{2,1,0:T(8,128)(2,1)S(1)} %pad_maximum_fusion.1.refs_0_), channel_id=1, source_target_pairs={{0,2},{2,0},{4,6},{6,4},{1,3},{3,1},{5,7},{7,5},{8,10},{10,8},{12,... | collective-permute-start | bytes 589832 | tf_op jit(solution)/shard_map/ppermute | solution.py:160
  49.1 3.1 %collective-permute-start.5 = (bf16[64,3072]{1,0:T(8,128)(2,1)S(1)}, bf16[64,3072]{1,0:T(8,128)(2,1)}, u32[]{:S(2)}, u32[]{:S(2)}) collective-permute-start(bf16[64,3072]{1,0:T(8,128)(2,1)S(1)} %collective-permute-done.4.refs_6_), channel_id=1, source_target_pairs={{0,16},{16,32},{32,48},{48,64},{64,80},{80,96},{96,112},{112,128},... | collective-permute-start | bytes 1179656 | tf_op jit(solution)/shard_map/ppermute | solution.py:153
  53.1 3.4 %collective-permute-start.11 = (bf16[64,3072]{1,0:T(8,128)(2,1)S(1)}, bf16[64,3072]{1,0:T(8,128)(2,1)}, u32[]{:S(2)}, u32[]{:S(2)}) collective-permute-start(bf16[64,3072]{1,0:T(8,128)(2,1)S(1)} %collective-permute-done.10.refs_4_), channel_id=1, source_target_pairs={{0,16},{16,32},{32,48},{48,64},{64,80},{80,96},{96,112},{112,128},... | collective-permute-start | bytes 1179656 | tf_op jit(solution)/shard_map/ppermute | solution.py:153
  56.5 0.9 pad_maximum_fusion
  57.4 4.4 %collective-permute-start.2 = (bf16[4,192,256]{2,1,0:T(8,128)(2,1)S(1)}, bf16[4,192,256]{2,1,0:T(8,128)(2,1)S(1)}, u32[]{:S(2)}, u32[]{:S(2)}) collective-permute-start(bf16[4,192,256]{2,1,0:T(8,128)(2,1)S(1)} %pad_maximum_fusion), channel_id=1, source_target_pairs={{0,6},{2,4},{4,2},{6,0},{1,7},{3,5},{5,3},{7,1},{8,14},{10,12},{12... | collective-permute-start | bytes 1179656 | tf_op jit(solution)/shard_map/ppermute | solution.py:161
  61.8 1.0 broadcast_in_dim.12.arc_rows
  62.8 0.8 fusion.12
  64.4 1.9 %collective-permute-start.6 = (bf16[64,3072]{1,0:T(8,128)(2,1)}, bf16[64,3072]{1,0:T(8,128)(2,1)}, u32[]{:S(2)}, u32[]{:S(2)}) collective-permute-start(bf16[64,3072]{1,0:T(8,128)(2,1)} %collective-permute-done.5.refs_7_), channel_id=1, source_target_pairs={{0,16},{16,32},{32,48},{48,64},{64,80},{80,96},{96,112},{112,128},... | collective-permute-start | bytes 1179656 | tf_op jit(solution)/shard_map/ppermute | solution.py:153
  66.3 1.9 %collective-permute-start.12 = (bf16[64,3072]{1,0:T(8,128)(2,1)}, bf16[64,3072]{1,0:T(8,128)(2,1)S(1)}, u32[]{:S(2)}, u32[]{:S(2)}) collective-permute-start(bf16[64,3072]{1,0:T(8,128)(2,1)} %collective-permute-done.11.refs_5_), channel_id=1, source_target_pairs={{0,16},{16,32},{32,48},{48,64},{64,80},{80,96},{96,112},{112,128},... | collective-permute-start | bytes 1179656 | tf_op jit(solution)/shard_map/ppermute | solution.py:153
  68.2 2.2 %collective-permute-done.2.refs_2_ = bf16[4,192,256]{2,1,0:T(8,128)(2,1)S(1)} collective-permute-done((bf16[4,192,256]{2,1,0:T(8,128)(2,1)S(1)}, bf16[4,192,256]{2,1,0:T(8,128)(2,1)S(1)}, u32[]{:S(2)}, u32[]{:S(2)}) %collective-permute-start.2) | collective-permute-done | bytes 393248 | tf_op jit(solution)/shard_map/ppermute | solution.py:161
  71.1 3.5 %shard_map.118.refs_0_ = bf16[1536,256]{1,0:T(8,128)(2,1)S(1)} custom-call(s32[8]{0:T(128)S(1)} %xor_add_fusion.places, f32[32]{0:T(128)S(1)} %copy-done, s32[1536,1]{1,0:T(8,128)S(1)} %broadcast_in_dim.12.arc_rows, s32[1,1664]{1,0:T(1,128)S(1)} %broadcast_in_dim.10.arc_ahead, s32[1,1664]{1,0:T(1,128)S(1)} %broadcast_in_dim.11.arc_behind, ...), custom_call_target="tpu_custom_call" | custom-call | flops 1585446912 | bytes 1572864 | tf_op jit(solution)/shard_map/pallas_call | solution.py:81
  74.6 1.9 %collective-permute-start.15 = (bf16[1536,256]{1,0:T(8,128)(2,1)S(1)}, bf16[1536,256]{1,0:T(8,128)(2,1)S(1)}, u32[]{:S(2)}, u32[]{:S(2)}) collective-permute-start(bf16[1536,256]{1,0:T(8,128)(2,1)S(1)} %shard_map.118.refs_0_), channel_id=1, source_target_pairs={{0,8},{8,0},{1,9},{9,1},{2,10},{10,2},{3,11},{11,3},{4,12},{12,4},... | collective-permute-start | bytes 2359304 | tf_op jit(solution)/shard_map/ppermute | solution.py:171
  76.5 1.1 collective-permute-done.12.refs_2_
  77.6 2.8 %collective-permute-start.13 = (bf16[64,3072]{1,0:T(8,128)(2,1)S(1)}, bf16[64,3072]{1,0:T(8,128)(2,1)S(1)}, u32[]{:S(2)}, u32[]{:S(2)}) collective-permute-start(bf16[64,3072]{1,0:T(8,128)(2,1)S(1)} %collective-permute-done.12.refs_2_), channel_id=1, source_target_pairs={{0,16},{16,32},{32,48},{48,64},{64,80},{80,96},{96,112},{112,128},... | collective-permute-start | bytes 1179656 | tf_op jit(solution)/shard_map/ppermute | solution.py:153
  80.4 1.9 %collective-permute-start.7 = (bf16[64,3072]{1,0:T(8,128)(2,1)}, bf16[64,3072]{1,0:T(8,128)(2,1)S(1)}, u32[]{:S(2)}, u32[]{:S(2)}) collective-permute-start(bf16[64,3072]{1,0:T(8,128)(2,1)} %collective-permute-done.6.refs_8_), channel_id=1, source_target_pairs={{0,16},{16,32},{32,48},{48,64},{64,80},{80,96},{96,112},{112,128},... | collective-permute-start | bytes 1179656 | tf_op jit(solution)/shard_map/ppermute | solution.py:153
  83.1 4.1 %shard_map.119 = (f32[256,3072]{1,0:T(8,128)S(1)}, f32[256,3072]{1,0:T(8,128)S(1)}) custom-call(s32[7]{0:T(128)S(1)} %fusion.1.at, bf16[1536,256]{1,0:T(8,128)(2,1)S(1)} %shard_map.118.refs_0_, bf16[1536,256]{1,0:T(8,128)(2,1)S(1)} %collective-permute-done.15.refs_1_, bf16[64,3072]{1,0:T(8,128)(2,1)S(1)} %all_gather.9.refs_2_, ...), custom_call_target="tpu_custom_call" | custom-call | flops 1409286144 | bytes 9043968 | tf_op jit(solution)/shard_map/pallas_call | solution.py:125
  87.2 3.4 %collective-permute-done.7.refs_3_ = bf16[64,3072]{1,0:T(8,128)(2,1)S(1)} collective-permute-done((bf16[64,3072]{1,0:T(8,128)(2,1)}, bf16[64,3072]{1,0:T(8,128)(2,1)S(1)}, u32[]{:S(2)}, u32[]{:S(2)}) %collective-permute-start.7) | collective-permute-done | bytes 393248 | tf_op jit(solution)/shard_map/ppermute | solution.py:153
  90.6 2.8 %shard_map.120 = (f32[256,3072]{1,0:T(8,128)S(1)}, f32[256,3072]{1,0:T(8,128)S(1)}) custom-call(s32[3]{0:T(128)S(1)} %fusion.at, bf16[1536,256]{1,0:T(8,128)(2,1)S(1)} %shard_map.118.refs_0_, bf16[1536,256]{1,0:T(8,128)(2,1)S(1)} %collective-permute-done.15.refs_1_, bf16[64,3072]{1,0:T(8,128)(2,1)S(1)} %collective-permute-done.12.refs_2_, ...), custom_call_target="tpu_custom_call" | custom-call | flops 603979776 | bytes 13762560 | tf_op jit(solution)/shard_map/pallas_call | solution.py:125
  93.4 4.6 %collective-permute-start.16 = (f32[256,3072]{1,0:T(8,128)S(1)}, f32[256,3072]{1,0:T(8,128)S(1)}, u32[]{:S(2)}, u32[]{:S(2)}) collective-permute-start(f32[256,3072]{1,0:T(8,128)S(1)} %get-tuple-element.12), channel_id=1, source_target_pairs={{0,8},{8,0},{1,9},{9,1},{2,10},{10,2},{3,11},{11,3},{4,12},{12,4},... | collective-permute-start | bytes 9437192 | tf_op jit(solution)/shard_map/ppermute | solution.py:185
  98.0 2.4 %collective-permute-start.14 = (bf16[64,3072]{1,0:T(8,128)(2,1)S(1)}, bf16[64,3072]{1,0:T(8,128)(2,1)S(1)}, u32[]{:S(2)}, u32[]{:S(2)}) collective-permute-start(bf16[64,3072]{1,0:T(8,128)(2,1)S(1)} %collective-permute-done.13.refs_4_), channel_id=1, source_target_pairs={{0,16},{16,32},{32,48},{48,64},{64,80},{80,96},{96,112},{112,128},... | collective-permute-start | bytes 1179656 | tf_op jit(solution)/shard_map/ppermute | solution.py:153
  100.4 2.4 %collective-permute-start.8 = (bf16[64,3072]{1,0:T(8,128)(2,1)S(1)}, bf16[64,3072]{1,0:T(8,128)(2,1)S(1)}, u32[]{:S(2)}, u32[]{:S(2)}) collective-permute-start(bf16[64,3072]{1,0:T(8,128)(2,1)S(1)} %collective-permute-done.7.refs_3_), channel_id=1, source_target_pairs={{0,16},{16,32},{32,48},{48,64},{64,80},{80,96},{96,112},{112,128},... | collective-permute-start | bytes 1179656 | tf_op jit(solution)/shard_map/ppermute | solution.py:153
  102.9 3.9 %collective-permute-done.14 = bf16[64,3072]{1,0:T(8,128)(2,1)S(1)} collective-permute-done((bf16[64,3072]{1,0:T(8,128)(2,1)S(1)}, bf16[64,3072]{1,0:T(8,128)(2,1)S(1)}, u32[]{:S(2)}, u32[]{:S(2)}) %collective-permute-start.14) | collective-permute-done | bytes 393248 | tf_op jit(solution)/shard_map/ppermute | solution.py:153
  106.8 4.1 %all_gather.11.refs_2_ = bf16[128,3072]{1,0:T(8,128)(2,1)S(1)} all-gather(bf16[64,3072]{1,0:T(8,128)(2,1)S(1)} %collective-permute-done.14), channel_id=1, replica_groups=mesh['short'=4,'ring'=12,'core'=2,'col_0'=4,'col_1'=2] {'core'}, dimensions={0}, use_global_device_ids=true | all-gather | bytes 1179648 | tf_op jit(solution)/shard_map/all_gather | solution.py:187
  111.0 4.1 %all_gather.10.refs_1_ = bf16[128,3072]{1,0:T(8,128)(2,1)S(1)} all-gather(bf16[64,3072]{1,0:T(8,128)(2,1)S(1)} %collective-permute-done.8), channel_id=1, replica_groups=mesh['short'=4,'ring'=12,'core'=2,'col_0'=4,'col_1'=2] {'core'}, dimensions={0}, use_global_device_ids=true | all-gather | bytes 1179648 | tf_op jit(solution)/shard_map/all_gather | solution.py:186
  115.1 3.4 %shard_map.121 = f32[256,3072]{1,0:T(8,128)} custom-call(s32[4]{0:T(128)S(1)} %fusion.9.at, bf16[1536,256]{1,0:T(8,128)(2,1)S(1)} %shard_map.118.refs_0_, bf16[128,3072]{1,0:T(8,128)(2,1)S(1)} %all_gather.10.refs_1_, bf16[128,3072]{1,0:T(8,128)(2,1)S(1)} %all_gather.11.refs_2_, f32[256,3072]{1,0:T(8,128)S(1)} %get-tuple-element.11.refs_3_, ...), custom_call_target="tpu_custom_call" | custom-call | flops 402653184 | bytes 11010048 | tf_op jit(solution)/shard_map/pallas_call | solution.py:125
  (33 shorter events, 3.5 us)
Async XLA Ops:
  12.7 27.6 %collective-permute-start.3 = (bf16[64,3072]{1,0:T(8,128)(2,1)S(1)}, bf16[64,3072]{1,0:T(8,128)(2,1)S(1)}, u32[]{:S(2)}, u32[]{:S(2)}) collective-permute-start(bf16[64,3072]{1,0:T(8,128)(2,1)S(1)} %all_gather.9.refs_2_), channel_id=1, source_target_pairs={{0,8},{8,0},{1,9},{9,1},{2,10},{10,2},{3,11},{11,3},{4,12},{12,4},... | collective-permute-start | bytes 1179656 | tf_op jit(solution)/shard_map/ppermute | solution.py:157
  26.9 15.6 %collective-permute-start.9 = (bf16[64,3072]{1,0:T(8,128)(2,1)S(1)}, bf16[64,3072]{1,0:T(8,128)(2,1)S(1)}, u32[]{:S(2)}, u32[]{:S(2)}) collective-permute-start(bf16[64,3072]{1,0:T(8,128)(2,1)S(1)} %all_gather.9.refs_2_), channel_id=1, source_target_pairs={{0,16},{16,32},{32,48},{48,64},{64,80},{80,96},{96,112},{112,128},... | collective-permute-start | bytes 1179656 | tf_op jit(solution)/shard_map/ppermute | solution.py:153
  32.7 12.0 %collective-permute-start = (bf16[192,256]{1,0:T(8,128)(2,1)}, bf16[192,256]{1,0:T(8,128)(2,1)S(1)}, u32[]{:S(2)}, u32[]{:S(2)}) collective-permute-start(bf16[192,256]{1,0:T(8,128)(2,1)} %param.12), channel_id=1, source_target_pairs={{0,1},{1,0},{2,3},{3,2},{4,5},{5,4},{6,7},{7,6},{8,9},{9,8},{10,11... | collective-permute-start | bytes 294920 | tf_op jit(solution)/shard_map/ppermute | solution.py:155
  40.3 8.8 %collective-permute-start.4 = (bf16[64,3072]{1,0:T(8,128)(2,1)S(1)}, bf16[64,3072]{1,0:T(8,128)(2,1)S(1)}, u32[]{:S(2)}, u32[]{:S(2)}) collective-permute-start(bf16[64,3072]{1,0:T(8,128)(2,1)S(1)} %collective-permute-done.3), channel_id=1, source_target_pairs={{0,16},{16,32},{32,48},{48,64},{64,80},{80,96},{96,112},{112,128},... | collective-permute-start | bytes 1179656 | tf_op jit(solution)/shard_map/ppermute | solution.py:153
  42.5 10.5 %collective-permute-start.10 = (bf16[64,3072]{1,0:T(8,128)(2,1)S(1)}, bf16[64,3072]{1,0:T(8,128)(2,1)S(1)}, u32[]{:S(2)}, u32[]{:S(2)}) collective-permute-start(bf16[64,3072]{1,0:T(8,128)(2,1)S(1)} %collective-permute-done.9.refs_3_), channel_id=1, source_target_pairs={{0,16},{16,32},{32,48},{48,64},{64,80},{80,96},{96,112},{112,128},... | collective-permute-start | bytes 1179656 | tf_op jit(solution)/shard_map/ppermute | solution.py:153
  45.6 10.8 %collective-permute-start.1 = (bf16[2,192,256]{2,1,0:T(8,128)(2,1)S(1)}, bf16[2,192,256]{2,1,0:T(8,128)(2,1)S(1)}, u32[]{:S(2)}, u32[]{:S(2)}) collective-permute-start(bf16[2,192,256]{2,1,0:T(8,128)(2,1)S(1)} %pad_maximum_fusion.1.refs_0_), channel_id=1, source_target_pairs={{0,2},{2,0},{4,6},{6,4},{1,3},{3,1},{5,7},{7,5},{8,10},{10,8},{12,... | collective-permute-start | bytes 589832 | tf_op jit(solution)/shard_map/ppermute | solution.py:160
  49.1 15.2 %collective-permute-start.5 = (bf16[64,3072]{1,0:T(8,128)(2,1)S(1)}, bf16[64,3072]{1,0:T(8,128)(2,1)}, u32[]{:S(2)}, u32[]{:S(2)}) collective-permute-start(bf16[64,3072]{1,0:T(8,128)(2,1)S(1)} %collective-permute-done.4.refs_6_), channel_id=1, source_target_pairs={{0,16},{16,32},{32,48},{48,64},{64,80},{80,96},{96,112},{112,128},... | collective-permute-start | bytes 1179656 | tf_op jit(solution)/shard_map/ppermute | solution.py:153
  53.1 13.2 %collective-permute-start.11 = (bf16[64,3072]{1,0:T(8,128)(2,1)S(1)}, bf16[64,3072]{1,0:T(8,128)(2,1)}, u32[]{:S(2)}, u32[]{:S(2)}) collective-permute-start(bf16[64,3072]{1,0:T(8,128)(2,1)S(1)} %collective-permute-done.10.refs_4_), channel_id=1, source_target_pairs={{0,16},{16,32},{32,48},{48,64},{64,80},{80,96},{96,112},{112,128},... | collective-permute-start | bytes 1179656 | tf_op jit(solution)/shard_map/ppermute | solution.py:153
  57.4 13.1 %collective-permute-start.2 = (bf16[4,192,256]{2,1,0:T(8,128)(2,1)S(1)}, bf16[4,192,256]{2,1,0:T(8,128)(2,1)S(1)}, u32[]{:S(2)}, u32[]{:S(2)}) collective-permute-start(bf16[4,192,256]{2,1,0:T(8,128)(2,1)S(1)} %pad_maximum_fusion), channel_id=1, source_target_pairs={{0,6},{2,4},{4,2},{6,0},{1,7},{3,5},{5,3},{7,1},{8,14},{10,12},{12... | collective-permute-start | bytes 1179656 | tf_op jit(solution)/shard_map/ppermute | solution.py:161
  62.8 19.6 %copy-start.4 = (s32[7]{0:T(128)S(1)}, s32[7]{0:T(128)}, u32[]{:S(2)}) copy-start(s32[7]{0:T(128)} %constant.81.clone) | copy-start | bytes 88
  62.8 20.3 %copy-start.1 = (s32[3]{0:T(128)S(1)}, s32[3]{0:T(128)}, u32[]{:S(2)}) copy-start(s32[3]{0:T(128)} %constant.83.clone) | copy-start | bytes 40
  62.8 20.3 %copy-start.2 = (s32[3]{0:T(128)S(1)}, s32[3]{0:T(128)}, u32[]{:S(2)}) copy-start(s32[3]{0:T(128)} %constant.84.clone) | copy-start | bytes 40
  62.8 20.3 %copy-start.3 = (s32[3]{0:T(128)S(1)}, s32[3]{0:T(128)}, u32[]{:S(2)}) copy-start(s32[3]{0:T(128)} %constant.93) | copy-start | bytes 40
  64.4 16.1 %collective-permute-start.6 = (bf16[64,3072]{1,0:T(8,128)(2,1)}, bf16[64,3072]{1,0:T(8,128)(2,1)}, u32[]{:S(2)}, u32[]{:S(2)}) collective-permute-start(bf16[64,3072]{1,0:T(8,128)(2,1)} %collective-permute-done.5.refs_7_), channel_id=1, source_target_pairs={{0,16},{16,32},{32,48},{48,64},{64,80},{80,96},{96,112},{112,128},... | collective-permute-start | bytes 1179656 | tf_op jit(solution)/shard_map/ppermute | solution.py:153
  66.3 11.3 %collective-permute-start.12 = (bf16[64,3072]{1,0:T(8,128)(2,1)}, bf16[64,3072]{1,0:T(8,128)(2,1)S(1)}, u32[]{:S(2)}, u32[]{:S(2)}) collective-permute-start(bf16[64,3072]{1,0:T(8,128)(2,1)} %collective-permute-done.11.refs_5_), channel_id=1, source_target_pairs={{0,16},{16,32},{32,48},{48,64},{64,80},{80,96},{96,112},{112,128},... | collective-permute-start | bytes 1179656 | tf_op jit(solution)/shard_map/ppermute | solution.py:153
  70.5 0.7 copy-start
  74.6 8.5 %collective-permute-start.15 = (bf16[1536,256]{1,0:T(8,128)(2,1)S(1)}, bf16[1536,256]{1,0:T(8,128)(2,1)S(1)}, u32[]{:S(2)}, u32[]{:S(2)}) collective-permute-start(bf16[1536,256]{1,0:T(8,128)(2,1)S(1)} %shard_map.118.refs_0_), channel_id=1, source_target_pairs={{0,8},{8,0},{1,9},{9,1},{2,10},{10,2},{3,11},{11,3},{4,12},{12,4},... | collective-permute-start | bytes 2359304 | tf_op jit(solution)/shard_map/ppermute | solution.py:171
  77.6 9.6 %collective-permute-start.13 = (bf16[64,3072]{1,0:T(8,128)(2,1)S(1)}, bf16[64,3072]{1,0:T(8,128)(2,1)S(1)}, u32[]{:S(2)}, u32[]{:S(2)}) collective-permute-start(bf16[64,3072]{1,0:T(8,128)(2,1)S(1)} %collective-permute-done.12.refs_2_), channel_id=1, source_target_pairs={{0,16},{16,32},{32,48},{48,64},{64,80},{80,96},{96,112},{112,128},... | collective-permute-start | bytes 1179656 | tf_op jit(solution)/shard_map/ppermute | solution.py:153
  80.4 10.2 %collective-permute-start.7 = (bf16[64,3072]{1,0:T(8,128)(2,1)}, bf16[64,3072]{1,0:T(8,128)(2,1)S(1)}, u32[]{:S(2)}, u32[]{:S(2)}) collective-permute-start(bf16[64,3072]{1,0:T(8,128)(2,1)} %collective-permute-done.6.refs_8_), channel_id=1, source_target_pairs={{0,16},{16,32},{32,48},{48,64},{64,80},{80,96},{96,112},{112,128},... | collective-permute-start | bytes 1179656 | tf_op jit(solution)/shard_map/ppermute | solution.py:153
  90.6 12.2 %copy-start.5 = (s32[4]{0:T(128)S(1)}, s32[4]{0:T(128)}, u32[]{:S(2)}) copy-start(s32[4]{0:T(128)} %constant.85.clone) | copy-start | bytes 52
  90.6 12.3 %copy-start.6 = (s32[4]{0:T(128)S(1)}, s32[4]{0:T(128)}, u32[]{:S(2)}) copy-start(s32[4]{0:T(128)} %constant.86.clone) | copy-start | bytes 52
  93.4 21.7 %collective-permute-start.16 = (f32[256,3072]{1,0:T(8,128)S(1)}, f32[256,3072]{1,0:T(8,128)S(1)}, u32[]{:S(2)}, u32[]{:S(2)}) collective-permute-start(f32[256,3072]{1,0:T(8,128)S(1)} %get-tuple-element.12), channel_id=1, source_target_pairs={{0,8},{8,0},{1,9},{9,1},{2,10},{10,2},{3,11},{11,3},{4,12},{12,4},... | collective-permute-start | bytes 9437192 | tf_op jit(solution)/shard_map/ppermute | solution.py:185
  98.0 8.8 %collective-permute-start.14 = (bf16[64,3072]{1,0:T(8,128)(2,1)S(1)}, bf16[64,3072]{1,0:T(8,128)(2,1)S(1)}, u32[]{:S(2)}, u32[]{:S(2)}) collective-permute-start(bf16[64,3072]{1,0:T(8,128)(2,1)S(1)} %collective-permute-done.13.refs_4_), channel_id=1, source_target_pairs={{0,16},{16,32},{32,48},{48,64},{64,80},{80,96},{96,112},{112,128},... | collective-permute-start | bytes 1179656 | tf_op jit(solution)/shard_map/ppermute | solution.py:153
  100.4 10.6 %collective-permute-start.8 = (bf16[64,3072]{1,0:T(8,128)(2,1)S(1)}, bf16[64,3072]{1,0:T(8,128)(2,1)S(1)}, u32[]{:S(2)}, u32[]{:S(2)}) collective-permute-start(bf16[64,3072]{1,0:T(8,128)(2,1)S(1)} %collective-permute-done.7.refs_3_), channel_id=1, source_target_pairs={{0,16},{16,32},{32,48},{48,64},{64,80},{80,96},{96,112},{112,128},... | collective-permute-start | bytes 1179656 | tf_op jit(solution)/shard_map/ppermute | solution.py:153

commit v5 on v4

v5 whole, which is shorter than its diff:
```python
import functools

import jax
import jax.numpy as jnp
from jax import lax
from jax.experimental import pallas as pl
from jax.experimental.pallas import tpu as pltpu
from jax.sharding import Mesh
from jax.sharding import PartitionSpec as P

BLOCK = 192
EDGE = 32
COL = ("col_0", "col_1")


def split(values, parts):
    pieces = []
    for _ in range(parts):
        piece = values.astype(jnp.bfloat16)
        pieces.append(piece)
        values = values - piece.astype(jnp.float32)
    return pieces


def banded(taps, lag):
    band = jnp.zeros(lag.shape, jnp.float32)
    for step in range(taps.shape[0]):
        band = jnp.where(lag == step, taps[step], band)
    return band


def weigh(groups, spot, taps, arc_id, *refs):
    stacks, (out, arcs, padded, *filtered) = refs[:3], refs[3:]
    rows, width = out.shape
    wide = BLOCK + EDGE
    down = lax.broadcasted_iota(jnp.int32, (BLOCK, wide), 0)
    across = lax.broadcasted_iota(jnp.int32, (BLOCK, wide), 1)
    forward = banded(taps, down + EDGE - across)
    backward = banded(taps, across - down)

    arcs[...] = jnp.full(arcs.shape, -1, jnp.int32)
    arcs[:, EDGE : EDGE + rows] = arc_id[...]

    def arc_column(start):
        row = arcs[:, start + EDGE : start + EDGE + 256]
        return jnp.broadcast_to(row, (8, 256)).T[:BLOCK, :1]

    padded[:EDGE] = jnp.zeros((EDGE, width), padded.dtype)
    blocks = [(stack, i) for stack in stacks for i in range(stack.shape[0])]
    for number, (stack, i) in enumerate(blocks):
        own = stack.shape[1]
        place = (spot[2] ^ (0, 1, 3, 2)[number // 2]) * 2 + (spot[3] ^ (number % 2))
        at = pl.multiple_of(EDGE + place * own, 32)
        padded[pl.ds(at, own)] = stack[i]
    for piece in filtered:
        piece[rows:] = jnp.zeros((EDGE, width), piece.dtype)
    dot = functools.partial(jnp.dot, preferred_element_type=jnp.float32)
    for start in range(0, rows, BLOCK):
        same = arc_column(start) == arcs[:, start : start + wide]
        window = padded[start : start + wide]
        total = jnp.zeros((BLOCK, width), jnp.float32)
        for piece in split(jnp.where(same, forward, 0.0), 3)[::-1]:
            total = total + dot(piece, window)
        for ref, piece in zip(filtered, split(total, 3), strict=True):
            ref[start : start + BLOCK] = piece
    per = rows // groups // 16
    for start in range(0, rows, BLOCK):
        same = arc_column(start) == arcs[:, start + EDGE : start + EDGE + wide]
        pieces = split(jnp.where(same, backward, 0.0), 3)
        total = jnp.zeros((BLOCK, width), jnp.float32)
        for i, j in ((2, 0), (1, 1), (0, 2), (1, 0), (0, 1), (0, 0)):
            total = total + dot(pieces[i], filtered[j][start : start + wide])
        total = total.astype(out.dtype)
        for tile in range(BLOCK // 16):
            group, spot = divmod(start // 16 + tile, per)
            at = (spot * groups + group) * 16
            out[at : at + 16] = total[tile * 16 : tile * 16 + 16]


SMEM = pl.BlockSpec(memory_space=pltpu.SMEM)
VMEM = pl.BlockSpec(memory_space=pltpu.VMEM)


def weighted(spot, stacks, taps, arc_id, groups):
    width = stacks[0].shape[-1]
    rows = arc_id.shape[0]
    return pl.pallas_call(
        functools.partial(weigh, groups),
        out_shape=jax.ShapeDtypeStruct((rows, width), jnp.bfloat16),
        in_specs=[SMEM, SMEM] + [VMEM] * (1 + len(stacks)),
        out_specs=VMEM,
        scratch_shapes=[pltpu.VMEM((1, rows + 128), jnp.int32)]
        + [pltpu.VMEM((rows + EDGE, width), jnp.bfloat16)] * 4,
        compiler_params=pltpu.CompilerParams(vmem_limit_bytes=12 << 20),
        cost_estimate=pl.CostEstimate(
            flops=18 * rows * (BLOCK + EDGE) * width,
            bytes_accessed=4 * rows * width,
            transcendentals=0,
        ),
    )(spot, taps, arc_id[None], *stacks)


def accumulate(count, sides, carried, met, spot, *refs):
    weights, refs = refs[:sides], refs[sides:]
    blocks, refs = refs[:count], refs[count:]
    priors, outs, left = refs[:carried], refs[carried : carried + sides], refs[-1]
    half = weights[0].shape[0] // 24
    ring, core = spot[0], spot[1]

    @pl.when(pl.program_id(0) == 0)
    def _():
        starts = []
        for part, steps, fixed in met:
            turn = 12 + steps if fixed else jnp.where(core == 0, 12 - steps, 12 + steps)
            origin = lax.rem(ring + turn, 12)
            which = part if fixed else core ^ part
            starts.append(pl.multiple_of((origin * 2 + which) * half, half))
        for side in range(sides):
            picked = [weights[side][pl.ds(start, half)] for start in starts]
            left[side] = jnp.concatenate(picked, axis=0).T

    right = jnp.concatenate([block[...] for block in blocks], axis=0)
    for side in range(sides):
        total = jnp.dot(left[side], right, preferred_element_type=jnp.float32)
        for prior in priors[side::sides]:
            total = total + prior[...].astype(jnp.float32)
        outs[side][...] = total.astype(outs[side].dtype)


def product(spot, weights, blocks, met, priors, kinds, tile):
    sides = len(weights)
    depth = sum(block.shape[0] for block in blocks)
    columns = blocks[0].shape[1]
    width = weights[0].shape[1]
    spec = pl.BlockSpec((width, tile), lambda i: (0, i))
    return pl.pallas_call(
        functools.partial(accumulate, len(blocks), sides, len(priors), tuple(met)),
        out_shape=[jax.ShapeDtypeStruct((width, columns), kind) for kind in kinds],
        grid=(columns // tile,),
        in_specs=[SMEM]
        + [VMEM] * sides
        + [pl.BlockSpec((b.shape[0], tile), lambda i: (0, i)) for b in blocks]
        + [spec] * len(priors),
        out_specs=[spec] * sides,
        scratch_shapes=[pltpu.VMEM((sides, width, depth), jnp.bfloat16)],
        compiler_params=pltpu.CompilerParams(vmem_limit_bytes=14 << 20),
        cost_estimate=pl.CostEstimate(
            flops=2 * sides * width * depth * columns,
            bytes_accessed=2 * depth * columns + 4 * (sides + len(priors)) * width * columns,
            transcendentals=0,
        ),
    )(spot, *weights, *blocks, *priors)


def block_of(static_design, tv_design, taps, arc_id):
    turns = lax.axis_size("ring")
    half = turns // 2
    swap = [(0, 1), (1, 0)]
    onward = [(2 * i, (i + 1) % turns * 2) for i in range(turns)]
    onward += [((i + 1) % turns * 2 + 1, i * 2 + 1) for i in range(turns)]

    def hop(block):
        return lax.ppermute(block, ("ring", "core"), onward)

    other = lax.ppermute(static_design, "col_1", swap)
    mine = [lax.all_gather(tv_design, "short", axis=0, tiled=True)]
    theirs = [lax.ppermute(mine[0], "core", swap)]

    pair = jnp.stack([static_design, other])
    beside = lax.ppermute(pair, "col_0", [(i, i ^ 1) for i in range(4)])
    opposite = lax.ppermute(jnp.concatenate([pair, beside]), "col_0", [(i, 3 - i) for i in range(4)])
    spot = jnp.stack([lax.axis_index(axis) for axis in ("ring", "core") + COL])

    for _ in range(1, half):
        mine.append(hop(mine[-1]))
        theirs.append(hop(theirs[-1]))
    mine.append(hop(mine[-1]))

    left = weighted(spot, (pair, beside, opposite), taps, arc_id, lax.axis_size("short"))
    lefts = (left, lax.ppermute(left, "core", swap))

    def near(blocks, priors, kinds):
        tv = [(mine, theirs)[part][steps] for part, steps in blocks]
        met = [(part, steps, False) for part, steps in blocks]
        return product(spot, lefts, tv, met, priors, kinds, 1024)

    f32 = jnp.float32
    first = [(0, d) for d in range(4)] + [(1, d) for d in range(1, 4)]
    sums = near(first, (), (f32, f32))
    sums = near([(0, 4), (1, 4), (0, 5)], sums, (f32, jnp.bfloat16))
    handed = lax.ppermute(sums[1], "core", swap)
    far = [lax.all_gather(theirs[half - 1], "core", axis=0, tiled=True)]
    far.append(lax.all_gather(mine[half], "core", axis=0, tiled=True))
    met = [(1, 1 - half, True), (0, half - 1, True), (0, -half, True), (1, half, True)]
    return product(spot, lefts[:1], far, met, (sums[0], handed), (f32,), 1024)[0]


def solution(mesh):
    finer = Mesh(
        mesh.devices.reshape(4, 12, 2, 4, 2),
        ("short", "ring", "core", "col_0", "col_1"),
    )
    row = ("short", "ring", "core")
    placed = (P(COL, row), P(row, COL), P(), P())
    return jax.shard_map(
        block_of, mesh=finer, in_specs=placed, out_specs=P(row, COL), check_vma=False
    )
```

time: 119 us -> 124 us (1.042)
  starting transfers between devices: 65.9 us -> 72.4 us
  other arithmetic: 3.25 us -> 1.93 us
    ppermute x11, starting transfers between devices: 30.1 us -> 41.4 us  [hop(): return lax.ppermute(block, ('ring', 'core'), onward)]
    ppermute x1, starting transfers between devices: 14.2 us -> 7.26 us  [block_of(): theirs = [lax.ppermute(mine[0], 'core', swap)]]
    ppermute x1, waiting for transfers between devices: 2.23 us -> 0.39 us  [block_of(): lax.ppermute(jnp.concatenate([pair, beside]), 'col_0', [(i, 3 - i) for i...]
    ppermute x1, starting transfers between devices: 4.57 us -> 6.06 us  [block_of(): handed = lax.ppermute(sums[1], 'core', swap)]
    pallas_call x1, Pallas kernels: 3.46 us -> 4.92 us  [weighted(): pl.pallas_call(functools.partial(weigh, groups), out_shape=jax.ShapeDtype...]
    add x4 -> x0, other arithmetic: 1.4 us -> none  [the longest x2 0.71 us: chosen(): return origin * 2 + (core + part) % 2]
  transfers between devices with their start and end apart: 17 -> 17, of which waited for: 7 -> 6; matrix products, arithmetic and copies ran while one was open for 4% -> 2% of each run, Pallas kernels for 6% -> 7%
where the time goes in v5:
time: 124 us; the launch traced here: 123 us
  starting transfers between devices  72.4 us (58%)
  blocking collectives  21.9 us (18%)
  Pallas kernels  14.6 us (12%)
  waiting for transfers between devices  11 us (9%)
  other arithmetic  1.93 us (2%)
  local copies, waits for them, and re-layouts  1.36 us (1%)
    ppermute x11, starting transfers between devices, hop(): return lax.ppermute(block, ('ring', 'core'), onward)  41.4 us
    all_gather x1, blocking collectives, block_of(): mine = [lax.all_gather(tv_design, 'short', axis=0, tiled=True)]  13.8 us
    ppermute x11, waiting for transfers between devices, hop(): return lax.ppermute(block, ('ring', 'core'), onward)  10.6 us
    pallas_call x3, Pallas kernels, product(): pl.pallas_call(functools.partial(accumulate, len(blocks), sides, len(prio...  9.65 us
    ppermute x1, starting transfers between devices, block_of(): other = lax.ppermute(static_design, 'col_1', swap)  8.26 us
    ppermute x1, starting transfers between devices, block_of(): theirs = [lax.ppermute(mine[0], 'core', swap)]  7.26 us
    ppermute x1, starting transfers between devices, block_of(): handed = lax.ppermute(sums[1], 'core', swap)  6.06 us
    pallas_call x1, Pallas kernels, weighted(): pl.pallas_call(functools.partial(weigh, groups), out_shape=jax.ShapeDtype...  4.92 us
  transfers between devices with their start and end apart: 17, of which 6 were waited for; matrix products, arithmetic and copies ran while one was open for 2% of the time, Pallas kernels for 7%

profile of v5, /device:TPU:1, one launch (start us, length us, event | category | flops | bytes accessed | tf_op | source)
XLA Modules:
  0.0 123.4 jit_solution(9180117532119067666)
XLA Ops:
  0.0 8.3 %collective-permute-start = (bf16[192,256]{1,0:T(8,128)(2,1)}, bf16[192,256]{1,0:T(8,128)(2,1)S(1)}, u32[]{:S(2)}, u32[]{:S(2)}) collective-permute-start(bf16[192,256]{1,0:T(8,128)(2,1)} %param.4), channel_id=1, source_target_pairs={{0,1},{1,0},{2,3},{3,2},{4,5},{5,4},{6,7},{7,6},{8,9},{9,8},{10,11... | collective-permute-start | bytes 294920 | tf_op jit(solution)/shard_map/ppermute | solution.py:165
  8.3 13.8 %all_gather.9.refs_2_ = bf16[64,3072]{1,0:T(8,128)(2,1)S(1)} all-gather(bf16[16,3072]{1,0:T(8,128)(2,1)} %param.5), channel_id=1, replica_groups=mesh['short'=4,'ring'=12,'core'=2,'col_0'=4,'col_1'=2] {'short'}, dimensions={0}, use_global_device_ids=true | all-gather | bytes 491520 | tf_op jit(solution)/shard_map/all_gather | solution.py:166
  22.0 7.3 %collective-permute-start.3 = (bf16[64,3072]{1,0:T(8,128)(2,1)S(1)}, bf16[64,3072]{1,0:T(8,128)(2,1)S(1)}, u32[]{:S(2)}, u32[]{:S(2)}) collective-permute-start(bf16[64,3072]{1,0:T(8,128)(2,1)S(1)} %all_gather.9.refs_2_), channel_id=1, source_target_pairs={{0,8},{8,0},{1,9},{9,1},{2,10},{10,2},{3,11},{11,3},{4,12},{12,4},... | collective-permute-start | bytes 1179656 | tf_op jit(solution)/shard_map/ppermute | solution.py:167
  29.3 11.4 %collective-permute-start.9 = (bf16[64,3072]{1,0:T(8,128)(2,1)S(1)}, bf16[64,3072]{1,0:T(8,128)(2,1)S(1)}, u32[]{:S(2)}, u32[]{:S(2)}) collective-permute-start(bf16[64,3072]{1,0:T(8,128)(2,1)S(1)} %all_gather.9.refs_2_), channel_id=1, source_target_pairs={{0,16},{16,32},{32,48},{48,64},{64,80},{80,96},{96,112},{112,128},... | collective-permute-start | bytes 1179656 | tf_op jit(solution)/shard_map/ppermute | solution.py:163
  40.7 0.9 pad_maximum_fusion.1.refs_0_
  41.7 3.1 %collective-permute-start.1 = (bf16[2,192,256]{2,1,0:T(8,128)(2,1)S(1)}, bf16[2,192,256]{2,1,0:T(8,128)(2,1)S(1)}, u32[]{:S(2)}, u32[]{:S(2)}) collective-permute-start(bf16[2,192,256]{2,1,0:T(8,128)(2,1)S(1)} %pad_maximum_fusion.1.refs_0_), channel_id=1, source_target_pairs={{0,2},{2,0},{4,6},{6,4},{1,3},{3,1},{5,7},{7,5},{8,10},{10,8},{12,... | collective-permute-start | bytes 589832 | tf_op jit(solution)/shard_map/ppermute | solution.py:170
  44.8 2.2 %collective-permute-start.4 = (bf16[64,3072]{1,0:T(8,128)(2,1)S(1)}, bf16[64,3072]{1,0:T(8,128)(2,1)S(1)}, u32[]{:S(2)}, u32[]{:S(2)}) collective-permute-start(bf16[64,3072]{1,0:T(8,128)(2,1)S(1)} %collective-permute-done.3), channel_id=1, source_target_pairs={{0,16},{16,32},{32,48},{48,64},{64,80},{80,96},{96,112},{112,128},... | collective-permute-start | bytes 1179656 | tf_op jit(solution)/shard_map/ppermute | solution.py:163
  47.0 3.4 %collective-permute-start.10 = (bf16[64,3072]{1,0:T(8,128)(2,1)S(1)}, bf16[64,3072]{1,0:T(8,128)(2,1)S(1)}, u32[]{:S(2)}, u32[]{:S(2)}) collective-permute-start(bf16[64,3072]{1,0:T(8,128)(2,1)S(1)} %collective-permute-done.9.refs_3_), channel_id=1, source_target_pairs={{0,16},{16,32},{32,48},{48,64},{64,80},{80,96},{96,112},{112,128},... | collective-permute-start | bytes 1179656 | tf_op jit(solution)/shard_map/ppermute | solution.py:163
  50.5 0.9 pad_maximum_fusion
  51.4 4.4 %collective-permute-start.2 = (bf16[4,192,256]{2,1,0:T(8,128)(2,1)S(1)}, bf16[4,192,256]{2,1,0:T(8,128)(2,1)S(1)}, u32[]{:S(2)}, u32[]{:S(2)}) collective-permute-start(bf16[4,192,256]{2,1,0:T(8,128)(2,1)S(1)} %pad_maximum_fusion), channel_id=1, source_target_pairs={{0,6},{2,4},{4,2},{6,0},{1,7},{3,5},{5,3},{7,1},{8,14},{10,12},{12... | collective-permute-start | bytes 1179656 | tf_op jit(solution)/shard_map/ppermute | solution.py:171
  55.8 2.0 %collective-permute-done.10.refs_4_ = bf16[64,3072]{1,0:T(8,128)(2,1)S(1)} collective-permute-done((bf16[64,3072]{1,0:T(8,128)(2,1)S(1)}, bf16[64,3072]{1,0:T(8,128)(2,1)S(1)}, u32[]{:S(2)}, u32[]{:S(2)}) %collective-permute-start.10) | collective-permute-done | bytes 393248 | tf_op jit(solution)/shard_map/ppermute | solution.py:163
  57.8 3.4 %collective-permute-start.11 = (bf16[64,3072]{1,0:T(8,128)(2,1)S(1)}, bf16[64,3072]{1,0:T(8,128)(2,1)S(1)}, u32[]{:S(2)}, u32[]{:S(2)}) collective-permute-start(bf16[64,3072]{1,0:T(8,128)(2,1)S(1)} %collective-permute-done.10.refs_4_), channel_id=1, source_target_pairs={{0,16},{16,32},{32,48},{48,64},{64,80},{80,96},{96,112},{112,128},... | collective-permute-start | bytes 1179656 | tf_op jit(solution)/shard_map/ppermute | solution.py:163
  61.2 1.9 %collective-permute-start.5 = (bf16[64,3072]{1,0:T(8,128)(2,1)S(1)}, bf16[64,3072]{1,0:T(8,128)(2,1)S(1)}, u32[]{:S(2)}, u32[]{:S(2)}) collective-permute-start(bf16[64,3072]{1,0:T(8,128)(2,1)S(1)} %collective-permute-done.4.refs_6_), channel_id=1, source_target_pairs={{0,16},{16,32},{32,48},{48,64},{64,80},{80,96},{96,112},{112,128},... | collective-permute-start | bytes 1179656 | tf_op jit(solution)/shard_map/ppermute | solution.py:163
  63.2 0.7 broadcast_in_dim.3.arc_id
  64.3 0.7 copy-done
  65.0 4.9 %shard_map.46.refs_0_ = bf16[1536,256]{1,0:T(8,128)(2,1)S(1)} custom-call(s32[4]{0:T(128)S(1)} %pad_add_fusion.spot, f32[32]{0:T(128)S(1)} %copy-done, s32[1,1536]{1,0:T(1,128)S(1)} %broadcast_in_dim.3.arc_id, bf16[2,192,256]{2,1,0:T(8,128)(2,1)S(1)} %pad_maximum_fusion.1.refs_0_, bf16[2,192,256]{2,1,0:T(8,128)(2,1)S(1)} %collective-permute-done.1.refs_1_, ...), custom_call_target="tpu_custom_call" | custom-call | flops 1585446912 | bytes 1572864 | tf_op jit(solution)/shard_map/pallas_call | solution.py:87
  69.9 1.9 %collective-permute-start.15 = (bf16[1536,256]{1,0:T(8,128)(2,1)S(1)}, bf16[1536,256]{1,0:T(8,128)(2,1)S(1)}, u32[]{:S(2)}, u32[]{:S(2)}) collective-permute-start(bf16[1536,256]{1,0:T(8,128)(2,1)S(1)} %shard_map.46.refs_0_), channel_id=1, source_target_pairs={{0,8},{8,0},{1,9},{9,1},{2,10},{10,2},{3,11},{11,3},{4,12},{12,4},... | collective-permute-start | bytes 2359304 | tf_op jit(solution)/shard_map/ppermute | solution.py:180
  71.9 3.7 %collective-permute-start.12 = (bf16[64,3072]{1,0:T(8,128)(2,1)S(1)}, bf16[64,3072]{1,0:T(8,128)(2,1)S(1)}, u32[]{:S(2)}, u32[]{:S(2)}) collective-permute-start(bf16[64,3072]{1,0:T(8,128)(2,1)S(1)} %collective-permute-done.11.refs_5_), channel_id=1, source_target_pairs={{0,16},{16,32},{32,48},{48,64},{64,80},{80,96},{96,112},{112,128},... | collective-permute-start | bytes 1179656 | tf_op jit(solution)/shard_map/ppermute | solution.py:163
  75.5 2.8 %collective-permute-start.6 = (bf16[64,3072]{1,0:T(8,128)(2,1)S(1)}, bf16[64,3072]{1,0:T(8,128)(2,1)S(1)}, u32[]{:S(2)}, u32[]{:S(2)}) collective-permute-start(bf16[64,3072]{1,0:T(8,128)(2,1)S(1)} %collective-permute-done.5.refs_7_), channel_id=1, source_target_pairs={{0,16},{16,32},{32,48},{48,64},{64,80},{80,96},{96,112},{112,128},... | collective-permute-start | bytes 1179656 | tf_op jit(solution)/shard_map/ppermute | solution.py:163
  78.3 2.4 %collective-permute-done.12.refs_2_ = bf16[64,3072]{1,0:T(8,128)(2,1)S(1)} collective-permute-done((bf16[64,3072]{1,0:T(8,128)(2,1)S(1)}, bf16[64,3072]{1,0:T(8,128)(2,1)S(1)}, u32[]{:S(2)}, u32[]{:S(2)}) %collective-permute-start.12) | collective-permute-done | bytes 393248 | tf_op jit(solution)/shard_map/ppermute | solution.py:163
  80.7 4.6 %collective-permute-start.13 = (bf16[64,3072]{1,0:T(8,128)(2,1)S(1)}, bf16[64,3072]{1,0:T(8,128)(2,1)S(1)}, u32[]{:S(2)}, u32[]{:S(2)}) collective-permute-start(bf16[64,3072]{1,0:T(8,128)(2,1)S(1)} %collective-permute-done.12.refs_2_), channel_id=1, source_target_pairs={{0,16},{16,32},{32,48},{48,64},{64,80},{80,96},{96,112},{112,128},... | collective-permute-start | bytes 1179656 | tf_op jit(solution)/shard_map/ppermute | solution.py:163
  85.3 4.2 %collective-permute-start.7 = (bf16[64,3072]{1,0:T(8,128)(2,1)S(1)}, bf16[64,3072]{1,0:T(8,128)(2,1)S(1)}, u32[]{:S(2)}, u32[]{:S(2)}) collective-permute-start(bf16[64,3072]{1,0:T(8,128)(2,1)S(1)} %collective-permute-done.6.refs_8_), channel_id=1, source_target_pairs={{0,16},{16,32},{32,48},{48,64},{64,80},{80,96},{96,112},{112,128},... | collective-permute-start | bytes 1179656 | tf_op jit(solution)/shard_map/ppermute | solution.py:163
  89.5 3.6 %shard_map.47 = (f32[256,3072]{1,0:T(8,128)S(1)}, f32[256,3072]{1,0:T(8,128)S(1)}) custom-call(s32[4]{0:T(128)S(1)} %pad_add_fusion.spot, bf16[1536,256]{1,0:T(8,128)(2,1)S(1)} %shard_map.46.refs_0_, bf16[1536,256]{1,0:T(8,128)(2,1)S(1)} %collective-permute-done.15.refs_1_, bf16[64,3072]{1,0:T(8,128)(2,1)S(1)} %all_gather.9.refs_2_, ...), custom_call_target="tpu_custom_call" | custom-call | flops 1409286144 | bytes 9043968 | tf_op jit(solution)/shard_map/pallas_call | solution.py:136
  93.1 1.1 collective-permute-done.7.refs_3_
  94.2 2.7 %shard_map.48 = (f32[256,3072]{1,0:T(8,128)S(1)}, bf16[256,3072]{1,0:T(8,128)(2,1)S(1)}) custom-call(s32[4]{0:T(128)S(1)} %pad_add_fusion.spot, bf16[1536,256]{1,0:T(8,128)(2,1)S(1)} %shard_map.46.refs_0_, bf16[1536,256]{1,0:T(8,128)(2,1)S(1)} %collective-permute-done.15.refs_1_, bf16[64,3072]{1,0:T(8,128)(2,1)S(1)} %collective-permute-done.12.refs_2_, ...), custom_call_target="tpu_custom_call" | custom-call | flops 603979776 | bytes 13762560 | tf_op jit(solution)/shard_map/pallas_call | solution.py:136
  96.9 6.1 %collective-permute-start.16 = (bf16[256,3072]{1,0:T(8,128)(2,1)S(1)}, bf16[256,3072]{1,0:T(8,128)(2,1)S(1)}, u32[]{:S(2)}, u32[]{:S(2)}) collective-permute-start(bf16[256,3072]{1,0:T(8,128)(2,1)S(1)} %get-tuple-element.12), channel_id=1, source_target_pairs={{0,8},{8,0},{1,9},{9,1},{2,10},{10,2},{3,11},{11,3},{4,12},{12,4},... | collective-permute-start | bytes 4718600 | tf_op jit(solution)/shard_map/ppermute | solution.py:191
  103.0 1.9 %collective-permute-start.14 = (bf16[64,3072]{1,0:T(8,128)(2,1)S(1)}, bf16[64,3072]{1,0:T(8,128)(2,1)S(1)}, u32[]{:S(2)}, u32[]{:S(2)}) collective-permute-start(bf16[64,3072]{1,0:T(8,128)(2,1)S(1)} %collective-permute-done.13.refs_4_), channel_id=1, source_target_pairs={{0,16},{16,32},{32,48},{48,64},{64,80},{80,96},{96,112},{112,128},... | collective-permute-start | bytes 1179656 | tf_op jit(solution)/shard_map/ppermute | solution.py:163
  104.9 1.9 %collective-permute-start.8 = (bf16[64,3072]{1,0:T(8,128)(2,1)S(1)}, bf16[64,3072]{1,0:T(8,128)(2,1)S(1)}, u32[]{:S(2)}, u32[]{:S(2)}) collective-permute-start(bf16[64,3072]{1,0:T(8,128)(2,1)S(1)} %collective-permute-done.7.refs_3_), channel_id=1, source_target_pairs={{0,16},{16,32},{32,48},{48,64},{64,80},{80,96},{96,112},{112,128},... | collective-permute-start | bytes 1179656 | tf_op jit(solution)/shard_map/ppermute | solution.py:163
  106.8 5.0 %collective-permute-done.14 = bf16[64,3072]{1,0:T(8,128)(2,1)S(1)} collective-permute-done((bf16[64,3072]{1,0:T(8,128)(2,1)S(1)}, bf16[64,3072]{1,0:T(8,128)(2,1)S(1)}, u32[]{:S(2)}, u32[]{:S(2)}) %collective-permute-start.14) | collective-permute-done | bytes 393248 | tf_op jit(solution)/shard_map/ppermute | solution.py:163
  111.8 4.1 %all_gather.11.refs_2_ = bf16[128,3072]{1,0:T(8,128)(2,1)S(1)} all-gather(bf16[64,3072]{1,0:T(8,128)(2,1)S(1)} %collective-permute-done.14), channel_id=1, replica_groups=mesh['short'=4,'ring'=12,'core'=2,'col_0'=4,'col_1'=2] {'core'}, dimensions={0}, use_global_device_ids=true | all-gather | bytes 1179648 | tf_op jit(solution)/shard_map/all_gather | solution.py:193
  116.0 4.1 %all_gather.10.refs_1_ = bf16[128,3072]{1,0:T(8,128)(2,1)S(1)} all-gather(bf16[64,3072]{1,0:T(8,128)(2,1)S(1)} %collective-permute-done.8), channel_id=1, replica_groups=mesh['short'=4,'ring'=12,'core'=2,'col_0'=4,'col_1'=2] {'core'}, dimensions={0}, use_global_device_ids=true | all-gather | bytes 1179648 | tf_op jit(solution)/shard_map/all_gather | solution.py:192
  120.1 3.4 %shard_map.49 = f32[256,3072]{1,0:T(8,128)} custom-call(s32[4]{0:T(128)S(1)} %pad_add_fusion.spot, bf16[1536,256]{1,0:T(8,128)(2,1)S(1)} %shard_map.46.refs_0_, bf16[128,3072]{1,0:T(8,128)(2,1)S(1)} %all_gather.10.refs_1_, bf16[128,3072]{1,0:T(8,128)(2,1)S(1)} %all_gather.11.refs_2_, f32[256,3072]{1,0:T(8,128)S(1)} %get-tuple-element.11.refs_3_, ...), custom_call_target="tpu_custom_call" | custom-call | flops 402653184 | bytes 11010048 | tf_op jit(solution)/shard_map/pallas_call | solution.py:136
  (15 shorter events, 0.7 us)
Async XLA Ops:
  0.0 40.7 %collective-permute-start = (bf16[192,256]{1,0:T(8,128)(2,1)}, bf16[192,256]{1,0:T(8,128)(2,1)S(1)}, u32[]{:S(2)}, u32[]{:S(2)}) collective-permute-start(bf16[192,256]{1,0:T(8,128)(2,1)} %param.4), channel_id=1, source_target_pairs={{0,1},{1,0},{2,3},{3,2},{4,5},{5,4},{6,7},{7,6},{8,9},{9,8},{10,11... | collective-permute-start | bytes 294920 | tf_op jit(solution)/shard_map/ppermute | solution.py:165
  22.0 22.7 %collective-permute-start.3 = (bf16[64,3072]{1,0:T(8,128)(2,1)S(1)}, bf16[64,3072]{1,0:T(8,128)(2,1)S(1)}, u32[]{:S(2)}, u32[]{:S(2)}) collective-permute-start(bf16[64,3072]{1,0:T(8,128)(2,1)S(1)} %all_gather.9.refs_2_), channel_id=1, source_target_pairs={{0,8},{8,0},{1,9},{9,1},{2,10},{10,2},{3,11},{11,3},{4,12},{12,4},... | collective-permute-start | bytes 1179656 | tf_op jit(solution)/shard_map/ppermute | solution.py:167
  29.3 17.7 %collective-permute-start.9 = (bf16[64,3072]{1,0:T(8,128)(2,1)S(1)}, bf16[64,3072]{1,0:T(8,128)(2,1)S(1)}, u32[]{:S(2)}, u32[]{:S(2)}) collective-permute-start(bf16[64,3072]{1,0:T(8,128)(2,1)S(1)} %all_gather.9.refs_2_), channel_id=1, source_target_pairs={{0,16},{16,32},{32,48},{48,64},{64,80},{80,96},{96,112},{112,128},... | collective-permute-start | bytes 1179656 | tf_op jit(solution)/shard_map/ppermute | solution.py:163
  41.7 8.8 %collective-permute-start.1 = (bf16[2,192,256]{2,1,0:T(8,128)(2,1)S(1)}, bf16[2,192,256]{2,1,0:T(8,128)(2,1)S(1)}, u32[]{:S(2)}, u32[]{:S(2)}) collective-permute-start(bf16[2,192,256]{2,1,0:T(8,128)(2,1)S(1)} %pad_maximum_fusion.1.refs_0_), channel_id=1, source_target_pairs={{0,2},{2,0},{4,6},{6,4},{1,3},{3,1},{5,7},{7,5},{8,10},{10,8},{12,... | collective-permute-start | bytes 589832 | tf_op jit(solution)/shard_map/ppermute | solution.py:170
  44.8 16.4 %collective-permute-start.4 = (bf16[64,3072]{1,0:T(8,128)(2,1)S(1)}, bf16[64,3072]{1,0:T(8,128)(2,1)S(1)}, u32[]{:S(2)}, u32[]{:S(2)}) collective-permute-start(bf16[64,3072]{1,0:T(8,128)(2,1)S(1)} %collective-permute-done.3), channel_id=1, source_target_pairs={{0,16},{16,32},{32,48},{48,64},{64,80},{80,96},{96,112},{112,128},... | collective-permute-start | bytes 1179656 | tf_op jit(solution)/shard_map/ppermute | solution.py:163
  47.0 10.8 %collective-permute-start.10 = (bf16[64,3072]{1,0:T(8,128)(2,1)S(1)}, bf16[64,3072]{1,0:T(8,128)(2,1)S(1)}, u32[]{:S(2)}, u32[]{:S(2)}) collective-permute-start(bf16[64,3072]{1,0:T(8,128)(2,1)S(1)} %collective-permute-done.9.refs_3_), channel_id=1, source_target_pairs={{0,16},{16,32},{32,48},{48,64},{64,80},{80,96},{96,112},{112,128},... | collective-permute-start | bytes 1179656 | tf_op jit(solution)/shard_map/ppermute | solution.py:163
  51.4 12.9 %collective-permute-start.2 = (bf16[4,192,256]{2,1,0:T(8,128)(2,1)S(1)}, bf16[4,192,256]{2,1,0:T(8,128)(2,1)S(1)}, u32[]{:S(2)}, u32[]{:S(2)}) collective-permute-start(bf16[4,192,256]{2,1,0:T(8,128)(2,1)S(1)} %pad_maximum_fusion), channel_id=1, source_target_pairs={{0,6},{2,4},{4,2},{6,0},{1,7},{3,5},{5,3},{7,1},{8,14},{10,12},{12... | collective-permute-start | bytes 1179656 | tf_op jit(solution)/shard_map/ppermute | solution.py:171
  57.8 14.0 %collective-permute-start.11 = (bf16[64,3072]{1,0:T(8,128)(2,1)S(1)}, bf16[64,3072]{1,0:T(8,128)(2,1)S(1)}, u32[]{:S(2)}, u32[]{:S(2)}) collective-permute-start(bf16[64,3072]{1,0:T(8,128)(2,1)S(1)} %collective-permute-done.10.refs_4_), channel_id=1, source_target_pairs={{0,16},{16,32},{32,48},{48,64},{64,80},{80,96},{96,112},{112,128},... | collective-permute-start | bytes 1179656 | tf_op jit(solution)/shard_map/ppermute | solution.py:163
  61.2 14.3 %collective-permute-start.5 = (bf16[64,3072]{1,0:T(8,128)(2,1)S(1)}, bf16[64,3072]{1,0:T(8,128)(2,1)S(1)}, u32[]{:S(2)}, u32[]{:S(2)}) collective-permute-start(bf16[64,3072]{1,0:T(8,128)(2,1)S(1)} %collective-permute-done.4.refs_6_), channel_id=1, source_target_pairs={{0,16},{16,32},{32,48},{48,64},{64,80},{80,96},{96,112},{112,128},... | collective-permute-start | bytes 1179656 | tf_op jit(solution)/shard_map/ppermute | solution.py:163
  64.3 0.7 copy-start
  69.9 19.6 %collective-permute-start.15 = (bf16[1536,256]{1,0:T(8,128)(2,1)S(1)}, bf16[1536,256]{1,0:T(8,128)(2,1)S(1)}, u32[]{:S(2)}, u32[]{:S(2)}) collective-permute-start(bf16[1536,256]{1,0:T(8,128)(2,1)S(1)} %shard_map.46.refs_0_), channel_id=1, source_target_pairs={{0,8},{8,0},{1,9},{9,1},{2,10},{10,2},{3,11},{11,3},{4,12},{12,4},... | collective-permute-start | bytes 2359304 | tf_op jit(solution)/shard_map/ppermute | solution.py:180
  71.9 8.8 %collective-permute-start.12 = (bf16[64,3072]{1,0:T(8,128)(2,1)S(1)}, bf16[64,3072]{1,0:T(8,128)(2,1)S(1)}, u32[]{:S(2)}, u32[]{:S(2)}) collective-permute-start(bf16[64,3072]{1,0:T(8,128)(2,1)S(1)} %collective-permute-done.11.refs_5_), channel_id=1, source_target_pairs={{0,16},{16,32},{32,48},{48,64},{64,80},{80,96},{96,112},{112,128},... | collective-permute-start | bytes 1179656 | tf_op jit(solution)/shard_map/ppermute | solution.py:163
  75.5 9.7 %collective-permute-start.6 = (bf16[64,3072]{1,0:T(8,128)(2,1)S(1)}, bf16[64,3072]{1,0:T(8,128)(2,1)S(1)}, u32[]{:S(2)}, u32[]{:S(2)}) collective-permute-start(bf16[64,3072]{1,0:T(8,128)(2,1)S(1)} %collective-permute-done.5.refs_7_), channel_id=1, source_target_pairs={{0,16},{16,32},{32,48},{48,64},{64,80},{80,96},{96,112},{112,128},... | collective-permute-start | bytes 1179656 | tf_op jit(solution)/shard_map/ppermute | solution.py:163
  80.7 12.4 %collective-permute-start.13 = (bf16[64,3072]{1,0:T(8,128)(2,1)S(1)}, bf16[64,3072]{1,0:T(8,128)(2,1)S(1)}, u32[]{:S(2)}, u32[]{:S(2)}) collective-permute-start(bf16[64,3072]{1,0:T(8,128)(2,1)S(1)} %collective-permute-done.12.refs_2_), channel_id=1, source_target_pairs={{0,16},{16,32},{32,48},{48,64},{64,80},{80,96},{96,112},{112,128},... | collective-permute-start | bytes 1179656 | tf_op jit(solution)/shard_map/ppermute | solution.py:163
  85.3 8.9 %collective-permute-start.7 = (bf16[64,3072]{1,0:T(8,128)(2,1)S(1)}, bf16[64,3072]{1,0:T(8,128)(2,1)S(1)}, u32[]{:S(2)}, u32[]{:S(2)}) collective-permute-start(bf16[64,3072]{1,0:T(8,128)(2,1)S(1)} %collective-permute-done.6.refs_8_), channel_id=1, source_target_pairs={{0,16},{16,32},{32,48},{48,64},{64,80},{80,96},{96,112},{112,128},... | collective-permute-start | bytes 1179656 | tf_op jit(solution)/shard_map/ppermute | solution.py:163
  96.9 23.2 %collective-permute-start.16 = (bf16[256,3072]{1,0:T(8,128)(2,1)S(1)}, bf16[256,3072]{1,0:T(8,128)(2,1)S(1)}, u32[]{:S(2)}, u32[]{:S(2)}) collective-permute-start(bf16[256,3072]{1,0:T(8,128)(2,1)S(1)} %get-tuple-element.12), channel_id=1, source_target_pairs={{0,8},{8,0},{1,9},{9,1},{2,10},{10,2},{3,11},{11,3},{4,12},{12,4},... | collective-permute-start | bytes 4718600 | tf_op jit(solution)/shard_map/ppermute | solution.py:191
  103.0 8.8 %collective-permute-start.14 = (bf16[64,3072]{1,0:T(8,128)(2,1)S(1)}, bf16[64,3072]{1,0:T(8,128)(2,1)S(1)}, u32[]{:S(2)}, u32[]{:S(2)}) collective-permute-start(bf16[64,3072]{1,0:T(8,128)(2,1)S(1)} %collective-permute-done.13.refs_4_), channel_id=1, source_target_pairs={{0,16},{16,32},{32,48},{48,64},{64,80},{80,96},{96,112},{112,128},... | collective-permute-start | bytes 1179656 | tf_op jit(solution)/shard_map/ppermute | solution.py:163
  104.9 11.1 %collective-permute-start.8 = (bf16[64,3072]{1,0:T(8,128)(2,1)S(1)}, bf16[64,3072]{1,0:T(8,128)(2,1)S(1)}, u32[]{:S(2)}, u32[]{:S(2)}) collective-permute-start(bf16[64,3072]{1,0:T(8,128)(2,1)S(1)} %collective-permute-done.7.refs_3_), channel_id=1, source_target_pairs={{0,16},{16,32},{32,48},{48,64},{64,80},{80,96},{96,112},{112,128},... | collective-permute-start | bytes 1179656 | tf_op jit(solution)/shard_map/ppermute | solution.py:163

commit v6 on v5

--- a/solution.py
+++ b/solution.py
@@ -29,21 +29,14 @@
     return band
 
 
-def weigh(groups, spot, taps, arc_id, *refs):
-    stacks, (out, arcs, padded, *filtered) = refs[:3], refs[3:]
+def weigh(groups, spot, taps, arc_rows, arcs, *refs):
+    stacks, (out, padded, *filtered) = refs[:3], refs[3:]
     rows, width = out.shape
     wide = BLOCK + EDGE
     down = lax.broadcasted_iota(jnp.int32, (BLOCK, wide), 0)
     across = lax.broadcasted_iota(jnp.int32, (BLOCK, wide), 1)
     forward = banded(taps, down + EDGE - across)
     backward = banded(taps, across - down)
-
-    arcs[...] = jnp.full(arcs.shape, -1, jnp.int32)
-    arcs[:, EDGE : EDGE + rows] = arc_id[...]
-
-    def arc_column(start):
-        row = arcs[:, start + EDGE : start + EDGE + 256]
-        return jnp.broadcast_to(row, (8, 256)).T[:BLOCK, :1]
 
     padded[:EDGE] = jnp.zeros((EDGE, width), padded.dtype)
     blocks = [(stack, i) for stack in stacks for i in range(stack.shape[0])]
@@ -56,7 +49,7 @@
         piece[rows:] = jnp.zeros((EDGE, width), piece.dtype)
     dot = functools.partial(jnp.dot, preferred_element_type=jnp.float32)
     for start in range(0, rows, BLOCK):
-        same = arc_column(start) == arcs[:, start : start + wide]
+        same = arc_rows[start : start + BLOCK] == arcs[:, start : start + wide]
         window = padded[start : start + wide]
         total = jnp.zeros((BLOCK, width), jnp.float32)
         for piece in split(jnp.where(same, forward, 0.0), 3)[::-1]:
@@ -65,7 +58,7 @@
             ref[start : start + BLOCK] = piece
     per = rows // groups // 16
     for start in range(0, rows, BLOCK):
-        same = arc_column(start) == arcs[:, start + EDGE : start + EDGE + wide]
+        same = arc_rows[start : start + BLOCK] == arcs[:, start + EDGE : start + EDGE + wide]
         pieces = split(jnp.where(same, backward, 0.0), 3)
         total = jnp.zeros((BLOCK, width), jnp.float32)
         for i, j in ((2, 0), (1, 1), (0, 2), (1, 0), (0, 1), (0, 0)):
@@ -84,20 +77,21 @@
 def weighted(spot, stacks, taps, arc_id, groups):
     width = stacks[0].shape[-1]
     rows = arc_id.shape[0]
+    arcs = jnp.pad(arc_id, (EDGE, 128 - EDGE), constant_values=-1)[None]
+    arc_rows = arc_id[:, None]
     return pl.pallas_call(
         functools.partial(weigh, groups),
         out_shape=jax.ShapeDtypeStruct((rows, width), jnp.bfloat16),
-        in_specs=[SMEM, SMEM] + [VMEM] * (1 + len(stacks)),
+        in_specs=[SMEM, SMEM] + [VMEM] * (2 + len(stacks)),
         out_specs=VMEM,
-        scratch_shapes=[pltpu.VMEM((1, rows + 128), jnp.int32)]
-        + [pltpu.VMEM((rows + EDGE, width), jnp.bfloat16)] * 4,
+        scratch_shapes=[pltpu.VMEM((rows + EDGE, width), jnp.bfloat16)] * 4,
         compiler_params=pltpu.CompilerParams(vmem_limit_bytes=12 << 20),
         cost_estimate=pl.CostEstimate(
             flops=18 * rows * (BLOCK + EDGE) * width,
             bytes_accessed=4 * rows * width,
             transcendentals=0,
         ),
-    )(spot, taps, arc_id[None], *stacks)
+    )(spot, taps, arc_rows, arcs, *stacks)
 
 
 def accumulate(count, sides, carried, met, spot, *refs):

time: 124 us -> 123 us (level)
  Pallas kernels: 14.6 us -> 13.2 us
    pallas_call x1, Pallas kernels: 4.92 us -> 3.58 us  [weighted(): pl.pallas_call(functools.partial(weigh, groups), out_shape=jax.ShapeDtype...]
  transfers between devices with their start and end apart: 17 -> 17, of which waited for: 6 -> 6; matrix products, arithmetic and copies ran while one was open for 2% -> 3% of each run, Pallas kernels for 7% -> 6%
where the time goes in v6:
time: 123 us
  starting transfers between devices  72.7 us (59%)
  blocking collectives  21.9 us (18%)
  Pallas kernels  13.2 us (11%)
  waiting for transfers between devices  10.3 us (8%)
  local copies, waits for them, and re-layouts  2.39 us (2%)
  other arithmetic  1.93 us (2%)
    ppermute x11, starting transfers between devices, hop(): return lax.ppermute(block, ('ring', 'core'), onward)  41.2 us
    all_gather x1, blocking collectives, block_of(): mine = [lax.all_gather(tv_design, 'short', axis=0, tiled=True)]  13.8 us
    ppermute x11, waiting for transfers between devices, hop(): return lax.ppermute(block, ('ring', 'core'), onward)  10.3 us
    pallas_call x3, Pallas kernels, product(): pl.pallas_call(functools.partial(accumulate, len(blocks), sides, len(prio...  9.66 us
    ppermute x1, starting transfers between devices, block_of(): other = lax.ppermute(static_design, 'col_1', swap)  8.26 us
    ppermute x1, starting transfers between devices, block_of(): theirs = [lax.ppermute(mine[0], 'core', swap)]  7.26 us
    ppermute x1, starting transfers between devices, block_of(): handed = lax.ppermute(sums[1], 'core', swap)  6.54 us
    ppermute x1, starting transfers between devices, block_of(): lax.ppermute(jnp.concatenate([pair, beside]), 'col_0', [(i, 3 - i) for i...  4.39 us
  transfers between devices with their start and end apart: 17, of which 6 were waited for; matrix products, arithmetic and copies ran while one was open for 3% of the time, Pallas kernels for 6%

profile of v6, /device:TPU:1, one launch (start us, length us, event | category | flops | bytes accessed | tf_op | source)
XLA Modules:
  0.0 122.7 jit_solution(4461015201998227257)
XLA Ops:
  0.0 8.3 %collective-permute-start = (bf16[192,256]{1,0:T(8,128)(2,1)}, bf16[192,256]{1,0:T(8,128)(2,1)S(1)}, u32[]{:S(2)}, u32[]{:S(2)}) collective-permute-start(bf16[192,256]{1,0:T(8,128)(2,1)} %param.4), channel_id=1, source_target_pairs={{0,1},{1,0},{2,3},{3,2},{4,5},{5,4},{6,7},{7,6},{8,9},{9,8},{10,11... | collective-permute-start | bytes 294920 | tf_op jit(solution)/shard_map/ppermute | solution.py:159
  8.3 13.8 %all_gather.9.refs_2_ = bf16[64,3072]{1,0:T(8,128)(2,1)S(1)} all-gather(bf16[16,3072]{1,0:T(8,128)(2,1)} %param.5), channel_id=1, replica_groups=mesh['short'=4,'ring'=12,'core'=2,'col_0'=4,'col_1'=2] {'short'}, dimensions={0}, use_global_device_ids=true | all-gather | bytes 491520 | tf_op jit(solution)/shard_map/all_gather | solution.py:160
  22.0 7.3 %collective-permute-start.3 = (bf16[64,3072]{1,0:T(8,128)(2,1)S(1)}, bf16[64,3072]{1,0:T(8,128)(2,1)S(1)}, u32[]{:S(2)}, u32[]{:S(2)}) collective-permute-start(bf16[64,3072]{1,0:T(8,128)(2,1)S(1)} %all_gather.9.refs_2_), channel_id=1, source_target_pairs={{0,8},{8,0},{1,9},{9,1},{2,10},{10,2},{3,11},{11,3},{4,12},{12,4},... | collective-permute-start | bytes 1179656 | tf_op jit(solution)/shard_map/ppermute | solution.py:161
  29.3 11.4 %collective-permute-start.9 = (bf16[64,3072]{1,0:T(8,128)(2,1)S(1)}, bf16[64,3072]{1,0:T(8,128)(2,1)S(1)}, u32[]{:S(2)}, u32[]{:S(2)}) collective-permute-start(bf16[64,3072]{1,0:T(8,128)(2,1)S(1)} %all_gather.9.refs_2_), channel_id=1, source_target_pairs={{0,16},{16,32},{32,48},{48,64},{64,80},{80,96},{96,112},{112,128},... | collective-permute-start | bytes 1179656 | tf_op jit(solution)/shard_map/ppermute | solution.py:157
  40.7 0.9 pad_maximum_fusion.1.refs_0_
  41.7 3.1 %collective-permute-start.1 = (bf16[2,192,256]{2,1,0:T(8,128)(2,1)S(1)}, bf16[2,192,256]{2,1,0:T(8,128)(2,1)S(1)}, u32[]{:S(2)}, u32[]{:S(2)}) collective-permute-start(bf16[2,192,256]{2,1,0:T(8,128)(2,1)S(1)} %pad_maximum_fusion.1.refs_0_), channel_id=1, source_target_pairs={{0,2},{2,0},{4,6},{6,4},{1,3},{3,1},{5,7},{7,5},{8,10},{10,8},{12,... | collective-permute-start | bytes 589832 | tf_op jit(solution)/shard_map/ppermute | solution.py:164
  44.8 2.2 %collective-permute-start.4 = (bf16[64,3072]{1,0:T(8,128)(2,1)S(1)}, bf16[64,3072]{1,0:T(8,128)(2,1)S(1)}, u32[]{:S(2)}, u32[]{:S(2)}) collective-permute-start(bf16[64,3072]{1,0:T(8,128)(2,1)S(1)} %collective-permute-done.3), channel_id=1, source_target_pairs={{0,16},{16,32},{32,48},{48,64},{64,80},{80,96},{96,112},{112,128},... | collective-permute-start | bytes 1179656 | tf_op jit(solution)/shard_map/ppermute | solution.py:157
  47.0 3.4 %collective-permute-start.10 = (bf16[64,3072]{1,0:T(8,128)(2,1)S(1)}, bf16[64,3072]{1,0:T(8,128)(2,1)S(1)}, u32[]{:S(2)}, u32[]{:S(2)}) collective-permute-start(bf16[64,3072]{1,0:T(8,128)(2,1)S(1)} %collective-permute-done.9.refs_3_), channel_id=1, source_target_pairs={{0,16},{16,32},{32,48},{48,64},{64,80},{80,96},{96,112},{112,128},... | collective-permute-start | bytes 1179656 | tf_op jit(solution)/shard_map/ppermute | solution.py:157
  50.5 0.9 pad_maximum_fusion
  51.4 4.4 %collective-permute-start.2 = (bf16[4,192,256]{2,1,0:T(8,128)(2,1)S(1)}, bf16[4,192,256]{2,1,0:T(8,128)(2,1)S(1)}, u32[]{:S(2)}, u32[]{:S(2)}) collective-permute-start(bf16[4,192,256]{2,1,0:T(8,128)(2,1)S(1)} %pad_maximum_fusion), channel_id=1, source_target_pairs={{0,6},{2,4},{4,2},{6,0},{1,7},{3,5},{5,3},{7,1},{8,14},{10,12},{12... | collective-permute-start | bytes 1179656 | tf_op jit(solution)/shard_map/ppermute | solution.py:165
  55.8 2.0 %collective-permute-done.10.refs_4_ = bf16[64,3072]{1,0:T(8,128)(2,1)S(1)} collective-permute-done((bf16[64,3072]{1,0:T(8,128)(2,1)S(1)}, bf16[64,3072]{1,0:T(8,128)(2,1)S(1)}, u32[]{:S(2)}, u32[]{:S(2)}) %collective-permute-start.10) | collective-permute-done | bytes 393248 | tf_op jit(solution)/shard_map/ppermute | solution.py:157
  57.8 3.4 %collective-permute-start.11 = (bf16[64,3072]{1,0:T(8,128)(2,1)S(1)}, bf16[64,3072]{1,0:T(8,128)(2,1)S(1)}, u32[]{:S(2)}, u32[]{:S(2)}) collective-permute-start(bf16[64,3072]{1,0:T(8,128)(2,1)S(1)} %collective-permute-done.10.refs_4_), channel_id=1, source_target_pairs={{0,16},{16,32},{32,48},{48,64},{64,80},{80,96},{96,112},{112,128},... | collective-permute-start | bytes 1179656 | tf_op jit(solution)/shard_map/ppermute | solution.py:157
  61.2 1.9 %collective-permute-start.5 = (bf16[64,3072]{1,0:T(8,128)(2,1)S(1)}, bf16[64,3072]{1,0:T(8,128)(2,1)S(1)}, u32[]{:S(2)}, u32[]{:S(2)}) collective-permute-start(bf16[64,3072]{1,0:T(8,128)(2,1)S(1)} %collective-permute-done.4.refs_6_), channel_id=1, source_target_pairs={{0,16},{16,32},{32,48},{48,64},{64,80},{80,96},{96,112},{112,128},... | collective-permute-start | bytes 1179656 | tf_op jit(solution)/shard_map/ppermute | solution.py:157
  63.2 1.0 broadcast_in_dim.8.arc_rows
  64.1 0.8 pad.4
  65.6 3.6 %shard_map.46.refs_0_ = bf16[1536,256]{1,0:T(8,128)(2,1)S(1)} custom-call(s32[4]{0:T(128)S(1)} %pad_add_fusion.spot, f32[32]{0:T(128)S(1)} %copy-done, s32[1536,1]{1,0:T(8,128)S(1)} %broadcast_in_dim.8.arc_rows, s32[1,1664]{1,0:T(1,128)S(1)} %broadcast_in_dim.7.arcs, bf16[2,192,256]{2,1,0:T(8,128)(2,1)S(1)} %pad_maximum_fusion.1.refs_0_, ...), custom_call_target="tpu_custom_call" | custom-call | flops 1585446912 | bytes 1572864 | tf_op jit(solution)/shard_map/pallas_call | solution.py:82
  69.2 1.9 %collective-permute-start.15 = (bf16[1536,256]{1,0:T(8,128)(2,1)S(1)}, bf16[1536,256]{1,0:T(8,128)(2,1)S(1)}, u32[]{:S(2)}, u32[]{:S(2)}) collective-permute-start(bf16[1536,256]{1,0:T(8,128)(2,1)S(1)} %shard_map.46.refs_0_), channel_id=1, source_target_pairs={{0,8},{8,0},{1,9},{9,1},{2,10},{10,2},{3,11},{11,3},{4,12},{12,4},... | collective-permute-start | bytes 2359304 | tf_op jit(solution)/shard_map/ppermute | solution.py:174
  71.2 3.2 %collective-permute-start.12 = (bf16[64,3072]{1,0:T(8,128)(2,1)S(1)}, bf16[64,3072]{1,0:T(8,128)(2,1)S(1)}, u32[]{:S(2)}, u32[]{:S(2)}) collective-permute-start(bf16[64,3072]{1,0:T(8,128)(2,1)S(1)} %collective-permute-done.11.refs_5_), channel_id=1, source_target_pairs={{0,16},{16,32},{32,48},{48,64},{64,80},{80,96},{96,112},{112,128},... | collective-permute-start | bytes 1179656 | tf_op jit(solution)/shard_map/ppermute | solution.py:157
  74.4 3.6 %collective-permute-start.6 = (bf16[64,3072]{1,0:T(8,128)(2,1)S(1)}, bf16[64,3072]{1,0:T(8,128)(2,1)S(1)}, u32[]{:S(2)}, u32[]{:S(2)}) collective-permute-start(bf16[64,3072]{1,0:T(8,128)(2,1)S(1)} %collective-permute-done.5.refs_7_), channel_id=1, source_target_pairs={{0,16},{16,32},{32,48},{48,64},{64,80},{80,96},{96,112},{112,128},... | collective-permute-start | bytes 1179656 | tf_op jit(solution)/shard_map/ppermute | solution.py:157
  78.0 2.0 %collective-permute-done.12.refs_2_ = bf16[64,3072]{1,0:T(8,128)(2,1)S(1)} collective-permute-done((bf16[64,3072]{1,0:T(8,128)(2,1)S(1)}, bf16[64,3072]{1,0:T(8,128)(2,1)S(1)}, u32[]{:S(2)}, u32[]{:S(2)}) %collective-permute-start.12) | collective-permute-done | bytes 393248 | tf_op jit(solution)/shard_map/ppermute | solution.py:157
  80.0 4.1 %collective-permute-start.13 = (bf16[64,3072]{1,0:T(8,128)(2,1)S(1)}, bf16[64,3072]{1,0:T(8,128)(2,1)S(1)}, u32[]{:S(2)}, u32[]{:S(2)}) collective-permute-start(bf16[64,3072]{1,0:T(8,128)(2,1)S(1)} %collective-permute-done.12.refs_2_), channel_id=1, source_target_pairs={{0,16},{16,32},{32,48},{48,64},{64,80},{80,96},{96,112},{112,128},... | collective-permute-start | bytes 1179656 | tf_op jit(solution)/shard_map/ppermute | solution.py:157
  84.2 4.1 %collective-permute-start.7 = (bf16[64,3072]{1,0:T(8,128)(2,1)S(1)}, bf16[64,3072]{1,0:T(8,128)(2,1)S(1)}, u32[]{:S(2)}, u32[]{:S(2)}) collective-permute-start(bf16[64,3072]{1,0:T(8,128)(2,1)S(1)} %collective-permute-done.6.refs_8_), channel_id=1, source_target_pairs={{0,16},{16,32},{32,48},{48,64},{64,80},{80,96},{96,112},{112,128},... | collective-permute-start | bytes 1179656 | tf_op jit(solution)/shard_map/ppermute | solution.py:157
  88.3 3.6 %shard_map.47 = (f32[256,3072]{1,0:T(8,128)S(1)}, f32[256,3072]{1,0:T(8,128)S(1)}) custom-call(s32[4]{0:T(128)S(1)} %pad_add_fusion.spot, bf16[1536,256]{1,0:T(8,128)(2,1)S(1)} %shard_map.46.refs_0_, bf16[1536,256]{1,0:T(8,128)(2,1)S(1)} %collective-permute-done.15.refs_1_, bf16[64,3072]{1,0:T(8,128)(2,1)S(1)} %all_gather.9.refs_2_, ...), custom_call_target="tpu_custom_call" | custom-call | flops 1409286144 | bytes 9043968 | tf_op jit(solution)/shard_map/pallas_call | solution.py:130
  91.9 1.1 collective-permute-done.7.refs_3_
  93.0 2.7 %shard_map.48 = (f32[256,3072]{1,0:T(8,128)S(1)}, bf16[256,3072]{1,0:T(8,128)(2,1)S(1)}) custom-call(s32[4]{0:T(128)S(1)} %pad_add_fusion.spot, bf16[1536,256]{1,0:T(8,128)(2,1)S(1)} %shard_map.46.refs_0_, bf16[1536,256]{1,0:T(8,128)(2,1)S(1)} %collective-permute-done.15.refs_1_, bf16[64,3072]{1,0:T(8,128)(2,1)S(1)} %collective-permute-done.12.refs_2_, ...), custom_call_target="tpu_custom_call" | custom-call | flops 603979776 | bytes 13762560 | tf_op jit(solution)/shard_map/pallas_call | solution.py:130
  95.7 6.5 %collective-permute-start.16 = (bf16[256,3072]{1,0:T(8,128)(2,1)S(1)}, bf16[256,3072]{1,0:T(8,128)(2,1)S(1)}, u32[]{:S(2)}, u32[]{:S(2)}) collective-permute-start(bf16[256,3072]{1,0:T(8,128)(2,1)S(1)} %get-tuple-element.12), channel_id=1, source_target_pairs={{0,8},{8,0},{1,9},{9,1},{2,10},{10,2},{3,11},{11,3},{4,12},{12,4},... | collective-permute-start | bytes 4718600 | tf_op jit(solution)/shard_map/ppermute | solution.py:185
  102.3 1.9 %collective-permute-start.14 = (bf16[64,3072]{1,0:T(8,128)(2,1)S(1)}, bf16[64,3072]{1,0:T(8,128)(2,1)S(1)}, u32[]{:S(2)}, u32[]{:S(2)}) collective-permute-start(bf16[64,3072]{1,0:T(8,128)(2,1)S(1)} %collective-permute-done.13.refs_4_), channel_id=1, source_target_pairs={{0,16},{16,32},{32,48},{48,64},{64,80},{80,96},{96,112},{112,128},... | collective-permute-start | bytes 1179656 | tf_op jit(solution)/shard_map/ppermute | solution.py:157
  104.2 2.0 %collective-permute-start.8 = (bf16[64,3072]{1,0:T(8,128)(2,1)S(1)}, bf16[64,3072]{1,0:T(8,128)(2,1)S(1)}, u32[]{:S(2)}, u32[]{:S(2)}) collective-permute-start(bf16[64,3072]{1,0:T(8,128)(2,1)S(1)} %collective-permute-done.7.refs_3_), channel_id=1, source_target_pairs={{0,16},{16,32},{32,48},{48,64},{64,80},{80,96},{96,112},{112,128},... | collective-permute-start | bytes 1179656 | tf_op jit(solution)/shard_map/ppermute | solution.py:157
  106.2 4.9 %collective-permute-done.14 = bf16[64,3072]{1,0:T(8,128)(2,1)S(1)} collective-permute-done((bf16[64,3072]{1,0:T(8,128)(2,1)S(1)}, bf16[64,3072]{1,0:T(8,128)(2,1)S(1)}, u32[]{:S(2)}, u32[]{:S(2)}) %collective-permute-start.14) | collective-permute-done | bytes 393248 | tf_op jit(solution)/shard_map/ppermute | solution.py:157
  111.1 4.1 %all_gather.11.refs_2_ = bf16[128,3072]{1,0:T(8,128)(2,1)S(1)} all-gather(bf16[64,3072]{1,0:T(8,128)(2,1)S(1)} %collective-permute-done.14), channel_id=1, replica_groups=mesh['short'=4,'ring'=12,'core'=2,'col_0'=4,'col_1'=2] {'core'}, dimensions={0}, use_global_device_ids=true | all-gather | bytes 1179648 | tf_op jit(solution)/shard_map/all_gather | solution.py:187
  115.3 4.1 %all_gather.10.refs_1_ = bf16[128,3072]{1,0:T(8,128)(2,1)S(1)} all-gather(bf16[64,3072]{1,0:T(8,128)(2,1)S(1)} %collective-permute-done.8), channel_id=1, replica_groups=mesh['short'=4,'ring'=12,'core'=2,'col_0'=4,'col_1'=2] {'core'}, dimensions={0}, use_global_device_ids=true | all-gather | bytes 1179648 | tf_op jit(solution)/shard_map/all_gather | solution.py:186
  119.4 3.4 %shard_map.49 = f32[256,3072]{1,0:T(8,128)} custom-call(s32[4]{0:T(128)S(1)} %pad_add_fusion.spot, bf16[1536,256]{1,0:T(8,128)(2,1)S(1)} %shard_map.46.refs_0_, bf16[128,3072]{1,0:T(8,128)(2,1)S(1)} %all_gather.10.refs_1_, bf16[128,3072]{1,0:T(8,128)(2,1)S(1)} %all_gather.11.refs_2_, f32[256,3072]{1,0:T(8,128)S(1)} %get-tuple-element.11.refs_3_, ...), custom_call_target="tpu_custom_call" | custom-call | flops 402653184 | bytes 11010048 | tf_op jit(solution)/shard_map/pallas_call | solution.py:130
  (17 shorter events, 1.0 us)
Async XLA Ops:
  0.0 40.7 %collective-permute-start = (bf16[192,256]{1,0:T(8,128)(2,1)}, bf16[192,256]{1,0:T(8,128)(2,1)S(1)}, u32[]{:S(2)}, u32[]{:S(2)}) collective-permute-start(bf16[192,256]{1,0:T(8,128)(2,1)} %param.4), channel_id=1, source_target_pairs={{0,1},{1,0},{2,3},{3,2},{4,5},{5,4},{6,7},{7,6},{8,9},{9,8},{10,11... | collective-permute-start | bytes 294920 | tf_op jit(solution)/shard_map/ppermute | solution.py:159
  22.0 22.7 %collective-permute-start.3 = (bf16[64,3072]{1,0:T(8,128)(2,1)S(1)}, bf16[64,3072]{1,0:T(8,128)(2,1)S(1)}, u32[]{:S(2)}, u32[]{:S(2)}) collective-permute-start(bf16[64,3072]{1,0:T(8,128)(2,1)S(1)} %all_gather.9.refs_2_), channel_id=1, source_target_pairs={{0,8},{8,0},{1,9},{9,1},{2,10},{10,2},{3,11},{11,3},{4,12},{12,4},... | collective-permute-start | bytes 1179656 | tf_op jit(solution)/shard_map/ppermute | solution.py:161
  29.3 17.7 %collective-permute-start.9 = (bf16[64,3072]{1,0:T(8,128)(2,1)S(1)}, bf16[64,3072]{1,0:T(8,128)(2,1)S(1)}, u32[]{:S(2)}, u32[]{:S(2)}) collective-permute-start(bf16[64,3072]{1,0:T(8,128)(2,1)S(1)} %all_gather.9.refs_2_), channel_id=1, source_target_pairs={{0,16},{16,32},{32,48},{48,64},{64,80},{80,96},{96,112},{112,128},... | collective-permute-start | bytes 1179656 | tf_op jit(solution)/shard_map/ppermute | solution.py:157
  41.7 8.8 %collective-permute-start.1 = (bf16[2,192,256]{2,1,0:T(8,128)(2,1)S(1)}, bf16[2,192,256]{2,1,0:T(8,128)(2,1)S(1)}, u32[]{:S(2)}, u32[]{:S(2)}) collective-permute-start(bf16[2,192,256]{2,1,0:T(8,128)(2,1)S(1)} %pad_maximum_fusion.1.refs_0_), channel_id=1, source_target_pairs={{0,2},{2,0},{4,6},{6,4},{1,3},{3,1},{5,7},{7,5},{8,10},{10,8},{12,... | collective-permute-start | bytes 589832 | tf_op jit(solution)/shard_map/ppermute | solution.py:164
  44.8 16.4 %collective-permute-start.4 = (bf16[64,3072]{1,0:T(8,128)(2,1)S(1)}, bf16[64,3072]{1,0:T(8,128)(2,1)S(1)}, u32[]{:S(2)}, u32[]{:S(2)}) collective-permute-start(bf16[64,3072]{1,0:T(8,128)(2,1)S(1)} %collective-permute-done.3), channel_id=1, source_target_pairs={{0,16},{16,32},{32,48},{48,64},{64,80},{80,96},{96,112},{112,128},... | collective-permute-start | bytes 1179656 | tf_op jit(solution)/shard_map/ppermute | solution.py:157
  47.0 10.8 %collective-permute-start.10 = (bf16[64,3072]{1,0:T(8,128)(2,1)S(1)}, bf16[64,3072]{1,0:T(8,128)(2,1)S(1)}, u32[]{:S(2)}, u32[]{:S(2)}) collective-permute-start(bf16[64,3072]{1,0:T(8,128)(2,1)S(1)} %collective-permute-done.9.refs_3_), channel_id=1, source_target_pairs={{0,16},{16,32},{32,48},{48,64},{64,80},{80,96},{96,112},{112,128},... | collective-permute-start | bytes 1179656 | tf_op jit(solution)/shard_map/ppermute | solution.py:157
  51.4 13.6 %collective-permute-start.2 = (bf16[4,192,256]{2,1,0:T(8,128)(2,1)S(1)}, bf16[4,192,256]{2,1,0:T(8,128)(2,1)S(1)}, u32[]{:S(2)}, u32[]{:S(2)}) collective-permute-start(bf16[4,192,256]{2,1,0:T(8,128)(2,1)S(1)} %pad_maximum_fusion), channel_id=1, source_target_pairs={{0,6},{2,4},{4,2},{6,0},{1,7},{3,5},{5,3},{7,1},{8,14},{10,12},{12... | collective-permute-start | bytes 1179656 | tf_op jit(solution)/shard_map/ppermute | solution.py:165
  57.8 13.3 %collective-permute-start.11 = (bf16[64,3072]{1,0:T(8,128)(2,1)S(1)}, bf16[64,3072]{1,0:T(8,128)(2,1)S(1)}, u32[]{:S(2)}, u32[]{:S(2)}) collective-permute-start(bf16[64,3072]{1,0:T(8,128)(2,1)S(1)} %collective-permute-done.10.refs_4_), channel_id=1, source_target_pairs={{0,16},{16,32},{32,48},{48,64},{64,80},{80,96},{96,112},{112,128},... | collective-permute-start | bytes 1179656 | tf_op jit(solution)/shard_map/ppermute | solution.py:157
  61.2 13.1 %collective-permute-start.5 = (bf16[64,3072]{1,0:T(8,128)(2,1)S(1)}, bf16[64,3072]{1,0:T(8,128)(2,1)S(1)}, u32[]{:S(2)}, u32[]{:S(2)}) collective-permute-start(bf16[64,3072]{1,0:T(8,128)(2,1)S(1)} %collective-permute-done.4.refs_6_), channel_id=1, source_target_pairs={{0,16},{16,32},{32,48},{48,64},{64,80},{80,96},{96,112},{112,128},... | collective-permute-start | bytes 1179656 | tf_op jit(solution)/shard_map/ppermute | solution.py:157
  65.0 0.7 copy-start
  69.2 19.1 %collective-permute-start.15 = (bf16[1536,256]{1,0:T(8,128)(2,1)S(1)}, bf16[1536,256]{1,0:T(8,128)(2,1)S(1)}, u32[]{:S(2)}, u32[]{:S(2)}) collective-permute-start(bf16[1536,256]{1,0:T(8,128)(2,1)S(1)} %shard_map.46.refs_0_), channel_id=1, source_target_pairs={{0,8},{8,0},{1,9},{9,1},{2,10},{10,2},{3,11},{11,3},{4,12},{12,4},... | collective-permute-start | bytes 2359304 | tf_op jit(solution)/shard_map/ppermute | solution.py:174
  71.2 8.8 %collective-permute-start.12 = (bf16[64,3072]{1,0:T(8,128)(2,1)S(1)}, bf16[64,3072]{1,0:T(8,128)(2,1)S(1)}, u32[]{:S(2)}, u32[]{:S(2)}) collective-permute-start(bf16[64,3072]{1,0:T(8,128)(2,1)S(1)} %collective-permute-done.11.refs_5_), channel_id=1, source_target_pairs={{0,16},{16,32},{32,48},{48,64},{64,80},{80,96},{96,112},{112,128},... | collective-permute-start | bytes 1179656 | tf_op jit(solution)/shard_map/ppermute | solution.py:157
  74.4 9.8 %collective-permute-start.6 = (bf16[64,3072]{1,0:T(8,128)(2,1)S(1)}, bf16[64,3072]{1,0:T(8,128)(2,1)S(1)}, u32[]{:S(2)}, u32[]{:S(2)}) collective-permute-start(bf16[64,3072]{1,0:T(8,128)(2,1)S(1)} %collective-permute-done.5.refs_7_), channel_id=1, source_target_pairs={{0,16},{16,32},{32,48},{48,64},{64,80},{80,96},{96,112},{112,128},... | collective-permute-start | bytes 1179656 | tf_op jit(solution)/shard_map/ppermute | solution.py:157
  80.0 11.9 %collective-permute-start.13 = (bf16[64,3072]{1,0:T(8,128)(2,1)S(1)}, bf16[64,3072]{1,0:T(8,128)(2,1)S(1)}, u32[]{:S(2)}, u32[]{:S(2)}) collective-permute-start(bf16[64,3072]{1,0:T(8,128)(2,1)S(1)} %collective-permute-done.12.refs_2_), channel_id=1, source_target_pairs={{0,16},{16,32},{32,48},{48,64},{64,80},{80,96},{96,112},{112,128},... | collective-permute-start | bytes 1179656 | tf_op jit(solution)/shard_map/ppermute | solution.py:157
  84.2 8.8 %collective-permute-start.7 = (bf16[64,3072]{1,0:T(8,128)(2,1)S(1)}, bf16[64,3072]{1,0:T(8,128)(2,1)S(1)}, u32[]{:S(2)}, u32[]{:S(2)}) collective-permute-start(bf16[64,3072]{1,0:T(8,128)(2,1)S(1)} %collective-permute-done.6.refs_8_), channel_id=1, source_target_pairs={{0,16},{16,32},{32,48},{48,64},{64,80},{80,96},{96,112},{112,128},... | collective-permute-start | bytes 1179656 | tf_op jit(solution)/shard_map/ppermute | solution.py:157
  95.7 23.6 %collective-permute-start.16 = (bf16[256,3072]{1,0:T(8,128)(2,1)S(1)}, bf16[256,3072]{1,0:T(8,128)(2,1)S(1)}, u32[]{:S(2)}, u32[]{:S(2)}) collective-permute-start(bf16[256,3072]{1,0:T(8,128)(2,1)S(1)} %get-tuple-element.12), channel_id=1, source_target_pairs={{0,8},{8,0},{1,9},{9,1},{2,10},{10,2},{3,11},{11,3},{4,12},{12,4},... | collective-permute-start | bytes 4718600 | tf_op jit(solution)/shard_map/ppermute | solution.py:185
  102.3 8.8 %collective-permute-start.14 = (bf16[64,3072]{1,0:T(8,128)(2,1)S(1)}, bf16[64,3072]{1,0:T(8,128)(2,1)S(1)}, u32[]{:S(2)}, u32[]{:S(2)}) collective-permute-start(bf16[64,3072]{1,0:T(8,128)(2,1)S(1)} %collective-permute-done.13.refs_4_), channel_id=1, source_target_pairs={{0,16},{16,32},{32,48},{48,64},{64,80},{80,96},{96,112},{112,128},... | collective-permute-start | bytes 1179656 | tf_op jit(solution)/shard_map/ppermute | solution.py:157
  104.2 11.1 %collective-permute-start.8 = (bf16[64,3072]{1,0:T(8,128)(2,1)S(1)}, bf16[64,3072]{1,0:T(8,128)(2,1)S(1)}, u32[]{:S(2)}, u32[]{:S(2)}) collective-permute-start(bf16[64,3072]{1,0:T(8,128)(2,1)S(1)} %collective-permute-done.7.refs_3_), channel_id=1, source_target_pairs={{0,16},{16,32},{32,48},{48,64},{64,80},{80,96},{96,112},{112,128},... | collective-permute-start | bytes 1179656 | tf_op jit(solution)/shard_map/ppermute | solution.py:157
